TPU v7x, 128 devices: a whole 4x4x4 slice. The times are simulated.
128 devices in a mesh: gx: 4 (over x), gy: 32 (over y, z, core).
Axes of the slice: x: 4, y: 4, z: 4, core: 2. Of those that a mesh axis runs over, the one named last changes fastest.
Arguments:
- old_state: float32 [1024, 6, 32768], P(('gx', 'gy')), may hold values from -6 to 6
- old_owner: int32 [512], replicated, may hold values from 0 to 127, as said below
- old_slot: int32 [512], replicated, may hold values from 0 to 7, as said below
- diffusivity: float32 [6], replicated, may hold values from 0.01 to 0.08
Outputs:
- new_state: float32 [512, 6, 32768], P(('gx', 'gy'))
Inputs may be any that keep to these rules, and one draw needn't show every extreme that they name: The curve is closed: with n = g // 4 the new owner of box g, old_owner[g] is n, or n - 1 modulo the device count for one of the first 2 boxes of n, or n + 1 modulo the device count for one of the last 2 boxes of n. `old_slot`: A box kept by its owner sits in slot 2 + g % 4; the j-th of the first 2 boxes of a device, when held by the device below, sat in that device's slot 6 + j; the j-th of the last 2 boxes, when held by the device above, sat in its slot j. Slots that hold no box hold anything. Some device takes over 2 boxes from each neighbour in every draw.
All inputs are finite; a program needn't handle non-finite values.
Results may differ from a plain program's by a relative error of at most 0.0003.
Values sent between devices are 32-bit elements; how exact they have to be, the bound alone decides.
No kernel may reach another device: no remote copies, remote signals or barrier semaphores. Data moves between devices by JAX's collectives and lax.ppermute only.
A program may use at most 128 MiB of HBM per device.

v0:
```python
import jax
import jax.numpy as jnp
from jax import lax
from jax.experimental import pallas as pl
from jax.experimental.pallas import tpu as pltpu
from jax.sharding import PartitionSpec as P

B = 32
F = 6
CAP = 4
ROWS = 8
LANES = 128
AXES = ("gx", "gy")
F32 = jnp.float32
HBM = pl.BlockSpec(memory_space=pl.ANY)
SMEM = pl.BlockSpec(memory_space=pltpu.SMEM)
MIB = 1 << 20


def run_all(copies):
    for copy in copies:
        copy.start()
    for copy in copies:
        copy.wait()


def pack_body(x, up, down, sem):
    copies = []
    for j in range(2):
        copies.append(pltpu.make_async_copy(x.at[:, :, :, 6 + j], up.at[j], sem.at[j]))
        copies.append(pltpu.make_async_copy(x.at[:, :, :, j], down.at[j], sem.at[2 + j]))
    run_all(copies)


def pack(x):
    shape = jax.ShapeDtypeStruct((2, F, B, ROWS, 1, LANES), F32)
    return pl.pallas_call(
        pack_body,
        name="pack",
        out_shape=(shape, shape),
        in_specs=[HBM],
        out_specs=(HBM, HBM),
        scratch_shapes=[pltpu.SemaphoreType.DMA((4,))],
    )(x)


def device_number():
    return lax.axis_index("gx") * lax.axis_size("gy") + lax.axis_index("gy")


def kept_flags(owner):
    device = device_number()
    return [owner[device * CAP + c] == device for c in range(CAP)]


def from_box(kept, c, x, up, down, pick, target, sem):
    moved = (up if c < 2 else down).at[c % 2]

    @pl.when(kept)
    def _():
        pltpu.make_async_copy(pick(x.at[:, :, :, 2 + c]), target, sem).start()

    @pl.when(jnp.logical_not(kept))
    def _():
        pltpu.make_async_copy(pick(moved), target, sem).start()

    return pltpu.make_async_copy(pick(moved), target, sem)


def lane_chunk(shape):
    return lax.broadcasted_iota(jnp.int32, shape, len(shape) - 1)


def edges_body(owner, x, up, down, z_low, z_high, y_low, y_high, first, last, sem, sem_y):
    kept = kept_flags(owner)
    waits, waits_y = [], []
    for c in range(CAP):
        part = lambda row: (lambda ref: ref.at[:, :, row, 0])
        waits_y.append(from_box(kept[c], c, x, up, down, part(0), first.at[c], sem_y.at[c]))
        waits_y.append(from_box(kept[c], c, x, up, down, part(7), last.at[c], sem_y.at[4 + c]))
    for c in range(CAP):
        waits.append(
            from_box(kept[c], c, x, up, down, lambda r: r.at[:, 0:2], z_low.at[c], sem.at[c])
        )
        waits.append(
            from_box(kept[c], c, x, up, down, lambda r: r.at[:, 30:32], z_high.at[c], sem.at[4 + c])
        )
    for wait in waits_y:
        wait.wait()
    left = lane_chunk((16, LANES)) < 64
    for c in range(CAP):
        for f in range(F):
            low, high = first[c, f, 0:16], first[c, f, 16:32]
            y_low[c, f] = jnp.where(left, low, pltpu.roll(high, 64, 1))
            low, high = last[c, f, 0:16], last[c, f, 16:32]
            y_high[c, f] = jnp.where(left, pltpu.roll(low, 64, 1), high)
    for wait in waits:
        wait.wait()


def edges(owner, x, up, down):
    z_shape = jax.ShapeDtypeStruct((CAP, F, 2, ROWS, 1, LANES), F32)
    y_shape = jax.ShapeDtypeStruct((CAP, F, 16, LANES), F32)
    vmem = pl.BlockSpec(memory_space=pltpu.VMEM)
    return pl.pallas_call(
        edges_body,
        name="edges",
        out_shape=(z_shape, z_shape, y_shape, y_shape),
        in_specs=[SMEM, HBM, HBM, HBM],
        out_specs=(HBM, HBM, vmem, vmem),
        scratch_shapes=[
            pltpu.VMEM((CAP, F, B, LANES), F32),
            pltpu.VMEM((CAP, F, B, LANES), F32),
            pltpu.SemaphoreType.DMA((8,)),
            pltpu.SemaphoreType.DMA((8,)),
        ],
    )(owner, x, up, down)


def minmod(a, b):
    return jnp.maximum(jnp.minimum(a, b), jnp.minimum(jnp.maximum(a, b), 0.0))


def conduction(v):
    return jnp.exp(0.5 * jnp.tanh(v))


def step_body(
    owner, spread, x, up, down, z_below, z_above, y_below, y_above, out,
    q, result, face_a, face_b, carry_p, carry_n, carry_c, sem, sem_z, sem_y, sem_out, halo_low, halo_high,
):
    kept = kept_flags(owner)
    gx, gy = lax.axis_index("gx"), lax.axis_index("gy")
    last_x, last_y = lax.axis_size("gx") - 1, lax.axis_size("gy") - 1
    copies = [
        pltpu.make_async_copy(z_below, q.at[:, :, 0:2], sem_z.at[0]),
        pltpu.make_async_copy(z_above, q.at[:, :, B + 2 : B + 4], sem_z.at[1]),
        pltpu.make_async_copy(y_below, halo_low, sem_y.at[0]),
        pltpu.make_async_copy(y_above, halo_high, sem_y.at[1]),
    ]
    for copy in copies:
        copy.start()
    for c in range(CAP):
        copies.append(
            from_box(
                kept[c], c, x, up, down, lambda r: r.at[:, :, :, 0], q.at[c, :, 2 : B + 2], sem.at[c]
            )
        )
    for copy in copies:
        copy.wait()

    @pl.when(gx == 0)
    def _():
        for c in range(CAP):
            for f in range(F):
                q[c, f, 0] = q[c, f, 2]
                q[c, f, 1] = q[c, f, 2]

    @pl.when(gx == last_x)
    def _():
        for c in range(CAP):
            for f in range(F):
                q[c, f, B + 2] = q[c, f, B + 1]
                q[c, f, B + 3] = q[c, f, B + 1]

    lane = lax.broadcasted_iota(jnp.int32, (8, LANES), 1)
    sub = lax.broadcasted_iota(jnp.int32, (8, LANES), 0)
    chunk = lane // 32
    x_in = lane % 32
    scale = [0.5 * spread[f] for f in range(F)]

    def y_faces(c, block):
        z0 = block * 8
        half = z0 // 16
        left = lane < 64

        def rows(f):
            below = halo_low[c, f, pl.ds(z0 - 16 * half, 8)]
            above = halo_high[c, f, pl.ds(z0 - 16 * half, 8)]
            row0 = q[c, f, z0 + 2 : z0 + 10, 0, :]
            row7 = q[c, f, z0 + 2 : z0 + 10, 7, :]
            r70, r71 = pltpu.roll(row7, 32, 1), pltpu.roll(row7, 64, 1)
            r02, r03 = pltpu.roll(row0, 64, 1), pltpu.roll(row0, 96, 1)
            if half == 0:
                below = pltpu.roll(below, 64, 1)
            else:
                above = pltpu.roll(above, 64, 1)
            above = jnp.where(gy == last_y, jnp.where(chunk == 0, r70, r71), above)
            below = jnp.where(gy == 0, jnp.where(chunk == 3, r03, r02), below)
            r = jnp.where(left, above, below)
            s1 = jnp.where(chunk == 0, r70, r03)
            return r, s1, r02

        r1, s11, _ = rows(1)
        weight = 0.0625 * (r1 + s11)
        r5, s15, _ = rows(5)
        cond = conduction(r5) + conduction(s15)
        for f in range(F):
            r, s1, s2 = rows(f)
            r2 = jnp.where(chunk == 0, pltpu.roll(r, 96, 1), pltpu.roll(r, 32, 1))
            da, db = r - s1, r2 - r
            e = (r + r) - minmod(da, db)
            m0 = (s1 + s1) - minmod(-da, s2 - s1)
            net = -(scale[f] * cond) * da - weight * jnp.where(weight > 0.0, e, m0)
            face_a[c, f, z0 : z0 + 8, :] = jnp.where(chunk == 0, r, -da)
            face_b[c, f, z0 : z0 + 8, :] = jnp.where(chunk == 0, e, net)

    for c in range(CAP):
        for block in range(4):
            y_faces(c, block)

    head = (sub == 0) & (lane < 32)
    tail = (sub == 7) & (lane >= 96)

    def y_next(value, row):
        m = pltpu.roll(jnp.where(head, row, value), 96, 1)
        return jnp.where(lane < 96, m, pltpu.roll(m, 7, 0))

    def y_last(value, row):
        m = pltpu.roll(jnp.where(tail, row, value), 32, 1)
        return jnp.where(lane >= 32, m, pltpu.roll(m, 1, 0))

    next_index = (lane & 96) | ((lane + 1) & 31)
    last_index = (lane & 96) | ((lane + 31) & 31)

    def x_next(values, ends):
        result = []
        for c in range(CAP):
            if c < CAP - 1:
                m = jnp.where(x_in == 0, values[c + 1], values[c])
                result.append(jnp.take_along_axis(m, next_index, axis=1))
            else:
                m = jnp.take_along_axis(values[c], next_index, axis=1)
                result.append(jnp.where(x_in == 31, ends, m))
        return result

    def x_last(values, ends):
        result = []
        for c in range(CAP):
            if c > 0:
                m = jnp.where(x_in == 31, values[c - 1], values[c])
                result.append(jnp.take_along_axis(m, last_index, axis=1))
            else:
                m = jnp.take_along_axis(values[c], last_index, axis=1)
                result.append(jnp.where(x_in == 0, ends, m))
        return result

    def z_face(c, f, z, weight, cond):
        here, after, more = q[c, f, z + 2], q[c, f, z + 3], q[c, f, z + 4]
        d = after - here
        slope = minmod(d, more - after)
        twice = after + after
        state = jnp.where(weight > 0.0, carry_p[c, f], twice - slope)
        carry_p[c, f] = twice + slope
        return (scale[f] * cond) * d - weight * state

    for c in range(CAP):
        carry_c[c] = conduction(q[c, 5, 2])
        cond = conduction(q[c, 5, 1]) + carry_c[c]
        weight = 0.0625 * (q[c, 2, 1] + q[c, 2, 2])
        for f in range(F):
            one, two, three = q[c, f, 0], q[c, f, 1], q[c, f, 2]
            carry_p[c, f] = (two + two) + minmod(two - one, three - two)
            carry_n[c, f] = z_face(c, f, -1, weight, cond)

    boxes = range(CAP)

    def plane(z, _):
        here = [carry_c[c] for c in boxes]
        above = [conduction(q[c, 5, z + 3]) for c in boxes]
        cond_z = [here[c] + above[c] for c in boxes]
        for c in boxes:
            carry_c[c] = above[c]
        cond_x = [a + b for a, b in zip(here, x_next(here, here[-1]))]
        edge5 = [face_a[c, 5, pl.ds(z, 1), :] for c in boxes]
        cond_y = [here[c] + y_next(here[c], conduction(edge5[c])) for c in boxes]
        u = [q[c, 0, z + 2] for c in boxes]
        weight_x = [0.0625 * (a + b) for a, b in zip(u, x_next(u, u[-1]))]
        v = [q[c, 1, z + 2] for c in boxes]
        weight_y = [0.0625 * (v[c] + y_next(v[c], face_a[c, 1, pl.ds(z, 1), :])) for c in boxes]
        weight_z = [0.0625 * (q[c, 2, z + 2] + q[c, 2, z + 3]) for c in boxes]
        for f in range(F):
            value = [q[c, f, z + 2] for c in boxes]
            twice = [a + a for a in value]
            total = []
            for c in boxes:
                net = z_face(c, f, z, weight_z[c], cond_z[c])
                total.append(value[c] + (net - carry_n[c, f]))
                carry_n[c, f] = net
            for c in boxes:
                row_a, row_b = face_a[c, f, pl.ds(z, 1), :], face_b[c, f, pl.ds(z, 1), :]
                d = y_next(value[c], row_a) - value[c]
                slope = minmod(y_last(d, row_a), d)
                right = y_next(twice[c] - slope, row_b)
                state = jnp.where(weight_y[c] > 0.0, twice[c] + slope, right)
                net = (scale[f] * cond_y[c]) * d - weight_y[c] * state
                total[c] = total[c] + (net - y_last(net, row_b))
            d = [b - a for a, b in zip(value, x_next(value, value[-1]))]
            slope = [minmod(a, b) for a, b in zip(x_last(d, 0.0), d)]
            right = x_next([a - b for a, b in zip(twice, slope)], twice[-1])
            net = []
            for c in boxes:
                state = jnp.where(weight_x[c] > 0.0, twice[c] + slope[c], right[c])
                net.append((scale[f] * cond_x[c]) * d[c] - weight_x[c] * state)
            before = x_last(net, -0.125 * u[0] * twice[0])
            for c in boxes:
                result[c, f, z] = total[c] + (net[c] - before[c])
        return 0

    lax.fori_loop(0, B, plane, 0)
    run_all(
        [
            pltpu.make_async_copy(result.at[c], out.at[:, :, :, c, 0], sem_out.at[c])
            for c in boxes
        ]
    )


def step(owner, spread, x, up, down, z_below, z_above, y_below, y_above):
    return pl.pallas_call(
        step_body,
        name="step",
        out_shape=jax.ShapeDtypeStruct((F, B, ROWS, CAP, 1, LANES), F32),
        in_specs=[SMEM, SMEM] + [HBM] * 7,
        out_specs=HBM,
        scratch_shapes=[
            pltpu.VMEM((CAP, F, B + 4, ROWS, LANES), F32),
            pltpu.VMEM((CAP, F, B, ROWS, LANES), F32),
            pltpu.VMEM((CAP, F, B, LANES), F32),
            pltpu.VMEM((CAP, F, B, LANES), F32),
            pltpu.VMEM((CAP, F, ROWS, LANES), F32),
            pltpu.VMEM((CAP, F, ROWS, LANES), F32),
            pltpu.VMEM((CAP, ROWS, LANES), F32),
            pltpu.SemaphoreType.DMA((CAP,)),
            pltpu.SemaphoreType.DMA((2,)),
            pltpu.SemaphoreType.DMA((2,)),
            pltpu.SemaphoreType.DMA((CAP,)),
            pltpu.VMEM((CAP, F, 16, LANES), F32),
            pltpu.VMEM((CAP, F, 16, LANES), F32),
        ],
        compiler_params=pltpu.CompilerParams(vmem_limit_bytes=24 * MIB),
    )(owner, spread, x, up, down, z_below, z_above, y_below, y_above)


def along_curve(block, distance):
    count = lax.axis_size(AXES)
    return lax.ppermute(block, AXES, [(i, (i + distance) % count) for i in range(count)])


def along_axis(block, axis, distance):
    count = lax.axis_size(axis)
    pairs = [(i, i + distance) for i in range(count) if 0 <= i + distance < count]
    return lax.ppermute(block, axis, pairs)


def local(old_state, old_owner, old_slot, diffusivity):
    x = old_state.reshape(8, F, B, ROWS, LANES).transpose(1, 2, 3, 0, 4)[..., None, :]
    up, down = pack(x)
    up = along_curve(up, 1)
    down = along_curve(down, -1)
    z_low, z_high, y_low, y_high = edges(old_owner, x, up, down)
    z_below = along_axis(z_high, "gx", 1)[:, :, :, :, 0]
    z_above = along_axis(z_low, "gx", -1)[:, :, :, :, 0]
    y_below = along_axis(y_high, "gy", 1)
    y_above = along_axis(y_low, "gy", -1)
    out = step(old_owner, diffusivity, x, up, down, z_below, z_above, y_below, y_above)
    return out[..., 0, :].transpose(3, 0, 1, 2, 4).reshape(CAP, F, B * B * B)


def solution(mesh):
    placed = (P(AXES, None, None), P(), P(), P())
    return jax.shard_map(
        local, mesh=mesh, in_specs=placed, out_specs=P(AXES, None, None), check_vma=False
    )
```

profile of v0, /device:TPU:27, one launch (start us, length us, event | category | flops | bytes accessed | tf_op | source)
XLA Modules:
  0.0 184.1 jit_solution(15984982162646479052)
XLA Ops:
  0.0 96.4 %pack.1 = (f32[2,6,32,8,1,128]{5,4,3,2,1,0:T(1,128)}, f32[2,6,32,8,1,128]{5,4,3,2,1,0:T(1,128)}) custom-call(f32[6,32,8,8,1,128]{5,4,3,2,1,0:T(1,128)} %bitcast.14), custom_call_target="tpu_custom_call" | custom-call | tf_op jit(solution)/shard_map/pack/pallas_call | solution.py:37
  96.4 2.3 %collective-permute-start = (f32[2,6,32,8,1,128]{5,4,3,2,1,0:T(1,128)}, f32[2,6,32,8,1,128]{5,4,3,2,1,0:T(1,128)S(1)}, u32[]{:S(2)}, u32[]{:S(2)}) collective-permute-start(f32[2,6,32,8,1,128]{5,4,3,2,1,0:T(1,128)} %get-tuple-element.11), channel_id=1, source_target_pairs={{0,1},{1,2},{2,3},{3,4},{4,5},{5,6},{6,7},{7,8},{8,9},{9,10},{10,1... | collective-permute-start | bytes 4718600 | tf_op jit(solution)/shard_map/ppermute | solution.py:347
  98.7 0.0 copy-start.5
  98.7 0.0 copy-start.6
  98.7 0.0 collective-permute-start.1
  98.7 17.7 %collective-permute-done.up = f32[2,6,32,8,1,128]{5,4,3,2,1,0:T(1,128)S(1)} collective-permute-done((f32[2,6,32,8,1,128]{5,4,3,2,1,0:T(1,128)}, f32[2,6,32,8,1,128]{5,4,3,2,1,0:T(1,128)S(1)}, u32[]{:S(2)}, u32[]{:S(2)}) %collective-permute-start) | collective-permute-done | bytes 1572896 | tf_op jit(solution)/shard_map/ppermute | solution.py:347
  116.4 2.6 %collective-permute-done.1.down = f32[2,6,32,8,1,128]{5,4,3,2,1,0:T(1,128)S(1)} collective-permute-done((f32[2,6,32,8,1,128]{5,4,3,2,1,0:T(1,128)}, f32[2,6,32,8,1,128]{5,4,3,2,1,0:T(1,128)S(1)}, u32[]{:S(2)}, u32[]{:S(2)}) %collective-permute-start.1) | collective-permute-done | bytes 1572896 | tf_op jit(solution)/shard_map/ppermute | solution.py:347
  118.9 0.0 copy-done.1
  119.0 1.2 copy-done.3
  120.1 14.6 %edges.1 = (f32[4,6,2,8,1,128]{5,4,3,2,1,0:T(1,128)}, f32[4,6,2,8,1,128]{5,4,3,2,1,0:T(1,128)}, f32[4,6,16,128]{3,2,1,0:T(8,128)}, f32[4,6,16,128]{3,2,1,0:T(8,128)}) custom-call(s32[512]{0:T(512)} %owner.3, f32[6,32,8,8,1,128]{5,4,3,2,1,0:T(1,128)} %bitcast.15, f32[2,6,32,8,1,128]{5,4,3,2,1,0:T(1,128)} %copy-done.1, f32[2,6,32,8,1,128]{5,4,3,2,1,0:T(1,128)} %copy-done.3), custom_call_target="tpu_custom_call" | custom-call | tf_op jit(solution)/shard_map/edges/pallas_call | solution.py:105
  134.8 2.2 %collective-permute-start.3 = (f32[4,6,2,8,1,128]{5,3,2,1,0,4:T(8,128)}, f32[4,6,2,8,1,128]{5,3,2,1,0,4:T(8,128)S(1)}, u32[]{:S(2)}, u32[]{:S(2)}) collective-permute-start(f32[4,6,2,8,1,128]{5,3,2,1,0,4:T(8,128)} %bitcast.20), channel_id=1, source_target_pairs={{32,0},{64,32},{96,64},{33,1},{65,33},{97,65},{34,2},{66,34},{98,6... | collective-permute-start | bytes 589832 | tf_op jit(solution)/shard_map/ppermute | solution.py:353
  136.9 3.1 %collective-permute-start.2 = (f32[4,6,2,8,1,128]{5,3,2,1,0,4:T(8,128)}, f32[4,6,2,8,1,128]{5,3,2,1,0,4:T(8,128)S(1)}, u32[]{:S(2)}, u32[]{:S(2)}) collective-permute-start(f32[4,6,2,8,1,128]{5,3,2,1,0,4:T(8,128)} %bitcast.19), channel_id=1, source_target_pairs={{0,32},{32,64},{64,96},{1,33},{33,65},{65,97},{2,34},{34,66},{66,9... | collective-permute-start | bytes 589832 | tf_op jit(solution)/shard_map/ppermute | solution.py:353
  140.1 3.4 %collective-permute-start.4 = (f32[4,6,16,128]{3,2,1,0:T(8,128)}, f32[4,6,16,128]{3,2,1,0:T(8,128)S(1)}, u32[]{:S(2)}, u32[]{:S(2)}) collective-permute-start(f32[4,6,16,128]{3,2,1,0:T(8,128)} %get-tuple-element.15), channel_id=1, source_target_pairs={{0,1},{1,2},{2,3},{3,4},{4,5},{5,6},{6,7},{7,8},{8,9},{9,10},{10,1... | collective-permute-start | bytes 589832 | tf_op jit(solution)/shard_map/ppermute | solution.py:353
  143.5 2.5 %collective-permute-start.5 = (f32[4,6,16,128]{3,2,1,0:T(8,128)}, f32[4,6,16,128]{3,2,1,0:T(8,128)S(1)}, u32[]{:S(2)}, u32[]{:S(2)}) collective-permute-start(f32[4,6,16,128]{3,2,1,0:T(8,128)} %get-tuple-element.16), channel_id=1, source_target_pairs={{1,0},{2,1},{3,2},{4,3},{5,4},{6,5},{7,6},{8,7},{9,8},{10,9},{11,1... | collective-permute-start | bytes 589832 | tf_op jit(solution)/shard_map/ppermute | solution.py:353
  146.0 0.0 collective-permute-done.3
  146.0 0.0 collective-permute-done.2
  146.0 0.4 collective-permute-done.4.y_below
  146.4 4.6 %collective-permute-done.5.y_above = f32[4,6,16,128]{3,2,1,0:T(8,128)S(1)} collective-permute-done((f32[4,6,16,128]{3,2,1,0:T(8,128)}, f32[4,6,16,128]{3,2,1,0:T(8,128)S(1)}, u32[]{:S(2)}, u32[]{:S(2)}) %collective-permute-start.5) | collective-permute-done | bytes 196640 | tf_op jit(solution)/shard_map/ppermute | solution.py:353
  151.0 0.0 copy-done.5
  151.0 0.0 copy-done.6
  151.0 2.8 %copy-done = f32[8,6,32768]{2,0,1:T(8,128)S(1)} copy-done((f32[8,6,32768]{2,0,1:T(8,128)S(1)}, f32[8,6,32768]{2,0,1:T(8,128)}, u32[]{:S(2)}) %copy-start) | copy-done | bytes 6291480
  153.8 1.4 copy-done.2
  155.2 1.4 copy-done.4
  156.6 27.6 %step.1 = f32[6,32,8,4,1,128]{5,4,3,2,1,0:T(1,128)} custom-call(s32[512]{0:T(512)S(1)} %copy-done.5, f32[6]{0:T(128)S(1)} %copy-done.6, f32[6,32,8,8,1,128]{5,4,3,2,1,0:T(1,128)S(1)} %bitcast.16, f32[2,6,32,8,1,128]{5,4,3,2,1,0:T(1,128)S(1)} %copy-done.2, f32[2,6,32,8,1,128]{5,4,3,2,1,0:T(1,128)S(1)} %copy-done.4, f32[4,6,2,8,128]{4,3,2,1,0:T(8,128)S(1)} %bitcast.18, ...), custom_call_target="tpu_custom_call" | custom-call | tf_op jit(solution)/shard_map/step/pallas_call | solution.py:320
  (5 shorter events, 0.0 us)
Async XLA Ops:
  96.4 19.9 %collective-permute-start = (f32[2,6,32,8,1,128]{5,4,3,2,1,0:T(1,128)}, f32[2,6,32,8,1,128]{5,4,3,2,1,0:T(1,128)S(1)}, u32[]{:S(2)}, u32[]{:S(2)}) collective-permute-start(f32[2,6,32,8,1,128]{5,4,3,2,1,0:T(1,128)} %get-tuple-element.11), channel_id=1, source_target_pairs={{0,1},{1,2},{2,3},{3,4},{4,5},{5,6},{6,7},{7,8},{8,9},{9,10},{10,1... | collective-permute-start | bytes 4718600 | tf_op jit(solution)/shard_map/ppermute | solution.py:347
  98.7 52.3 %copy-start.5 = (s32[512]{0:T(512)S(1)}, s32[512]{0:T(512)}, u32[]{:S(2)}) copy-start(s32[512]{0:T(512)} %owner.3) | copy-start | bytes 6148
  98.7 52.3 %copy-start.6 = (f32[6]{0:T(128)S(1)}, f32[6]{0:T(128)}, u32[]{:S(2)}) copy-start(f32[6]{0:T(128)} %spread.1) | copy-start | bytes 76
  98.7 20.2 %collective-permute-start.1 = (f32[2,6,32,8,1,128]{5,4,3,2,1,0:T(1,128)}, f32[2,6,32,8,1,128]{5,4,3,2,1,0:T(1,128)S(1)}, u32[]{:S(2)}, u32[]{:S(2)}) collective-permute-start(f32[2,6,32,8,1,128]{5,4,3,2,1,0:T(1,128)} %get-tuple-element.12), channel_id=1, source_target_pairs={{0,127},{1,0},{2,1},{3,2},{4,3},{5,4},{6,5},{7,6},{8,7},{9,8},{10,... | collective-permute-start | bytes 4718600 | tf_op jit(solution)/shard_map/ppermute | solution.py:347
  116.4 2.6 %copy-start.1 = (f32[2,6,32,8,1,128]{5,4,3,2,1,0:T(1,128)}, f32[2,6,32,8,1,128]{5,4,3,2,1,0:T(1,128)S(1)}, u32[]{:S(2)}) copy-start(f32[2,6,32,8,1,128]{5,4,3,2,1,0:T(1,128)S(1)} %collective-permute-done.up) | copy-start | bytes 4718596
  118.9 1.2 copy-start.3
  134.8 11.2 %collective-permute-start.3 = (f32[4,6,2,8,1,128]{5,3,2,1,0,4:T(8,128)}, f32[4,6,2,8,1,128]{5,3,2,1,0,4:T(8,128)S(1)}, u32[]{:S(2)}, u32[]{:S(2)}) collective-permute-start(f32[4,6,2,8,1,128]{5,3,2,1,0,4:T(8,128)} %bitcast.20), channel_id=1, source_target_pairs={{32,0},{64,32},{96,64},{33,1},{65,33},{97,65},{34,2},{66,34},{98,6... | collective-permute-start | bytes 589832 | tf_op jit(solution)/shard_map/ppermute | solution.py:353
  136.9 9.1 %collective-permute-start.2 = (f32[4,6,2,8,1,128]{5,3,2,1,0,4:T(8,128)}, f32[4,6,2,8,1,128]{5,3,2,1,0,4:T(8,128)S(1)}, u32[]{:S(2)}, u32[]{:S(2)}) collective-permute-start(f32[4,6,2,8,1,128]{5,3,2,1,0,4:T(8,128)} %bitcast.19), channel_id=1, source_target_pairs={{0,32},{32,64},{64,96},{1,33},{33,65},{65,97},{2,34},{34,66},{66,9... | collective-permute-start | bytes 589832 | tf_op jit(solution)/shard_map/ppermute | solution.py:353
  140.1 6.3 %collective-permute-start.4 = (f32[4,6,16,128]{3,2,1,0:T(8,128)}, f32[4,6,16,128]{3,2,1,0:T(8,128)S(1)}, u32[]{:S(2)}, u32[]{:S(2)}) collective-permute-start(f32[4,6,16,128]{3,2,1,0:T(8,128)} %get-tuple-element.15), channel_id=1, source_target_pairs={{0,1},{1,2},{2,3},{3,4},{4,5},{5,6},{6,7},{7,8},{8,9},{9,10},{10,1... | collective-permute-start | bytes 589832 | tf_op jit(solution)/shard_map/ppermute | solution.py:353
  143.5 7.5 %collective-permute-start.5 = (f32[4,6,16,128]{3,2,1,0:T(8,128)}, f32[4,6,16,128]{3,2,1,0:T(8,128)S(1)}, u32[]{:S(2)}, u32[]{:S(2)}) collective-permute-start(f32[4,6,16,128]{3,2,1,0:T(8,128)} %get-tuple-element.16), channel_id=1, source_target_pairs={{1,0},{2,1},{3,2},{4,3},{5,4},{6,5},{7,6},{8,7},{9,8},{10,9},{11,1... | collective-permute-start | bytes 589832 | tf_op jit(solution)/shard_map/ppermute | solution.py:353
  151.0 2.8 %copy-start = (f32[8,6,32768]{2,0,1:T(8,128)S(1)}, f32[8,6,32768]{2,0,1:T(8,128)}, u32[]{:S(2)}) copy-start(f32[8,6,32768]{2,0,1:T(8,128)} %param.4) | copy-start | bytes 18874372
  153.8 1.4 copy-start.2
  155.2 1.4 copy-start.4
where the time goes:
time: 188 us; the launch traced here: 184 us
  Pallas kernels  139 us (74%)
  waiting for transfers between devices  25.2 us (13%)
  starting transfers between devices  13.5 us (7%)
  local copies, waits for them, and re-layouts  6.78 us (4%)
    pallas_call x1, Pallas kernels, pack(): pl.pallas_call(pack_body, name='pack', out_shape=(shape, shape), in_specs...  96.4 us
    pallas_call x1, Pallas kernels, step(): pl.pallas_call(step_body, name='step', out_shape=jax.ShapeDtypeStruct((F,...  27.6 us
    ppermute x2, waiting for transfers between devices, along_curve(): lax.ppermute(block, AXES, [(i, (i + distance) % count) for i in range(cou...  20.2 us
    pallas_call x1, Pallas kernels, edges(): pl.pallas_call(edges_body, name='edges', out_shape=(z_shape, z_shape, y_s...  14.6 us
    ppermute x4, starting transfers between devices, along_axis(): return lax.ppermute(block, axis, pairs)  11.2 us
    unnamed x14, local copies, waits for them, and re-layouts  6.78 us
    ppermute x4, waiting for transfers between devices, along_axis(): return lax.ppermute(block, axis, pairs)  4.96 us
  transfers between devices with their start and end apart: 6, of which 4 were waited for; matrix products, arithmetic and copies ran while one was open for 0% of the time, Pallas kernels for 0%

commit v1 on v0

v1 whole, which is shorter than its diff:
```python
import jax
import jax.numpy as jnp
from jax import lax
from jax.experimental import pallas as pl
from jax.experimental.pallas import tpu as pltpu
from jax.sharding import PartitionSpec as P

B = 32
F = 6
CAP = 4
ROWS = 8
LANES = 128
AXES = ("gx", "gy")
F32 = jnp.float32
HBM = pl.BlockSpec(memory_space=pl.ANY)
VMEM = pl.BlockSpec(memory_space=pltpu.VMEM)
SMEM = pl.BlockSpec(memory_space=pltpu.SMEM)
WIDE = 56 << 20


def run_all(copies):
    for copy in copies:
        copy.start()
    for copy in copies:
        copy.wait()


def pack_body(x, up, down, sem):
    copies = []
    for j in range(2):
        copies.append(pltpu.make_async_copy(x.at[:, :, :, 6 + j, 0], up.at[j], sem.at[j]))
        copies.append(pltpu.make_async_copy(x.at[:, :, :, j, 0], down.at[j], sem.at[2 + j]))
    run_all(copies)


def pack(x):
    shape = jax.ShapeDtypeStruct((2, F, B, ROWS, LANES), F32)
    return pl.pallas_call(
        pack_body,
        name="pack",
        out_shape=(shape, shape),
        in_specs=[HBM],
        out_specs=(VMEM, VMEM),
        scratch_shapes=[pltpu.SemaphoreType.DMA((4,))],
        compiler_params=pltpu.CompilerParams(vmem_limit_bytes=WIDE),
    )(x)


def device_number():
    return lax.axis_index("gx") * lax.axis_size("gy") + lax.axis_index("gy")


def kept_flags(owner):
    device = device_number()
    return [owner[device * CAP + c] == device for c in range(CAP)]


def from_box(kept, c, x, up, down, pick, target, sem):
    moved = (up if c < 2 else down).at[c % 2]

    @pl.when(kept)
    def _():
        pltpu.make_async_copy(pick(x.at[:, :, :, 2 + c]), target, sem).start()

    @pl.when(jnp.logical_not(kept))
    def _():
        pltpu.make_async_copy(pick(moved), target, sem).start()

    return pltpu.make_async_copy(pick(moved), target, sem)


def chunk_of_lane(shape):
    return lax.broadcasted_iota(jnp.int32, shape, len(shape) - 1) // 32


def layers(rows, j):
    chunk = chunk_of_lane(rows[0].shape)
    parts = [row if c == j else pltpu.roll(row, 32 * (c - j) % 128, 1) for c, row in enumerate(rows)]
    low = jnp.where(chunk == 0, parts[0], parts[1])
    high = jnp.where(chunk == 2, parts[2], parts[3])
    return jnp.where(chunk < 2, low, high)


def edges_body(owner, x, up, down, z_low, z_high, y_low, y_high, first, last, sem, sem_y):
    kept = kept_flags(owner)
    waits, waits_y = [], []
    for c in range(CAP):
        part = lambda row: (lambda ref: ref.at[:, :, row, 0])
        waits_y.append(from_box(kept[c], c, x, up, down, part(0), first.at[c], sem_y.at[c]))
        waits_y.append(from_box(kept[c], c, x, up, down, part(7), last.at[c], sem_y.at[4 + c]))
    for c in range(CAP):
        part = lambda z: (lambda ref: ref.at[:, z : z + 2, :, 0])
        waits.append(from_box(kept[c], c, x, up, down, part(0), z_low.at[c], sem.at[c]))
        waits.append(from_box(kept[c], c, x, up, down, part(30), z_high.at[c], sem.at[4 + c]))
    for wait in waits_y:
        wait.wait()
    for f in range(F):
        rows = [first[c, f] for c in range(CAP)]
        y_low[f, 0], y_low[f, 1] = layers(rows, 0), layers(rows, 1)
        rows = [last[c, f] for c in range(CAP)]
        y_high[f, 0], y_high[f, 1] = layers(rows, 2), layers(rows, 3)
    for wait in waits:
        wait.wait()


def edges(owner, x, up, down):
    z_shape = jax.ShapeDtypeStruct((CAP, F, 2, ROWS, LANES), F32)
    y_shape = jax.ShapeDtypeStruct((F, 2, B, LANES), F32)
    return pl.pallas_call(
        edges_body,
        name="edges",
        out_shape=(z_shape, z_shape, y_shape, y_shape),
        in_specs=[SMEM, HBM, HBM, HBM],
        out_specs=(VMEM, VMEM, VMEM, VMEM),
        scratch_shapes=[
            pltpu.VMEM((CAP, F, B, LANES), F32),
            pltpu.VMEM((CAP, F, B, LANES), F32),
            pltpu.SemaphoreType.DMA((8,)),
            pltpu.SemaphoreType.DMA((8,)),
        ],
        compiler_params=pltpu.CompilerParams(vmem_limit_bytes=WIDE),
    )(owner, x, up, down)


def minmod(a, b):
    return jnp.maximum(jnp.minimum(a, b), jnp.minimum(jnp.maximum(a, b), 0.0))


def conduction(v):
    return jnp.exp(0.5 * jnp.tanh(v))


def swap_64(a, b, lane):
    low = lane < 64
    m = pltpu.roll(jnp.where(low, b, a), 64, 1)
    return jnp.where(low, a, m), jnp.where(low, m, b)


def swap_32(a, b, lane):
    even = (lane & 32) == 0
    m = jnp.where(even, b, a)
    return jnp.where(even, a, pltpu.roll(m, 32, 1)), jnp.where(even, pltpu.roll(m, 96, 1), b)


LEAD = 5
J = range(4)


def step_body(
    owner, spread, x, up, down, z_below, z_above, y_below, y_above, out,
    box, q, result, left_d, left_n, right_q, right_m, right_c, carry_p, carry_n, carry_c,
    half, dx, dx_old, cx, cx_old, px, mx, nx, done, turned, sem, sem_z, sem_out,
):
    kept = kept_flags(owner)
    gx, gy = lax.axis_index("gx"), lax.axis_index("gy")
    last_x, last_y = lax.axis_size("gx") - 1, lax.axis_size("gy") - 1
    copies = [
        pltpu.make_async_copy(z_below, box.at[:, :, 0:2], sem_z.at[0]),
        pltpu.make_async_copy(z_above, box.at[:, :, B + 2 : B + 4], sem_z.at[1]),
    ]
    for copy in copies:
        copy.start()
    for c in range(CAP):
        copies.append(
            from_box(
                kept[c], c, x, up, down, lambda r: r.at[:, :, :, 0], box.at[c, :, 2 : B + 2], sem.at[c]
            )
        )
    for copy in copies:
        copy.wait()

    lane = lax.broadcasted_iota(jnp.int32, (8, LANES), 1)
    sub = lax.broadcasted_iota(jnp.int32, (8, LANES), 0)
    scale = [0.5 * spread[f] for f in range(F)]

    def turn_first(p):
        for f in range(F):
            v = [box[c, f, p] for c in range(CAP)]
            half[f, 0], half[f, 2] = swap_64(v[0], v[2], lane)
            half[f, 1], half[f, 3] = swap_64(v[1], v[3], lane)

    def turn(p, _):
        for f in range(F):
            q[f, p, 0], q[f, p, 1] = swap_32(half[f, 0], half[f, 1], lane)
            q[f, p, 2], q[f, p, 3] = swap_32(half[f, 2], half[f, 3], lane)
        turn_first(p)
        return 0

    turn_first(0)
    lax.fori_loop(1, B + 5, turn, 0)

    @pl.when(gx == 0)
    def _():
        for f in range(F):
            q[f, 1] = q[f, 3]
            q[f, 2] = q[f, 3]

    @pl.when(gx == last_x)
    def _():
        for f in range(F):
            q[f, B + 3] = q[f, B + 2]
            q[f, B + 4] = q[f, B + 2]

    for block in range(4):
        z0 = 8 * block
        span, rows = slice(z0, z0 + 8), slice(z0 + 8, z0 + 16)
        layer = lambda f, j, s: q[f, z0 + 3 : z0 + 11, j, s, :]

        def low(f):
            q0 = layer(f, 0, 0)
            first = gy == 0
            return (
                jnp.where(first, q0, y_below[f, 0, span, :]),
                jnp.where(first, q0, y_below[f, 1, span, :]),
                q0,
                layer(f, 1, 0),
            )

        def high(f):
            q31 = layer(f, 3, 7)
            end = gy == last_y
            return (
                q31,
                jnp.where(end, q31, y_above[f, 0, span, :]),
                jnp.where(end, q31, y_above[f, 1, span, :]),
            )

        _, v1, v0, _ = low(1)
        weight = 0.0625 * (v1 + v0)
        _, v1, v0, _ = low(5)
        cond = conduction(v1) + conduction(v0)
        right_c[rows, :] = conduction(high(5)[1])
        for f in range(F):
            qm2, qm1, q0, q1 = low(f)
            d = q0 - qm1
            p = (qm1 + qm1) + minmod(qm1 - qm2, d)
            m = (q0 + q0) - minmod(d, q1 - q0)
            left_d[f, rows, :] = d
            left_n[f, rows, :] = (scale[f] * cond) * d - weight * jnp.where(weight > 0.0, p, m)
            q31, q32, q33 = high(f)
            right_q[f, rows, :] = q32
            right_m[f, rows, :] = (q32 + q32) - minmod(q32 - q31, q33 - q32)

    def y_next(value, row):
        return pltpu.roll(jnp.where(sub == 0, row, value), 7, 0)

    def y_last(value, row):
        return pltpu.roll(jnp.where(sub == 7, row, value), 1, 0)

    def x_next(value, ends):
        return jnp.where(lane == 127, ends, pltpu.roll(value, 127, 1))

    def x_last(value, ends):
        return jnp.where(lane == 0, ends, pltpu.roll(value, 1, 1))

    def plane(i, _):
        for f in range(F):
            for j in (0, 2):
                result[j, f, i], result[j + 1, f, i] = swap_32(turned[f, j], turned[f, j + 1], lane)
        for f in range(F):
            for j in (0, 1):
                turned[f, j], turned[f, j + 2] = swap_64(done[f, j], done[f, j + 2], lane)

        row = pl.ds(i + 5, 1)
        here = [carry_c[j] for j in J]
        above = [conduction(q[5, i + 1, j]) for j in J]
        cond_z = [a + b for a, b in zip(here, above)]
        for j in J:
            carry_c[j] = above[j]
        beyond = here[1:] + [y_next(here[0], right_c[row, :])]
        cond_y = [a + b for a, b in zip(here, beyond)]
        v = [q[1, i, j] for j in J]
        beyond = v[1:] + [y_next(v[0], right_q[1, row, :])]
        weight_y = [0.0625 * (a + b) for a, b in zip(v, beyond)]
        weight_z = [0.0625 * (q[2, i, j] + q[2, i + 1, j]) for j in J]
        edge_x = [-0.125 * q[0, i, j] for j in J]
        for f in range(F):
            value = [q[f, i, j] for j in J]
            twice = [a + a for a in value]
            total = []
            for j in J:
                after = q[f, i + 1, j]
                d = after - value[j]
                slope = minmod(d, q[f, i + 2, j] - after)
                double = after + after
                state = jnp.where(weight_z[j] > 0.0, carry_p[f, j], double - slope)
                carry_p[f, j] = double + slope
                net = (scale[f] * cond_z[j]) * d - weight_z[j] * state
                total.append(value[j] + (net - carry_n[f, j]))
                carry_n[f, j] = net
            beyond = value[1:] + [y_next(value[0], right_q[f, row, :])]
            d = [b - a for a, b in zip(value, beyond)]
            before = [y_last(d[3], left_d[f, row, :])] + d[:3]
            slope = [minmod(a, b) for a, b in zip(before, d)]
            right = [a - b for a, b in zip(twice, slope)]
            right = right[1:] + [y_next(right[0], right_m[f, row, :])]
            net = []
            for j in J:
                state = jnp.where(weight_y[j] > 0.0, twice[j] + slope[j], right[j])
                net.append((scale[f] * cond_y[j]) * d[j] - weight_y[j] * state)
            before = [y_last(net[3], left_n[f, row, :])] + net[:3]
            for j in J:
                n = nx[f, j]
                t = total[j] + (net[j] - before[j])
                done[f, j] = t + (n - x_last(n, edge_x[j] * twice[j]))
        for j in J:
            u = q[0, i + 1, j]
            weight = 0.0625 * ((u + u) + dx_old[0, j])
            cond = cx_old[j]
            for f in range(F):
                a = q[f, i + 1, j]
                state = jnp.where(weight > 0.0, px[f, j], x_next(mx[f, j], a + a))
                nx[f, j] = (scale[f] * cond) * dx_old[f, j] - weight * state
        for j in J:
            cx_old[j] = cx[j]
            for f in range(F):
                a, d = q[f, i + 2, j], dx[f, j]
                slope = minmod(x_last(d, 0.0), d)
                px[f, j], mx[f, j] = (a + a) + slope, (a + a) - slope
                dx_old[f, j] = d
        for j in J:
            c = conduction(q[5, i + 3, j])
            cx[j] = c + x_next(c, c)
            for f in range(F):
                a = q[f, i + 3, j]
                dx[f, j] = x_next(a, a) - a
        return 0

    lax.fori_loop(0, B + LEAD, plane, 0)
    run_all(
        [
            pltpu.make_async_copy(result.at[c, :, LEAD:], out.at[:, :, :, c, 0], sem_out.at[c])
            for c in range(CAP)
        ]
    )


def step(owner, spread, x, up, down, z_below, z_above, y_below, y_above):
    planes = lambda *lead: pltpu.VMEM((*lead, ROWS, LANES), F32)
    rows = pltpu.VMEM((F, B + 16, LANES), F32)
    return pl.pallas_call(
        step_body,
        name="step",
        out_shape=jax.ShapeDtypeStruct((F, B, ROWS, CAP, 1, LANES), F32),
        in_specs=[SMEM, SMEM, HBM, HBM, HBM, HBM, HBM, VMEM, VMEM],
        out_specs=HBM,
        scratch_shapes=[
            planes(CAP, F, B + 5),
            planes(F, B + 8, 4),
            planes(CAP, F, B + LEAD),
            rows,
            rows,
            rows,
            rows,
            pltpu.VMEM((B + 16, LANES), F32),
            planes(F, 4),
            planes(F, 4),
            planes(4),
            planes(F, 4),
            planes(F, 4),
            planes(F, 4),
            planes(4),
            planes(4),
            planes(F, 4),
            planes(F, 4),
            planes(F, 4),
            planes(F, 4),
            planes(F, 4),
            pltpu.SemaphoreType.DMA((CAP,)),
            pltpu.SemaphoreType.DMA((2,)),
            pltpu.SemaphoreType.DMA((CAP,)),
        ],
        compiler_params=pltpu.CompilerParams(vmem_limit_bytes=WIDE),
    )(owner, spread, x, up, down, z_below, z_above, y_below, y_above)


def along_curve(block, distance):
    count = lax.axis_size(AXES)
    return lax.ppermute(block, AXES, [(i, (i + distance) % count) for i in range(count)])


def along_axis(block, axis, distance):
    count = lax.axis_size(axis)
    pairs = [(i, i + distance) for i in range(count) if 0 <= i + distance < count]
    return lax.ppermute(block, axis, pairs)


def local(old_state, old_owner, old_slot, diffusivity):
    x = old_state.reshape(8, F, B, ROWS, LANES).transpose(1, 2, 3, 0, 4)[..., None, :]
    up, down = pack(x)
    up = along_curve(up, 1)[..., None, :]
    down = along_curve(down, -1)[..., None, :]
    z_low, z_high, y_low, y_high = edges(old_owner, x, up, down)
    z_below = along_axis(z_high, "gx", 1)
    z_above = along_axis(z_low, "gx", -1)
    y_below = along_axis(y_high, "gy", 1)
    y_above = along_axis(y_low, "gy", -1)
    out = step(old_owner, diffusivity, x, up, down, z_below, z_above, y_below, y_above)
    return out[..., 0, :].transpose(3, 0, 1, 2, 4).reshape(CAP, F, B * B * B)


def solution(mesh):
    placed = (P(AXES, None, None), P(), P(), P())
    return jax.shard_map(
        local, mesh=mesh, in_specs=placed, out_specs=P(AXES, None, None), check_vma=False
    )
```

time: 188 us -> 68.9 us (0.37)
  the two profiles are of different devices: /device:TPU:27 before, /device:TPU:111 now
where the time goes in v1:
time: 68.9 us; the launch traced here: 68.6 us
  waiting for transfers between devices  29.2 us (42%)
  Pallas kernels  26.4 us (38%)
  starting transfers between devices  11.1 us (16%)
  local copies, waits for them, and re-layouts  1.83 us (3%)
    ppermute x2, waiting for transfers between devices, along_curve(): lax.ppermute(block, AXES, [(i, (i + distance) % count) for i in range(cou...  21.9 us
    pallas_call x1, Pallas kernels, step(): pl.pallas_call(step_body, name='step', out_shape=jax.ShapeDtypeStruct((F,...  19.5 us
    ppermute x4, starting transfers between devices, along_axis(): return lax.ppermute(block, axis, pairs)  10.2 us
    ppermute x4, waiting for transfers between devices, along_axis(): return lax.ppermute(block, axis, pairs)  7.34 us
    pallas_call x1, Pallas kernels, pack(): pl.pallas_call(pack_body, name='pack', out_shape=(shape, shape), in_specs...  3.59 us
    pallas_call x1, Pallas kernels, edges(): pl.pallas_call(edges_body, name='edges', out_shape=(z_shape, z_shape, y_s...  3.33 us
    unnamed x12, local copies, waits for them, and re-layouts  1.83 us
  transfers between devices with their start and end apart: 6, of which 4 were waited for; matrix products, arithmetic and copies ran while one was open for 0% of the time, Pallas kernels for 0%

profile of v1, /device:TPU:111, one launch (start us, length us, event | category | flops | bytes accessed | tf_op | source)
XLA Modules:
  0.0 68.6 jit_solution(1800272013930960194)
XLA Ops:
  0.0 3.6 %pack.1 = (f32[2,6,32,8,128]{4,3,2,1,0:T(8,128)}, f32[2,6,32,8,128]{4,3,2,1,0:T(8,128)}) custom-call(f32[6,32,8,8,1,128]{5,4,3,2,1,0:T(1,128)} %bitcast.12), custom_call_target="tpu_custom_call" | custom-call | tf_op jit(solution)/shard_map/pack/pallas_call | solution.py:38
  3.6 0.6 collective-permute-start
  4.2 0.3 collective-permute-start.1
  4.4 17.4 %collective-permute-done = f32[2,6,32,8,128]{4,3,2,1,0:T(8,128)S(1)} collective-permute-done((f32[2,6,32,8,128]{4,3,2,1,0:T(8,128)}, f32[2,6,32,8,128]{4,3,2,1,0:T(8,128)S(1)}, u32[]{:S(2)}, u32[]{:S(2)}) %collective-permute-start) | collective-permute-done | bytes 1572896 | tf_op jit(solution)/shard_map/ppermute | solution.py:379
  21.8 4.5 %collective-permute-done.1 = f32[2,6,32,8,128]{4,3,2,1,0:T(8,128)S(1)} collective-permute-done((f32[2,6,32,8,128]{4,3,2,1,0:T(8,128)}, f32[2,6,32,8,128]{4,3,2,1,0:T(8,128)S(1)}, u32[]{:S(2)}, u32[]{:S(2)}) %collective-permute-start.1) | collective-permute-done | bytes 1572896 | tf_op jit(solution)/shard_map/ppermute | solution.py:379
  26.3 0.0 copy-done
  26.3 1.1 %copy-done.1 = f32[2,6,32,8,128]{4,3,2,1,0:T(8,128)} copy-done((f32[2,6,32,8,128]{4,3,2,1,0:T(8,128)}, f32[2,6,32,8,128]{4,3,2,1,0:T(8,128)S(1)}, u32[]{:S(2)}) %copy-start.1) | copy-done | bytes 1572888
  27.5 3.3 %edges.1 = (f32[4,6,2,8,128]{4,3,2,1,0:T(8,128)}, f32[4,6,2,8,128]{4,3,2,1,0:T(8,128)}, f32[6,2,32,128]{3,2,1,0:T(8,128)}, f32[6,2,32,128]{3,2,1,0:T(8,128)}) custom-call(s32[512]{0:T(512)} %owner.3, f32[6,32,8,8,1,128]{5,4,3,2,1,0:T(1,128)} %bitcast.13, f32[2,6,32,8,1,128]{5,4,3,2,1,0:T(1,128)} %bitcast.15, f32[2,6,32,8,1,128]{5,4,3,2,1,0:T(1,128)} %bitcast.17), custom_call_target="tpu_custom_call" | custom-call | tf_op jit(solution)/shard_map/edges/pallas_call | solution.py:109
  30.8 1.3 %collective-permute-start.2 = (f32[4,6,2,8,128]{4,3,2,1,0:T(8,128)}, f32[4,6,2,8,128]{4,3,2,1,0:T(8,128)S(1)}, u32[]{:S(2)}, u32[]{:S(2)}) collective-permute-start(f32[4,6,2,8,128]{4,3,2,1,0:T(8,128)} %get-tuple-element.13), channel_id=1, source_target_pairs={{0,32},{32,64},{64,96},{1,33},{33,65},{65,97},{2,34},{34,66},{66,9... | collective-permute-start | bytes 589832 | tf_op jit(solution)/shard_map/ppermute | solution.py:385
  32.1 4.0 %collective-permute-start.3 = (f32[4,6,2,8,128]{4,3,2,1,0:T(8,128)}, f32[4,6,2,8,128]{4,3,2,1,0:T(8,128)S(1)}, u32[]{:S(2)}, u32[]{:S(2)}) collective-permute-start(f32[4,6,2,8,128]{4,3,2,1,0:T(8,128)} %get-tuple-element.14), channel_id=1, source_target_pairs={{32,0},{64,32},{96,64},{33,1},{65,33},{97,65},{34,2},{66,34},{98,6... | collective-permute-start | bytes 589832 | tf_op jit(solution)/shard_map/ppermute | solution.py:385
  36.1 3.0 %collective-permute-start.4 = (f32[6,2,32,128]{3,2,1,0:T(8,128)}, f32[6,2,32,128]{3,2,1,0:T(8,128)S(1)}, u32[]{:S(2)}, u32[]{:S(2)}) collective-permute-start(f32[6,2,32,128]{3,2,1,0:T(8,128)} %get-tuple-element.15), channel_id=1, source_target_pairs={{0,1},{1,2},{2,3},{3,4},{4,5},{5,6},{6,7},{7,8},{8,9},{9,10},{10,1... | collective-permute-start | bytes 589832 | tf_op jit(solution)/shard_map/ppermute | solution.py:385
  39.1 1.9 %collective-permute-start.5 = (f32[6,2,32,128]{3,2,1,0:T(8,128)}, f32[6,2,32,128]{3,2,1,0:T(8,128)S(1)}, u32[]{:S(2)}, u32[]{:S(2)}) collective-permute-start(f32[6,2,32,128]{3,2,1,0:T(8,128)} %get-tuple-element.16), channel_id=1, source_target_pairs={{1,0},{2,1},{3,2},{4,3},{5,4},{6,5},{7,6},{8,7},{9,8},{10,9},{11,1... | collective-permute-start | bytes 589832 | tf_op jit(solution)/shard_map/ppermute | solution.py:385
  41.1 0.0 collective-permute-done.2.z_below
  41.1 0.0 copy-start.2
  41.1 0.0 collective-permute-done.3.z_above
  41.1 0.0 copy-start.3
  41.1 0.9 %collective-permute-done.4.y_below = f32[6,2,32,128]{3,2,1,0:T(8,128)S(1)} collective-permute-done((f32[6,2,32,128]{3,2,1,0:T(8,128)}, f32[6,2,32,128]{3,2,1,0:T(8,128)S(1)}, u32[]{:S(2)}, u32[]{:S(2)}) %collective-permute-start.4) | collective-permute-done | bytes 196640 | tf_op jit(solution)/shard_map/ppermute | solution.py:385
  42.0 6.4 %collective-permute-done.5.y_above = f32[6,2,32,128]{3,2,1,0:T(8,128)S(1)} collective-permute-done((f32[6,2,32,128]{3,2,1,0:T(8,128)}, f32[6,2,32,128]{3,2,1,0:T(8,128)S(1)}, u32[]{:S(2)}, u32[]{:S(2)}) %collective-permute-start.5) | collective-permute-done | bytes 196640 | tf_op jit(solution)/shard_map/ppermute | solution.py:385
  48.4 0.0 copy-done.2
  48.4 0.0 copy-done.3
  48.4 0.0 copy-done.4
  48.5 0.0 copy-start.5
  48.5 0.7 copy-done.5
  49.1 19.5 %step.1 = f32[6,32,8,4,1,128]{5,4,3,2,1,0:T(1,128)} custom-call(s32[512]{0:T(512)} %owner.3, f32[6]{0:T(128)} %spread.1, f32[6,32,8,8,1,128]{5,4,3,2,1,0:T(1,128)} %bitcast.14, f32[2,6,32,8,1,128]{5,4,3,2,1,0:T(1,128)} %bitcast.16, f32[2,6,32,8,1,128]{5,4,3,2,1,0:T(1,128)} %bitcast.18, f32[4,6,2,8,128]{4,3,2,1,0:T(8,128)} %copy-done.2, ...), custom_call_target="tpu_custom_call" | custom-call | tf_op jit(solution)/shard_map/step/pallas_call | solution.py:341
  (3 shorter events, 0.0 us)
Async XLA Ops:
  3.6 18.2 %collective-permute-start = (f32[2,6,32,8,128]{4,3,2,1,0:T(8,128)}, f32[2,6,32,8,128]{4,3,2,1,0:T(8,128)S(1)}, u32[]{:S(2)}, u32[]{:S(2)}) collective-permute-start(f32[2,6,32,8,128]{4,3,2,1,0:T(8,128)} %get-tuple-element.11), channel_id=1, source_target_pairs={{0,1},{1,2},{2,3},{3,4},{4,5},{5,6},{6,7},{7,8},{8,9},{9,10},{10,1... | collective-permute-start | bytes 4718600 | tf_op jit(solution)/shard_map/ppermute | solution.py:379
  4.2 22.2 %collective-permute-start.1 = (f32[2,6,32,8,128]{4,3,2,1,0:T(8,128)}, f32[2,6,32,8,128]{4,3,2,1,0:T(8,128)S(1)}, u32[]{:S(2)}, u32[]{:S(2)}) collective-permute-start(f32[2,6,32,8,128]{4,3,2,1,0:T(8,128)} %get-tuple-element.12), channel_id=1, source_target_pairs={{0,127},{1,0},{2,1},{3,2},{4,3},{5,4},{6,5},{7,6},{8,7},{9,8},{10,... | collective-permute-start | bytes 4718600 | tf_op jit(solution)/shard_map/ppermute | solution.py:379
  21.8 4.5 %copy-start = (f32[2,6,32,8,128]{4,3,2,1,0:T(8,128)}, f32[2,6,32,8,128]{4,3,2,1,0:T(8,128)S(1)}, u32[]{:S(2)}) copy-start(f32[2,6,32,8,128]{4,3,2,1,0:T(8,128)S(1)} %collective-permute-done) | copy-start | bytes 4718596
  26.3 1.1 %copy-start.1 = (f32[2,6,32,8,128]{4,3,2,1,0:T(8,128)}, f32[2,6,32,8,128]{4,3,2,1,0:T(8,128)S(1)}, u32[]{:S(2)}) copy-start(f32[2,6,32,8,128]{4,3,2,1,0:T(8,128)S(1)} %collective-permute-done.1) | copy-start | bytes 4718596
  30.8 10.3 %collective-permute-start.2 = (f32[4,6,2,8,128]{4,3,2,1,0:T(8,128)}, f32[4,6,2,8,128]{4,3,2,1,0:T(8,128)S(1)}, u32[]{:S(2)}, u32[]{:S(2)}) collective-permute-start(f32[4,6,2,8,128]{4,3,2,1,0:T(8,128)} %get-tuple-element.13), channel_id=1, source_target_pairs={{0,32},{32,64},{64,96},{1,33},{33,65},{65,97},{2,34},{34,66},{66,9... | collective-permute-start | bytes 589832 | tf_op jit(solution)/shard_map/ppermute | solution.py:385
  32.1 9.0 %collective-permute-start.3 = (f32[4,6,2,8,128]{4,3,2,1,0:T(8,128)}, f32[4,6,2,8,128]{4,3,2,1,0:T(8,128)S(1)}, u32[]{:S(2)}, u32[]{:S(2)}) collective-permute-start(f32[4,6,2,8,128]{4,3,2,1,0:T(8,128)} %get-tuple-element.14), channel_id=1, source_target_pairs={{32,0},{64,32},{96,64},{33,1},{65,33},{97,65},{34,2},{66,34},{98,6... | collective-permute-start | bytes 589832 | tf_op jit(solution)/shard_map/ppermute | solution.py:385
  36.1 5.9 %collective-permute-start.4 = (f32[6,2,32,128]{3,2,1,0:T(8,128)}, f32[6,2,32,128]{3,2,1,0:T(8,128)S(1)}, u32[]{:S(2)}, u32[]{:S(2)}) collective-permute-start(f32[6,2,32,128]{3,2,1,0:T(8,128)} %get-tuple-element.15), channel_id=1, source_target_pairs={{0,1},{1,2},{2,3},{3,4},{4,5},{5,6},{6,7},{7,8},{8,9},{9,10},{10,1... | collective-permute-start | bytes 589832 | tf_op jit(solution)/shard_map/ppermute | solution.py:385
  39.1 9.3 %collective-permute-start.5 = (f32[6,2,32,128]{3,2,1,0:T(8,128)}, f32[6,2,32,128]{3,2,1,0:T(8,128)S(1)}, u32[]{:S(2)}, u32[]{:S(2)}) collective-permute-start(f32[6,2,32,128]{3,2,1,0:T(8,128)} %get-tuple-element.16), channel_id=1, source_target_pairs={{1,0},{2,1},{3,2},{4,3},{5,4},{6,5},{7,6},{8,7},{9,8},{10,9},{11,1... | collective-permute-start | bytes 589832 | tf_op jit(solution)/shard_map/ppermute | solution.py:385
  41.1 7.4 %copy-start.2 = (f32[4,6,2,8,128]{4,3,2,1,0:T(8,128)}, f32[4,6,2,8,128]{4,3,2,1,0:T(8,128)S(1)}, u32[]{:S(2)}) copy-start(f32[4,6,2,8,128]{4,3,2,1,0:T(8,128)S(1)} %collective-permute-done.2.z_below) | copy-start | bytes 589828
  41.1 7.4 %copy-start.3 = (f32[4,6,2,8,128]{4,3,2,1,0:T(8,128)}, f32[4,6,2,8,128]{4,3,2,1,0:T(8,128)S(1)}, u32[]{:S(2)}) copy-start(f32[4,6,2,8,128]{4,3,2,1,0:T(8,128)S(1)} %collective-permute-done.3.z_above) | copy-start | bytes 589828
  42.0 6.4 %copy-start.4 = (f32[6,2,32,128]{3,2,1,0:T(8,128)}, f32[6,2,32,128]{3,2,1,0:T(8,128)S(1)}, u32[]{:S(2)}) copy-start(f32[6,2,32,128]{3,2,1,0:T(8,128)S(1)} %collective-permute-done.4.y_below) | copy-start | bytes 589828
  48.5 0.7 copy-start.5

commit v2 on v1

--- a/solution.py
+++ b/solution.py
@@ -25,25 +25,74 @@
         copy.wait()
 
 
-def pack_body(x, up, down, sem):
+def shell_body(x, up, down, first, last, sem, sem_y):
+    waits, waits_y = [], []
+    for k in range(4):
+        target, slot = (up, 6 + k) if k < 2 else (down, k - 2)
+        shell = target.at[k % 2]
+        waits_y.append(pltpu.make_async_copy(x.at[:, :, 0, slot, 0], first.at[k], sem_y.at[k]))
+        waits_y.append(pltpu.make_async_copy(x.at[:, :, 7, slot, 0], last.at[k], sem_y.at[4 + k]))
+        waits.append(pltpu.make_async_copy(x.at[:, 0:2, :, slot, 0], shell.at[:, 0:2], sem.at[k]))
+        waits.append(
+            pltpu.make_async_copy(x.at[:, 30:32, :, slot, 0], shell.at[:, 2:4], sem.at[4 + k])
+        )
+    for copy in waits_y + waits:
+        copy.start()
+    for copy in waits_y:
+        copy.wait()
+    left = lax.broadcasted_iota(jnp.int32, (8, LANES), 1) < 64
+    for k in range(4):
+        target = up if k < 2 else down
+        for f in range(F):
+            for b in range(4):
+                span = slice(8 * b, 8 * b + 8)
+                target[k % 2, f, 4 + b] = jnp.where(left, first[k, f, span, :], last[k, f, span, :])
+    for copy in waits:
+        copy.wait()
+
+
+def inner_body(x, up, down, sem):
     copies = []
     for j in range(2):
-        copies.append(pltpu.make_async_copy(x.at[:, :, :, 6 + j, 0], up.at[j], sem.at[j]))
-        copies.append(pltpu.make_async_copy(x.at[:, :, :, j, 0], down.at[j], sem.at[2 + j]))
+        copies.append(pltpu.make_async_copy(x.at[:, 2:30, :, 6 + j, 0], up.at[j], sem.at[j]))
+        copies.append(pltpu.make_async_copy(x.at[:, 2:30, :, j, 0], down.at[j], sem.at[2 + j]))
     run_all(copies)
 
 
-def pack(x):
-    shape = jax.ShapeDtypeStruct((2, F, B, ROWS, LANES), F32)
+def hold_body(x, hold, sem):
+    run_all(
+        [pltpu.make_async_copy(x.at[:, :, :, 2 + c, 0], hold.at[c], sem.at[c]) for c in range(CAP)]
+    )
+
+
+def from_slots(body, name, x, shapes, scratch, micros):
+    shapes = tuple(jax.ShapeDtypeStruct(shape, F32) for shape in shapes)
     return pl.pallas_call(
-        pack_body,
-        name="pack",
-        out_shape=(shape, shape),
+        body,
+        name=name,
+        out_shape=shapes,
         in_specs=[HBM],
-        out_specs=(VMEM, VMEM),
-        scratch_shapes=[pltpu.SemaphoreType.DMA((4,))],
+        out_specs=(VMEM,) * len(shapes),
+        scratch_shapes=scratch,
         compiler_params=pltpu.CompilerParams(vmem_limit_bytes=WIDE),
+        cost_estimate=pl.CostEstimate(flops=0, bytes_accessed=micros * 3000000, transcendentals=0),
     )(x)
+
+
+def shell(x):
+    rows = pltpu.VMEM((4, F, B, LANES), F32)
+    sems = pltpu.SemaphoreType.DMA((8,))
+    return from_slots(shell_body, "shell", x, [(2, F, 8, ROWS, LANES)] * 2, [rows, rows, sems, sems], 2)
+
+
+def inner(x):
+    sems = pltpu.SemaphoreType.DMA((4,))
+    return from_slots(inner_body, "inner", x, [(2, F, 28, ROWS, LANES)] * 2, [sems], 3)
+
+
+def held(x):
+    sems = pltpu.SemaphoreType.DMA((4,))
+    return from_slots(hold_body, "held", x, [(CAP, F, B, ROWS, LANES)], [sems], 4)[0]
 
 
 def device_number():
@@ -55,71 +104,56 @@
     return [owner[device * CAP + c] == device for c in range(CAP)]
 
 
-def from_box(kept, c, x, up, down, pick, target, sem):
-    moved = (up if c < 2 else down).at[c % 2]
-
-    @pl.when(kept)
-    def _():
-        pltpu.make_async_copy(pick(x.at[:, :, :, 2 + c]), target, sem).start()
-
-    @pl.when(jnp.logical_not(kept))
-    def _():
-        pltpu.make_async_copy(pick(moved), target, sem).start()
-
-    return pltpu.make_async_copy(pick(moved), target, sem)
-
-
-def chunk_of_lane(shape):
-    return lax.broadcasted_iota(jnp.int32, shape, len(shape) - 1) // 32
-
-
-def layers(rows, j):
-    chunk = chunk_of_lane(rows[0].shape)
-    parts = [row if c == j else pltpu.roll(row, 32 * (c - j) % 128, 1) for c, row in enumerate(rows)]
-    low = jnp.where(chunk == 0, parts[0], parts[1])
-    high = jnp.where(chunk == 2, parts[2], parts[3])
-    return jnp.where(chunk < 2, low, high)
-
-
-def edges_body(owner, x, up, down, z_low, z_high, y_low, y_high, first, last, sem, sem_y):
+def swap_64(a, b, lane):
+    low = lane < 64
+    m = pltpu.roll(jnp.where(low, b, a), 64, 1)
+    return jnp.where(low, a, m), jnp.where(low, m, b)
+
+
+def swap_32(a, b, lane):
+    even = (lane & 32) == 0
+    m = jnp.where(even, b, a)
+    return jnp.where(even, a, pltpu.roll(m, 32, 1)), jnp.where(even, pltpu.roll(m, 96, 1), b)
+
+
+def turned_to_layers(v, lane):
+    a, c = swap_64(v[0], v[2], lane)
+    b, d = swap_64(v[1], v[3], lane)
+    return *swap_32(a, b, lane), *swap_32(c, d, lane)
+
+
+def edges_body(owner, hold, up, down, z_low, z_high, y_low, y_high):
     kept = kept_flags(owner)
-    waits, waits_y = [], []
-    for c in range(CAP):
-        part = lambda row: (lambda ref: ref.at[:, :, row, 0])
-        waits_y.append(from_box(kept[c], c, x, up, down, part(0), first.at[c], sem_y.at[c]))
-        waits_y.append(from_box(kept[c], c, x, up, down, part(7), last.at[c], sem_y.at[4 + c]))
-    for c in range(CAP):
-        part = lambda z: (lambda ref: ref.at[:, z : z + 2, :, 0])
-        waits.append(from_box(kept[c], c, x, up, down, part(0), z_low.at[c], sem.at[c]))
-        waits.append(from_box(kept[c], c, x, up, down, part(30), z_high.at[c], sem.at[4 + c]))
-    for wait in waits_y:
-        wait.wait()
+    moved = [(up if c < 2 else down).at[c % 2] for c in range(CAP)]
+    lane = lax.broadcasted_iota(jnp.int32, (8, LANES), 1)
     for f in range(F):
-        rows = [first[c, f] for c in range(CAP)]
-        y_low[f, 0], y_low[f, 1] = layers(rows, 0), layers(rows, 1)
-        rows = [last[c, f] for c in range(CAP)]
-        y_high[f, 0], y_high[f, 1] = layers(rows, 2), layers(rows, 3)
-    for wait in waits:
-        wait.wait()
-
-
-def edges(owner, x, up, down):
-    z_shape = jax.ShapeDtypeStruct((CAP, F, 2, ROWS, LANES), F32)
+        for k, z in enumerate((0, 1, 30, 31)):
+            v = [jnp.where(kept[c], hold[c, f, z], moved[c][f, k]) for c in range(CAP)]
+            target = (z_low if k < 2 else z_high).at[f, k % 2]
+            for j, value in enumerate(turned_to_layers(v, lane)):
+                target[j] = value
+        for b in range(4):
+            span = slice(8 * b, 8 * b + 8)
+            rows = []
+            for c in range(CAP):
+                here = jnp.where(lane < 64, hold[c, f, span, 0, :], hold[c, f, span, 7, :])
+                rows.append(jnp.where(kept[c], here, moved[c][f, 4 + b]))
+            for j, value in enumerate(turned_to_layers(rows, lane)):
+                (y_low if j < 2 else y_high)[f, j % 2, span, :] = value
+
+
+def edges(owner, hold, up, down):
+    z_shape = jax.ShapeDtypeStruct((F, 2, 4, ROWS, LANES), F32)
     y_shape = jax.ShapeDtypeStruct((F, 2, B, LANES), F32)
     return pl.pallas_call(
         edges_body,
         name="edges",
         out_shape=(z_shape, z_shape, y_shape, y_shape),
-        in_specs=[SMEM, HBM, HBM, HBM],
+        in_specs=[SMEM, VMEM, VMEM, VMEM],
         out_specs=(VMEM, VMEM, VMEM, VMEM),
-        scratch_shapes=[
-            pltpu.VMEM((CAP, F, B, LANES), F32),
-            pltpu.VMEM((CAP, F, B, LANES), F32),
-            pltpu.SemaphoreType.DMA((8,)),
-            pltpu.SemaphoreType.DMA((8,)),
-        ],
-        compiler_params=pltpu.CompilerParams(vmem_limit_bytes=WIDE),
-    )(owner, x, up, down)
+        compiler_params=pltpu.CompilerParams(vmem_limit_bytes=16 << 20),
+        cost_estimate=pl.CostEstimate(flops=0, bytes_accessed=6000000, transcendentals=0),
+    )(owner, hold, up, down)
 
 
 def minmod(a, b):
@@ -130,76 +164,58 @@
     return jnp.exp(0.5 * jnp.tanh(v))
 
 
-def swap_64(a, b, lane):
-    low = lane < 64
-    m = pltpu.roll(jnp.where(low, b, a), 64, 1)
-    return jnp.where(low, a, m), jnp.where(low, m, b)
-
-
-def swap_32(a, b, lane):
-    even = (lane & 32) == 0
-    m = jnp.where(even, b, a)
-    return jnp.where(even, a, pltpu.roll(m, 32, 1)), jnp.where(even, pltpu.roll(m, 96, 1), b)
-
-
 LEAD = 5
 J = range(4)
 
 
 def step_body(
-    owner, spread, x, up, down, z_below, z_above, y_below, y_above, out,
-    box, q, result, left_d, left_n, right_q, right_m, right_c, carry_p, carry_n, carry_c,
-    half, dx, dx_old, cx, cx_old, px, mx, nx, done, turned, sem, sem_z, sem_out,
+    owner, spread, hold, shell_up, shell_down, up, down, z_below, z_above, y_below, y_above, out,
+    q, result, left_d, left_n, right_q, right_m, right_c, carry_p, carry_n, carry_c,
+    half, dx, dx_old, cx, cx_old, px, mx, nx, done, turned, sem_out,
 ):
     kept = kept_flags(owner)
     gx, gy = lax.axis_index("gx"), lax.axis_index("gy")
     last_x, last_y = lax.axis_size("gx") - 1, lax.axis_size("gy") - 1
-    copies = [
-        pltpu.make_async_copy(z_below, box.at[:, :, 0:2], sem_z.at[0]),
-        pltpu.make_async_copy(z_above, box.at[:, :, B + 2 : B + 4], sem_z.at[1]),
-    ]
-    for copy in copies:
-        copy.start()
-    for c in range(CAP):
-        copies.append(
-            from_box(
-                kept[c], c, x, up, down, lambda r: r.at[:, :, :, 0], box.at[c, :, 2 : B + 2], sem.at[c]
-            )
-        )
-    for copy in copies:
-        copy.wait()
-
     lane = lax.broadcasted_iota(jnp.int32, (8, LANES), 1)
     sub = lax.broadcasted_iota(jnp.int32, (8, LANES), 0)
     scale = [0.5 * spread[f] for f in range(F)]
 
-    def turn_first(p):
-        for f in range(F):
-            v = [box[c, f, p] for c in range(CAP)]
-            half[f, 0], half[f, 2] = swap_64(v[0], v[2], lane)
-            half[f, 1], half[f, 3] = swap_64(v[1], v[3], lane)
-
-    def turn(p, _):
-        for f in range(F):
-            q[f, p, 0], q[f, p, 1] = swap_32(half[f, 0], half[f, 1], lane)
-            q[f, p, 2], q[f, p, 3] = swap_32(half[f, 2], half[f, 3], lane)
-        turn_first(p)
+    moved = [(up if c < 2 else down).at[c % 2] for c in range(CAP)]
+    shells = [(shell_up if c < 2 else shell_down).at[c % 2] for c in range(CAP)]
+
+    def turn_first(k, z):
+        for f in range(F):
+            v = [jnp.where(kept[c], hold[c, f, z], moved[c][f, z - 2]) for c in range(CAP)]
+            half[k, f, 0], half[k, f, 2] = swap_64(v[0], v[2], lane)
+            half[k, f, 1], half[k, f, 3] = swap_64(v[1], v[3], lane)
+
+    def turn_last(k, z):
+        for f in range(F):
+            q[f, z + 3, 0], q[f, z + 3, 1] = swap_32(half[k, f, 0], half[k, f, 1], lane)
+            q[f, z + 3, 2], q[f, z + 3, 3] = swap_32(half[k, f, 2], half[k, f, 3], lane)
+
+    def turn(i, _):
+        for k in range(4):
+            turn_last(k, 4 * i - 2 + k)
+        for k in range(4):
+            turn_first(k, 4 * i + 2 + k)
         return 0
 
-    turn_first(0)
-    lax.fori_loop(1, B + 5, turn, 0)
-
-    @pl.when(gx == 0)
-    def _():
-        for f in range(F):
-            q[f, 1] = q[f, 3]
-            q[f, 2] = q[f, 3]
-
-    @pl.when(gx == last_x)
-    def _():
-        for f in range(F):
-            q[f, B + 3] = q[f, B + 2]
-            q[f, B + 4] = q[f, B + 2]
+    for k in range(4):
+        turn_first(k, 2 + k)
+    lax.fori_loop(1, 7, turn, 0)
+    for k in range(4):
+        turn_last(k, 26 + k)
+    for f in range(F):
+        for k, z in enumerate((0, 1, 30, 31)):
+            v = [jnp.where(kept[c], hold[c, f, z], shells[c][f, k]) for c in range(CAP)]
+            for j, value in enumerate(turned_to_layers(v, lane)):
+                q[f, z + 3, j] = value
+    for f in range(F):
+        for j in J:
+            for k in range(2):
+                q[f, 1 + k, j] = jnp.where(gx == 0, q[f, 3, j], z_below[f, k, j])
+                q[f, B + 3 + k, j] = jnp.where(gx == last_x, q[f, B + 2, j], z_above[f, k, j])
 
     for block in range(4):
         z0 = 8 * block
@@ -335,17 +351,16 @@
     )
 
 
-def step(owner, spread, x, up, down, z_below, z_above, y_below, y_above):
+def step(owner, spread, *arrays):
     planes = lambda *lead: pltpu.VMEM((*lead, ROWS, LANES), F32)
     rows = pltpu.VMEM((F, B + 16, LANES), F32)
     return pl.pallas_call(
         step_body,
         name="step",
         out_shape=jax.ShapeDtypeStruct((F, B, ROWS, CAP, 1, LANES), F32),
-        in_specs=[SMEM, SMEM, HBM, HBM, HBM, HBM, HBM, VMEM, VMEM],
+        in_specs=[SMEM, SMEM] + [VMEM] * len(arrays),
         out_specs=HBM,
         scratch_shapes=[
-            planes(CAP, F, B + 5),
             planes(F, B + 8, 4),
             planes(CAP, F, B + LEAD),
             rows,
@@ -356,7 +371,7 @@
             planes(F, 4),
             planes(F, 4),
             planes(4),
-            planes(F, 4),
+            planes(4, F, 4),
             planes(F, 4),
             planes(F, 4),
             planes(4),
@@ -367,11 +382,10 @@
             planes(F, 4),
             planes(F, 4),
             pltpu.SemaphoreType.DMA((CAP,)),
-            pltpu.SemaphoreType.DMA((2,)),
-            pltpu.SemaphoreType.DMA((CAP,)),
         ],
-        compiler_params=pltpu.CompilerParams(vmem_limit_bytes=WIDE),
-    )(owner, spread, x, up, down, z_below, z_above, y_below, y_above)
+        compiler_params=pltpu.CompilerParams(vmem_limit_bytes=24 << 20),
+        cost_estimate=pl.CostEstimate(flops=0, bytes_accessed=40000000, transcendentals=0),
+    )(owner, spread, *arrays)
 
 
 def along_curve(block, distance):
@@ -387,15 +401,21 @@
 
 def local(old_state, old_owner, old_slot, diffusivity):
     x = old_state.reshape(8, F, B, ROWS, LANES).transpose(1, 2, 3, 0, 4)[..., None, :]
-    up, down = pack(x)
-    up = along_curve(up, 1)[..., None, :]
-    down = along_curve(down, -1)[..., None, :]
-    z_low, z_high, y_low, y_high = edges(old_owner, x, up, down)
+    shell_up, shell_down = shell(x)
+    up, down = inner(x)
+    shell_up = along_curve(shell_up, 1)
+    up = along_curve(up, 1)
+    shell_down = along_curve(shell_down, -1)
+    down = along_curve(down, -1)
+    hold = held(x)
+    z_low, z_high, y_low, y_high = edges(old_owner, hold, shell_up, shell_down)
+    y_below = along_axis(y_high, "gy", 1)
+    y_above = along_axis(y_low, "gy", -1)
     z_below = along_axis(z_high, "gx", 1)
     z_above = along_axis(z_low, "gx", -1)
-    y_below = along_axis(y_high, "gy", 1)
-    y_above = along_axis(y_low, "gy", -1)
-    out = step(old_owner, diffusivity, x, up, down, z_below, z_above, y_below, y_above)
+    out = step(
+        old_owner, diffusivity, hold, shell_up, shell_down, up, down, z_below, z_above, y_below, y_above
+    )
     return out[..., 0, :].transpose(3, 0, 1, 2, 4).reshape(CAP, F, B * B * B)
 
 

time: 68.9 us -> 65.5 us (0.951)
  the two profiles are of different devices: /device:TPU:111 before, /device:TPU:95 now
where the time goes in v2:
time: 65.5 us; the launch traced here: 65.2 us
  Pallas kernels  27.2 us (42%)
  waiting for transfers between devices  22.5 us (34%)
  starting transfers between devices  13.5 us (21%)
  local copies, waits for them, and re-layouts  1.9 us (3%)
    pallas_call x1, Pallas kernels, step(): pl.pallas_call(step_body, name='step', out_shape=jax.ShapeDtypeStruct((F,...  15.3 us
    ppermute x4, waiting for transfers between devices, along_curve(): lax.ppermute(block, AXES, [(i, (i + distance) % count) for i in range(cou...  14.4 us
    ppermute x4, starting transfers between devices, along_axis(): return lax.ppermute(block, axis, pairs)  9.68 us
    pallas_call x3, Pallas kernels, from_slots(): pl.pallas_call(body, name=name, out_shape=shapes, in_specs=[HBM], out_spe...  9.36 us
    ppermute x4, waiting for transfers between devices, along_axis(): return lax.ppermute(block, axis, pairs)  8.1 us
    ppermute x4, starting transfers between devices, along_curve(): lax.ppermute(block, AXES, [(i, (i + distance) % count) for i in range(cou...  3.79 us
    pallas_call x1, Pallas kernels, edges(): pl.pallas_call(edges_body, name='edges', out_shape=(z_shape, z_shape, y_s...  2.56 us
    unnamed x8, local copies, waits for them, and re-layouts  1.9 us
  transfers between devices with their start and end apart: 8, of which 4 were waited for; matrix products, arithmetic and copies ran while one was open for 0% of the time, Pallas kernels for 13%

profile of v2, /device:TPU:95, one launch (start us, length us, event | category | flops | bytes accessed | tf_op | source)
XLA Modules:
  0.0 65.2 jit_solution(18360062112423968972)
XLA Ops:
  0.0 3.4 %inner.1 = (f32[2,6,28,8,128]{4,3,2,1,0:T(8,128)}, f32[2,6,28,8,128]{4,3,2,1,0:T(8,128)}) custom-call(f32[6,32,8,8,1,128]{5,4,3,2,1,0:T(1,128)} %bitcast.10), custom_call_target="tpu_custom_call" | custom-call | bytes 9000000 | tf_op jit(solution)/shard_map/inner/pallas_call | solution.py:70
  3.4 2.0 %collective-permute-start.2 = (f32[2,6,28,8,128]{4,3,2,1,0:T(8,128)}, f32[2,6,28,8,128]{4,3,2,1,0:T(8,128)S(1)}, u32[]{:S(2)}, u32[]{:S(2)}) collective-permute-start(f32[2,6,28,8,128]{4,3,2,1,0:T(8,128)} %get-tuple-element.15), channel_id=1, source_target_pairs={{0,1},{1,2},{2,3},{3,4},{4,5},{5,6},{6,7},{7,8},{8,9},{9,10},{10,1... | collective-permute-start | bytes 4128776 | tf_op jit(solution)/shard_map/ppermute | solution.py:393
  5.4 0.0 collective-permute-start.3
  5.4 2.4 %shell.1 = (f32[2,6,8,8,128]{4,3,2,1,0:T(8,128)}, f32[2,6,8,8,128]{4,3,2,1,0:T(8,128)}) custom-call(f32[6,32,8,8,1,128]{5,4,3,2,1,0:T(1,128)} %bitcast.11), custom_call_target="tpu_custom_call" | custom-call | bytes 6000000 | tf_op jit(solution)/shard_map/shell/pallas_call | solution.py:70
  7.8 1.8 %collective-permute-start = (f32[2,6,8,8,128]{4,3,2,1,0:T(8,128)}, f32[2,6,8,8,128]{4,3,2,1,0:T(8,128)S(1)}, u32[]{:S(2)}, u32[]{:S(2)}) collective-permute-start(f32[2,6,8,8,128]{4,3,2,1,0:T(8,128)} %get-tuple-element.13), channel_id=1, source_target_pairs={{0,1},{1,2},{2,3},{3,4},{4,5},{5,6},{6,7},{7,8},{8,9},{9,10},{10,1... | collective-permute-start | bytes 1179656 | tf_op jit(solution)/shard_map/ppermute | solution.py:393
  9.6 0.0 collective-permute-start.1
  9.6 3.6 %held.1.hold = f32[4,6,32,8,128]{4,3,2,1,0:T(8,128)} custom-call(f32[6,32,8,8,1,128]{5,4,3,2,1,0:T(1,128)} %bitcast.12), custom_call_target="tpu_custom_call" | custom-call | bytes 12000000 | tf_op jit(solution)/shard_map/held/pallas_call | solution.py:70
  13.2 12.0 %collective-permute-done.up.shell_up = f32[2,6,8,8,128]{4,3,2,1,0:T(8,128)S(1)} collective-permute-done((f32[2,6,8,8,128]{4,3,2,1,0:T(8,128)}, f32[2,6,8,8,128]{4,3,2,1,0:T(8,128)S(1)}, u32[]{:S(2)}, u32[]{:S(2)}) %collective-permute-start) | collective-permute-done | bytes 393248 | tf_op jit(solution)/shard_map/ppermute | solution.py:393
  25.2 2.4 %collective-permute-done.1.down.shell_down = f32[2,6,8,8,128]{4,3,2,1,0:T(8,128)S(1)} collective-permute-done((f32[2,6,8,8,128]{4,3,2,1,0:T(8,128)}, f32[2,6,8,8,128]{4,3,2,1,0:T(8,128)S(1)}, u32[]{:S(2)}, u32[]{:S(2)}) %collective-permute-start.1) | collective-permute-done | bytes 393248 | tf_op jit(solution)/shard_map/ppermute | solution.py:393
  27.6 0.0 copy-done.2
  27.6 1.9 %copy-done = f32[4,6,32,8,128]{4,3,2,1,0:T(8,128)S(1)} copy-done((f32[4,6,32,8,128]{4,3,2,1,0:T(8,128)S(1)}, f32[4,6,32,8,128]{4,3,2,1,0:T(8,128)}, u32[]{:S(2)}) %copy-start) | copy-done | bytes 3145752
  29.5 2.6 %edges.1 = (f32[6,2,4,8,128]{4,3,2,1,0:T(8,128)S(1)}, f32[6,2,4,8,128]{4,3,2,1,0:T(8,128)S(1)}, f32[6,2,32,128]{3,2,1,0:T(8,128)S(1)}, f32[6,2,32,128]{3,2,1,0:T(8,128)S(1)}) custom-call(s32[512]{0:T(512)S(1)} %copy-done.2, f32[4,6,32,8,128]{4,3,2,1,0:T(8,128)S(1)} %copy-done, f32[2,6,8,8,128]{4,3,2,1,0:T(8,128)S(1)} %collective-permute-done.up.shell_up, ...), custom_call_target="tpu_custom_call" | custom-call | bytes 6000000 | tf_op jit(solution)/shard_map/edges/pallas_call | solution.py:148
  32.0 1.3 %collective-permute-start.4 = (f32[6,2,4,8,128]{4,3,2,1,0:T(8,128)S(1)}, f32[6,2,4,8,128]{4,3,2,1,0:T(8,128)S(1)}, u32[]{:S(2)}, u32[]{:S(2)}) collective-permute-start(f32[6,2,4,8,128]{4,3,2,1,0:T(8,128)S(1)} %get-tuple-element.17), channel_id=1, source_target_pairs={{0,32},{32,64},{64,96},{1,33},{33,65},{65,97},{2,34},{34,66},{66,9... | collective-permute-start | bytes 589832 | tf_op jit(solution)/shard_map/ppermute | solution.py:399
  33.3 4.0 %collective-permute-start.5 = (f32[6,2,4,8,128]{4,3,2,1,0:T(8,128)S(1)}, f32[6,2,4,8,128]{4,3,2,1,0:T(8,128)S(1)}, u32[]{:S(2)}, u32[]{:S(2)}) collective-permute-start(f32[6,2,4,8,128]{4,3,2,1,0:T(8,128)S(1)} %get-tuple-element.18), channel_id=1, source_target_pairs={{32,0},{64,32},{96,64},{33,1},{65,33},{97,65},{34,2},{66,34},{98,6... | collective-permute-start | bytes 589832 | tf_op jit(solution)/shard_map/ppermute | solution.py:399
  37.3 2.5 %collective-permute-start.6 = (f32[6,2,32,128]{3,2,1,0:T(8,128)S(1)}, f32[6,2,32,128]{3,2,1,0:T(8,128)S(1)}, u32[]{:S(2)}, u32[]{:S(2)}) collective-permute-start(f32[6,2,32,128]{3,2,1,0:T(8,128)S(1)} %get-tuple-element.19), channel_id=1, source_target_pairs={{0,1},{1,2},{2,3},{3,4},{4,5},{5,6},{6,7},{7,8},{8,9},{9,10},{10,1... | collective-permute-start | bytes 589832 | tf_op jit(solution)/shard_map/ppermute | solution.py:399
  39.8 0.0 collective-permute-done.4.z_below
  39.8 1.9 %collective-permute-start.7 = (f32[6,2,32,128]{3,2,1,0:T(8,128)S(1)}, f32[6,2,32,128]{3,2,1,0:T(8,128)S(1)}, u32[]{:S(2)}, u32[]{:S(2)}) collective-permute-start(f32[6,2,32,128]{3,2,1,0:T(8,128)S(1)} %get-tuple-element.20), channel_id=1, source_target_pairs={{1,0},{2,1},{3,2},{4,3},{5,4},{6,5},{7,6},{8,7},{9,8},{10,9},{11,1... | collective-permute-start | bytes 589832 | tf_op jit(solution)/shard_map/ppermute | solution.py:399
  41.7 0.0 collective-permute-done.5.z_above
  41.7 0.6 collective-permute-done.6.y_below
  42.4 7.5 %collective-permute-done.7.y_above = f32[6,2,32,128]{3,2,1,0:T(8,128)S(1)} collective-permute-done((f32[6,2,32,128]{3,2,1,0:T(8,128)S(1)}, f32[6,2,32,128]{3,2,1,0:T(8,128)S(1)}, u32[]{:S(2)}, u32[]{:S(2)}) %collective-permute-start.7) | collective-permute-done | bytes 196640 | tf_op jit(solution)/shard_map/ppermute | solution.py:399
  49.8 0.0 collective-permute-done.2.up
  49.8 0.0 collective-permute-done.3.down
  49.9 0.0 copy-done.1
  49.9 15.3 %step.1 = f32[6,32,8,4,1,128]{5,4,3,2,1,0:T(1,128)} custom-call(s32[512]{0:T(512)S(1)} %copy-done.2, f32[6]{0:T(128)S(1)} %copy-done.3, f32[4,6,32,8,128]{4,3,2,1,0:T(8,128)S(1)} %copy-done.1, f32[2,6,8,8,128]{4,3,2,1,0:T(8,128)S(1)} %collective-permute-done.up.shell_up, f32[2,6,8,8,128]{4,3,2,1,0:T(8,128)S(1)} %collective-permute-done.1.down.shell_down, ...), custom_call_target="tpu_custom_call" | custom-call | bytes 40000000 | tf_op jit(solution)/shard_map/step/pallas_call | solution.py:357
  (5 shorter events, 0.0 us)
Async XLA Ops:
  3.4 46.4 %collective-permute-start.2 = (f32[2,6,28,8,128]{4,3,2,1,0:T(8,128)}, f32[2,6,28,8,128]{4,3,2,1,0:T(8,128)S(1)}, u32[]{:S(2)}, u32[]{:S(2)}) collective-permute-start(f32[2,6,28,8,128]{4,3,2,1,0:T(8,128)} %get-tuple-element.15), channel_id=1, source_target_pairs={{0,1},{1,2},{2,3},{3,4},{4,5},{5,6},{6,7},{7,8},{8,9},{9,10},{10,1... | collective-permute-start | bytes 4128776 | tf_op jit(solution)/shard_map/ppermute | solution.py:393
  5.4 44.5 %collective-permute-start.3 = (f32[2,6,28,8,128]{4,3,2,1,0:T(8,128)}, f32[2,6,28,8,128]{4,3,2,1,0:T(8,128)S(1)}, u32[]{:S(2)}, u32[]{:S(2)}) collective-permute-start(f32[2,6,28,8,128]{4,3,2,1,0:T(8,128)} %get-tuple-element.16), channel_id=1, source_target_pairs={{0,127},{1,0},{2,1},{3,2},{4,3},{5,4},{6,5},{7,6},{8,7},{9,8},{10,... | collective-permute-start | bytes 4128776 | tf_op jit(solution)/shard_map/ppermute | solution.py:393
  7.8 17.4 %collective-permute-start = (f32[2,6,8,8,128]{4,3,2,1,0:T(8,128)}, f32[2,6,8,8,128]{4,3,2,1,0:T(8,128)S(1)}, u32[]{:S(2)}, u32[]{:S(2)}) collective-permute-start(f32[2,6,8,8,128]{4,3,2,1,0:T(8,128)} %get-tuple-element.13), channel_id=1, source_target_pairs={{0,1},{1,2},{2,3},{3,4},{4,5},{5,6},{6,7},{7,8},{8,9},{9,10},{10,1... | collective-permute-start | bytes 1179656 | tf_op jit(solution)/shard_map/ppermute | solution.py:393
  9.6 18.0 %copy-start.2 = (s32[512]{0:T(512)S(1)}, s32[512]{0:T(512)}, u32[]{:S(2)}) copy-start(s32[512]{0:T(512)} %owner.3) | copy-start | bytes 6148
  9.6 18.0 %collective-permute-start.1 = (f32[2,6,8,8,128]{4,3,2,1,0:T(8,128)}, f32[2,6,8,8,128]{4,3,2,1,0:T(8,128)S(1)}, u32[]{:S(2)}, u32[]{:S(2)}) collective-permute-start(f32[2,6,8,8,128]{4,3,2,1,0:T(8,128)} %get-tuple-element.14), channel_id=1, source_target_pairs={{0,127},{1,0},{2,1},{3,2},{4,3},{5,4},{6,5},{7,6},{8,7},{9,8},{10,... | collective-permute-start | bytes 1179656 | tf_op jit(solution)/shard_map/ppermute | solution.py:393
  9.6 40.3 %copy-start.3 = (f32[6]{0:T(128)S(1)}, f32[6]{0:T(128)}, u32[]{:S(2)}) copy-start(f32[6]{0:T(128)} %spread.1) | copy-start | bytes 76
  27.6 1.9 %copy-start = (f32[4,6,32,8,128]{4,3,2,1,0:T(8,128)S(1)}, f32[4,6,32,8,128]{4,3,2,1,0:T(8,128)}, u32[]{:S(2)}) copy-start(f32[4,6,32,8,128]{4,3,2,1,0:T(8,128)} %held.1.hold) | copy-start | bytes 9437188
  29.4 20.4 %copy-start.1 = (f32[4,6,32,8,128]{4,3,2,1,0:T(8,128)S(1)}, f32[4,6,32,8,128]{4,3,2,1,0:T(8,128)}, u32[]{:S(2)}) copy-start(f32[4,6,32,8,128]{4,3,2,1,0:T(8,128)} %held.1.hold) | copy-start | bytes 9437188
  32.0 7.8 %collective-permute-start.4 = (f32[6,2,4,8,128]{4,3,2,1,0:T(8,128)S(1)}, f32[6,2,4,8,128]{4,3,2,1,0:T(8,128)S(1)}, u32[]{:S(2)}, u32[]{:S(2)}) collective-permute-start(f32[6,2,4,8,128]{4,3,2,1,0:T(8,128)S(1)} %get-tuple-element.17), channel_id=1, source_target_pairs={{0,32},{32,64},{64,96},{1,33},{33,65},{65,97},{2,34},{34,66},{66,9... | collective-permute-start | bytes 589832 | tf_op jit(solution)/shard_map/ppermute | solution.py:399
  33.3 8.4 %collective-permute-start.5 = (f32[6,2,4,8,128]{4,3,2,1,0:T(8,128)S(1)}, f32[6,2,4,8,128]{4,3,2,1,0:T(8,128)S(1)}, u32[]{:S(2)}, u32[]{:S(2)}) collective-permute-start(f32[6,2,4,8,128]{4,3,2,1,0:T(8,128)S(1)} %get-tuple-element.18), channel_id=1, source_target_pairs={{32,0},{64,32},{96,64},{33,1},{65,33},{97,65},{34,2},{66,34},{98,6... | collective-permute-start | bytes 589832 | tf_op jit(solution)/shard_map/ppermute | solution.py:399
  37.3 5.1 %collective-permute-start.6 = (f32[6,2,32,128]{3,2,1,0:T(8,128)S(1)}, f32[6,2,32,128]{3,2,1,0:T(8,128)S(1)}, u32[]{:S(2)}, u32[]{:S(2)}) collective-permute-start(f32[6,2,32,128]{3,2,1,0:T(8,128)S(1)} %get-tuple-element.19), channel_id=1, source_target_pairs={{0,1},{1,2},{2,3},{3,4},{4,5},{5,6},{6,7},{7,8},{8,9},{9,10},{10,1... | collective-permute-start | bytes 589832 | tf_op jit(solution)/shard_map/ppermute | solution.py:399
  39.8 10.0 %collective-permute-start.7 = (f32[6,2,32,128]{3,2,1,0:T(8,128)S(1)}, f32[6,2,32,128]{3,2,1,0:T(8,128)S(1)}, u32[]{:S(2)}, u32[]{:S(2)}) collective-permute-start(f32[6,2,32,128]{3,2,1,0:T(8,128)S(1)} %get-tuple-element.20), channel_id=1, source_target_pairs={{1,0},{2,1},{3,2},{4,3},{5,4},{6,5},{7,6},{8,7},{9,8},{10,9},{11,1... | collective-permute-start | bytes 589832 | tf_op jit(solution)/shard_map/ppermute | solution.py:399

commit v3 on v2

--- a/solution.py
+++ b/solution.py
@@ -25,74 +25,70 @@
         copy.wait()
 
 
-def shell_body(x, up, down, first, last, sem, sem_y):
-    waits, waits_y = [], []
-    for k in range(4):
-        target, slot = (up, 6 + k) if k < 2 else (down, k - 2)
-        shell = target.at[k % 2]
-        waits_y.append(pltpu.make_async_copy(x.at[:, :, 0, slot, 0], first.at[k], sem_y.at[k]))
-        waits_y.append(pltpu.make_async_copy(x.at[:, :, 7, slot, 0], last.at[k], sem_y.at[4 + k]))
-        waits.append(pltpu.make_async_copy(x.at[:, 0:2, :, slot, 0], shell.at[:, 0:2], sem.at[k]))
-        waits.append(
-            pltpu.make_async_copy(x.at[:, 30:32, :, slot, 0], shell.at[:, 2:4], sem.at[4 + k])
-        )
-    for copy in waits_y + waits:
-        copy.start()
-    for copy in waits_y:
-        copy.wait()
-    left = lax.broadcasted_iota(jnp.int32, (8, LANES), 1) < 64
-    for k in range(4):
-        target = up if k < 2 else down
-        for f in range(F):
-            for b in range(4):
-                span = slice(8 * b, 8 * b + 8)
-                target[k % 2, f, 4 + b] = jnp.where(left, first[k, f, span, :], last[k, f, span, :])
-    for copy in waits:
-        copy.wait()
-
-
-def inner_body(x, up, down, sem):
-    copies = []
-    for j in range(2):
-        copies.append(pltpu.make_async_copy(x.at[:, 2:30, :, 6 + j, 0], up.at[j], sem.at[j]))
-        copies.append(pltpu.make_async_copy(x.at[:, 2:30, :, j, 0], down.at[j], sem.at[2 + j]))
-    run_all(copies)
-
-
-def hold_body(x, hold, sem):
+def odd(axis):
+    return lax.axis_index(axis) % 2 == 1
+
+
+def leave_body(near, x, leaving, sem):
+    first = jnp.where(odd("gy"), 0, 6) if near else jnp.where(odd("gy"), 6, 0)
+    run_all(
+        [
+            pltpu.make_async_copy(x.at[:, :, :, first + j, 0], leaving.at[j], sem.at[j])
+            for j in range(2)
+        ]
+    )
+
+
+def leave_far(x, leaving, sem):
+    leave_body(False, x, leaving, sem)
+
+
+def leave_near(x, after, leaving, sem):
+    leave_body(True, x, leaving, sem)
+
+
+def hold_body(x, after, hold, rim, sem):
     run_all(
         [pltpu.make_async_copy(x.at[:, :, :, 2 + c, 0], hold.at[c], sem.at[c]) for c in range(CAP)]
     )
-
-
-def from_slots(body, name, x, shapes, scratch, micros):
+    left = lax.broadcasted_iota(jnp.int32, (8, LANES), 1) < 64
+    for c in range(CAP):
+        for f in range(F):
+            for k, z in enumerate((0, 1, 30, 31)):
+                rim[c, f, k] = hold[c, f, z]
+            for b in range(4):
+                span = slice(8 * b, 8 * b + 8)
+                rim[c, f, 4 + b] = jnp.where(left, hold[c, f, span, 0, :], hold[c, f, span, 7, :])
+
+
+def from_slots(body, name, arrays, shapes, scratch, micros):
     shapes = tuple(jax.ShapeDtypeStruct(shape, F32) for shape in shapes)
     return pl.pallas_call(
         body,
         name=name,
         out_shape=shapes,
-        in_specs=[HBM],
+        in_specs=[HBM] * len(arrays),
         out_specs=(VMEM,) * len(shapes),
         scratch_shapes=scratch,
         compiler_params=pltpu.CompilerParams(vmem_limit_bytes=WIDE),
-        cost_estimate=pl.CostEstimate(flops=0, bytes_accessed=micros * 3000000, transcendentals=0),
-    )(x)
-
-
-def shell(x):
-    rows = pltpu.VMEM((4, F, B, LANES), F32)
-    sems = pltpu.SemaphoreType.DMA((8,))
-    return from_slots(shell_body, "shell", x, [(2, F, 8, ROWS, LANES)] * 2, [rows, rows, sems, sems], 2)
-
-
-def inner(x):
+        cost_estimate=pl.CostEstimate(flops=0, bytes_accessed=1000, transcendentals=0),
+    )(*arrays)
+
+
+def far_boxes(x):
+    sems = pltpu.SemaphoreType.DMA((2,))
+    return from_slots(leave_far, "far", [x], [(2, F, B, ROWS, LANES)], [sems], 2)[0]
+
+
+def near_boxes(x, after):
+    sems = pltpu.SemaphoreType.DMA((2,))
+    return from_slots(leave_near, "near", [x, after], [(2, F, B, ROWS, LANES)], [sems], 2)[0]
+
+
+def held(x, after):
     sems = pltpu.SemaphoreType.DMA((4,))
-    return from_slots(inner_body, "inner", x, [(2, F, 28, ROWS, LANES)] * 2, [sems], 3)
-
-
-def held(x):
-    sems = pltpu.SemaphoreType.DMA((4,))
-    return from_slots(hold_body, "held", x, [(CAP, F, B, ROWS, LANES)], [sems], 4)[0]
+    shapes = [(CAP, F, B, ROWS, LANES), (CAP, F, 8, ROWS, LANES)]
+    return from_slots(hold_body, "held", [x, after], shapes, [sems], 4)
 
 
 def device_number():
@@ -102,6 +98,11 @@
 def kept_flags(owner):
     device = device_number()
     return [owner[device * CAP + c] == device for c in range(CAP)]
+
+
+def arrived(kept, here, c, far, near):
+    from_far = odd("gy") if c >= 2 else jnp.logical_not(odd("gy"))
+    return jnp.where(kept, here, jnp.where(from_far, far, near))
 
 
 def swap_64(a, b, lane):
@@ -122,27 +123,43 @@
     return *swap_32(a, b, lane), *swap_32(c, d, lane)
 
 
-def edges_body(owner, hold, up, down, z_low, z_high, y_low, y_high):
+def edges_body(owner, rim, far, near, z_pair, z_cross, y_near, y_far):
     kept = kept_flags(owner)
-    moved = [(up if c < 2 else down).at[c % 2] for c in range(CAP)]
     lane = lax.broadcasted_iota(jnp.int32, (8, LANES), 1)
+    odd_z, odd_y = odd("gx"), odd("gy")
+
+    def strip(ref, j, f, span):
+        return jnp.where(lane < 64, ref[j, f, span, 0, :], ref[j, f, span, 7, :])
+
     for f in range(F):
+        z_layers = []
         for k, z in enumerate((0, 1, 30, 31)):
-            v = [jnp.where(kept[c], hold[c, f, z], moved[c][f, k]) for c in range(CAP)]
-            target = (z_low if k < 2 else z_high).at[f, k % 2]
-            for j, value in enumerate(turned_to_layers(v, lane)):
-                target[j] = value
+            v = [
+                arrived(kept[c], rim[c, f, k], c, far[c % 2, f, z], near[c % 2, f, z])
+                for c in range(CAP)
+            ]
+            z_layers.append(turned_to_layers(v, lane))
+        for k in range(2):
+            for j in range(4):
+                low, high = z_layers[k][j], z_layers[2 + k][j]
+                z_pair[f, k, j] = jnp.where(odd_z, low, high)
+                z_cross[f, k, j] = jnp.where(odd_z, high, low)
         for b in range(4):
             span = slice(8 * b, 8 * b + 8)
-            rows = []
-            for c in range(CAP):
-                here = jnp.where(lane < 64, hold[c, f, span, 0, :], hold[c, f, span, 7, :])
-                rows.append(jnp.where(kept[c], here, moved[c][f, 4 + b]))
-            for j, value in enumerate(turned_to_layers(rows, lane)):
-                (y_low if j < 2 else y_high)[f, j % 2, span, :] = value
-
-
-def edges(owner, hold, up, down):
+            v = [
+                arrived(
+                    kept[c], rim[c, f, 4 + b], c, strip(far, c % 2, f, span), strip(near, c % 2, f, span)
+                )
+                for c in range(CAP)
+            ]
+            layers = turned_to_layers(v, lane)
+            for k in range(2):
+                low, high = layers[k], layers[2 + k]
+                y_near[f, k, span, :] = jnp.where(odd_y, low, high)
+                y_far[f, k, span, :] = jnp.where(odd_y, high, low)
+
+
+def edges(owner, rim, far, near):
     z_shape = jax.ShapeDtypeStruct((F, 2, 4, ROWS, LANES), F32)
     y_shape = jax.ShapeDtypeStruct((F, 2, B, LANES), F32)
     return pl.pallas_call(
@@ -153,7 +170,7 @@
         out_specs=(VMEM, VMEM, VMEM, VMEM),
         compiler_params=pltpu.CompilerParams(vmem_limit_bytes=16 << 20),
         cost_estimate=pl.CostEstimate(flops=0, bytes_accessed=6000000, transcendentals=0),
-    )(owner, hold, up, down)
+    )(owner, rim, far, near)
 
 
 def minmod(a, b):
@@ -169,7 +186,7 @@
 
 
 def step_body(
-    owner, spread, hold, shell_up, shell_down, up, down, z_below, z_above, y_below, y_above, out,
+    owner, spread, hold, far, near, z_pair, z_cross, y_near, y_far, out,
     q, result, left_d, left_n, right_q, right_m, right_c, carry_p, carry_n, carry_c,
     half, dx, dx_old, cx, cx_old, px, mx, nx, done, turned, sem_out,
 ):
@@ -180,12 +197,14 @@
     sub = lax.broadcasted_iota(jnp.int32, (8, LANES), 0)
     scale = [0.5 * spread[f] for f in range(F)]
 
-    moved = [(up if c < 2 else down).at[c % 2] for c in range(CAP)]
-    shells = [(shell_up if c < 2 else shell_down).at[c % 2] for c in range(CAP)]
+    odd_z, odd_y = odd("gx"), odd("gy")
 
     def turn_first(k, z):
         for f in range(F):
-            v = [jnp.where(kept[c], hold[c, f, z], moved[c][f, z - 2]) for c in range(CAP)]
+            v = [
+                arrived(kept[c], hold[c, f, z], c, far[c % 2, f, z], near[c % 2, f, z])
+                for c in range(CAP)
+            ]
             half[k, f, 0], half[k, f, 2] = swap_64(v[0], v[2], lane)
             half[k, f, 1], half[k, f, 3] = swap_64(v[1], v[3], lane)
 
@@ -196,26 +215,31 @@
 
     def turn(i, _):
         for k in range(4):
-            turn_last(k, 4 * i - 2 + k)
+            turn_last(k, 4 * i - 4 + k)
         for k in range(4):
-            turn_first(k, 4 * i + 2 + k)
+            turn_first(k, 4 * i + k)
         return 0
 
     for k in range(4):
-        turn_first(k, 2 + k)
-    lax.fori_loop(1, 7, turn, 0)
+        turn_first(k, k)
+    lax.fori_loop(1, 8, turn, 0)
     for k in range(4):
-        turn_last(k, 26 + k)
-    for f in range(F):
-        for k, z in enumerate((0, 1, 30, 31)):
-            v = [jnp.where(kept[c], hold[c, f, z], shells[c][f, k]) for c in range(CAP)]
-            for j, value in enumerate(turned_to_layers(v, lane)):
-                q[f, z + 3, j] = value
+        turn_last(k, 28 + k)
     for f in range(F):
         for j in J:
             for k in range(2):
-                q[f, 1 + k, j] = jnp.where(gx == 0, q[f, 3, j], z_below[f, k, j])
-                q[f, B + 3 + k, j] = jnp.where(gx == last_x, q[f, B + 2, j], z_above[f, k, j])
+                q[f, 1 + k, j] = jnp.where(
+                    gx == 0, q[f, 3, j], jnp.where(odd_z, z_pair[f, k, j], z_cross[f, k, j])
+                )
+                q[f, B + 3 + k, j] = jnp.where(
+                    gx == last_x, q[f, B + 2, j], jnp.where(odd_z, z_cross[f, k, j], z_pair[f, k, j])
+                )
+
+    def below(f, k, span):
+        return jnp.where(odd_y, y_near[f, k, span, :], y_far[f, k, span, :])
+
+    def above(f, k, span):
+        return jnp.where(odd_y, y_far[f, k, span, :], y_near[f, k, span, :])
 
     for block in range(4):
         z0 = 8 * block
@@ -226,8 +250,8 @@
             q0 = layer(f, 0, 0)
             first = gy == 0
             return (
-                jnp.where(first, q0, y_below[f, 0, span, :]),
-                jnp.where(first, q0, y_below[f, 1, span, :]),
+                jnp.where(first, q0, below(f, 0, span)),
+                jnp.where(first, q0, below(f, 1, span)),
                 q0,
                 layer(f, 1, 0),
             )
@@ -237,8 +261,8 @@
             end = gy == last_y
             return (
                 q31,
-                jnp.where(end, q31, y_above[f, 0, span, :]),
-                jnp.where(end, q31, y_above[f, 1, span, :]),
+                jnp.where(end, q31, above(f, 0, span)),
+                jnp.where(end, q31, above(f, 1, span)),
             )
 
         _, v1, v0, _ = low(1)
@@ -268,6 +292,15 @@
 
     def x_last(value, ends):
         return jnp.where(lane == 0, ends, pltpu.roll(value, 1, 1))
+
+    def leaving(k):
+        z = 8 * k
+        return [
+            pltpu.make_async_copy(
+                result.at[c, :, pl.ds(z + LEAD, 8)], out.at[:, pl.ds(z, 8), :, c, 0], sem_out.at[k, c]
+            )
+            for c in range(CAP)
+        ]
 
     def plane(i, _):
         for f in range(F):
@@ -340,15 +373,18 @@
             for f in range(F):
                 a = q[f, i + 3, j]
                 dx[f, j] = x_next(a, a) - a
+
+        @pl.when((i >= 12) & (i % 8 == 4))
+        def _():
+            for copy in leaving((i - 12) // 8):
+                copy.start()
+
         return 0
 
     lax.fori_loop(0, B + LEAD, plane, 0)
-    run_all(
-        [
-            pltpu.make_async_copy(result.at[c, :, LEAD:], out.at[:, :, :, c, 0], sem_out.at[c])
-            for c in range(CAP)
-        ]
-    )
+    for k in range(4):
+        for copy in leaving(k):
+            copy.wait()
 
 
 def step(owner, spread, *arrays):
@@ -381,41 +417,37 @@
             planes(F, 4),
             planes(F, 4),
             planes(F, 4),
-            pltpu.SemaphoreType.DMA((CAP,)),
+            pltpu.SemaphoreType.DMA((4, CAP)),
         ],
         compiler_params=pltpu.CompilerParams(vmem_limit_bytes=24 << 20),
         cost_estimate=pl.CostEstimate(flops=0, bytes_accessed=40000000, transcendentals=0),
     )(owner, spread, *arrays)
 
 
-def along_curve(block, distance):
-    count = lax.axis_size(AXES)
-    return lax.ppermute(block, AXES, [(i, (i + distance) % count) for i in range(count)])
-
-
-def along_axis(block, axis, distance):
-    count = lax.axis_size(axis)
-    pairs = [(i, i + distance) for i in range(count) if 0 <= i + distance < count]
-    return lax.ppermute(block, axis, pairs)
+def exchange(block, axes, first, wrap=False):
+    count = lax.axis_size(axes)
+    pairs = []
+    for i in range(first, count, 2):
+        j = (i + 1) % count
+        if i + 1 < count or wrap:
+            pairs += [(i, j), (j, i)]
+    return lax.ppermute(block, axes, pairs)
 
 
 def local(old_state, old_owner, old_slot, diffusivity):
     x = old_state.reshape(8, F, B, ROWS, LANES).transpose(1, 2, 3, 0, 4)[..., None, :]
-    shell_up, shell_down = shell(x)
-    up, down = inner(x)
-    shell_up = along_curve(shell_up, 1)
-    up = along_curve(up, 1)
-    shell_down = along_curve(shell_down, -1)
-    down = along_curve(down, -1)
-    hold = held(x)
-    z_low, z_high, y_low, y_high = edges(old_owner, hold, shell_up, shell_down)
-    y_below = along_axis(y_high, "gy", 1)
-    y_above = along_axis(y_low, "gy", -1)
-    z_below = along_axis(z_high, "gx", 1)
-    z_above = along_axis(z_low, "gx", -1)
-    out = step(
-        old_owner, diffusivity, hold, shell_up, shell_down, up, down, z_below, z_above, y_below, y_above
-    )
+    far = far_boxes(x)
+    near = near_boxes(x, far)
+    near_sent = near
+    far = exchange(far, AXES, 1, wrap=True)
+    near = exchange(near, AXES, 0)
+    hold, rim = held(x, near_sent)
+    z_pair, z_cross, y_near, y_far = edges(old_owner, rim, far, near)
+    y_far = exchange(y_far, "gy", 1)
+    z_pair = exchange(z_pair, "gx", 0)
+    z_cross = exchange(z_cross, "gx", 1)
+    y_near = exchange(y_near, "gy", 0)
+    out = step(old_owner, diffusivity, hold, far, near, z_pair, z_cross, y_near, y_far)
     return out[..., 0, :].transpose(3, 0, 1, 2, 4).reshape(CAP, F, B * B * B)
 
 

time: 65.5 us -> 62 us (0.947)
  the two profiles are of different devices: /device:TPU:95 before, /device:TPU:5 now
where the time goes in v3:
time: 62 us; the launch traced here: 61.8 us
  Pallas kernels  27.1 us (44%)
  waiting for transfers between devices  19.3 us (31%)
  starting transfers between devices  14.2 us (23%)
  local copies, waits for them, and re-layouts  1.15 us (2%)
    ppermute x6, waiting for transfers between devices, exchange(): return lax.ppermute(block, axes, pairs)  19.3 us
    pallas_call x1, Pallas kernels, step(): pl.pallas_call(step_body, name='step', out_shape=jax.ShapeDtypeStruct((F,...  15 us
    ppermute x6, starting transfers between devices, exchange(): return lax.ppermute(block, axes, pairs)  14.2 us
    pallas_call x3, Pallas kernels, from_slots(): pl.pallas_call(body, name=name, out_shape=shapes, in_specs=[HBM] * len(ar...  9.44 us
    pallas_call x1, Pallas kernels, edges(): pl.pallas_call(edges_body, name='edges', out_shape=(z_shape, z_shape, y_s...  2.6 us
  transfers between devices with their start and end apart: 6, of which 2 were waited for; matrix products, arithmetic and copies ran while one was open for 0% of the time, Pallas kernels for 7%

profile of v3, /device:TPU:5, one launch (start us, length us, event | category | flops | bytes accessed | tf_op | source)
XLA Modules:
  0.0 61.8 jit_solution(6290526890251854217)
XLA Ops:
  0.0 2.5 %far.1.after = f32[2,6,32,8,128]{4,3,2,1,0:T(8,128)} custom-call(f32[6,32,8,8,1,128]{5,4,3,2,1,0:T(1,128)} %bitcast.10), custom_call_target="tpu_custom_call" | custom-call | bytes 1000 | tf_op jit(solution)/shard_map/far/pallas_call | solution.py:66
  2.5 0.0 copy-start.4
  2.5 2.7 %near.1.after = f32[2,6,32,8,128]{4,3,2,1,0:T(8,128)} custom-call(f32[6,32,8,8,1,128]{5,4,3,2,1,0:T(1,128)} %bitcast.11, f32[2,6,32,8,128]{4,3,2,1,0:T(8,128)} %far.1.after), custom_call_target="tpu_custom_call" | custom-call | bytes 1000 | tf_op jit(solution)/shard_map/near/pallas_call | solution.py:66
  5.2 0.0 copy-start.2
  5.3 0.8 %collective-permute-start.1 = (f32[2,6,32,8,128]{4,3,2,1,0:T(8,128)}, f32[2,6,32,8,128]{4,3,2,1,0:T(8,128)S(1)}, u32[]{:S(2)}, u32[]{:S(2)}) collective-permute-start(f32[2,6,32,8,128]{4,3,2,1,0:T(8,128)} %near.1.after), channel_id=1, source_target_pairs={{0,1},{1,0},{2,3},{3,2},{4,5},{5,4},{6,7},{7,6},{8,9},{9,8},{10,11... | collective-permute-start | bytes 4718600 | tf_op jit(solution)/shard_map/ppermute | solution.py:434
  6.0 0.0 copy-done.4
  6.0 1.6 %collective-permute-start = (f32[2,6,32,8,128]{4,3,2,1,0:T(8,128)S(1)}, f32[2,6,32,8,128]{4,3,2,1,0:T(8,128)S(1)}, u32[]{:S(2)}, u32[]{:S(2)}) collective-permute-start(f32[2,6,32,8,128]{4,3,2,1,0:T(8,128)S(1)} %copy-done.4), channel_id=1, source_target_pairs={{1,2},{2,1},{3,4},{4,3},{5,6},{6,5},{7,8},{8,7},{9,10},{10,9},{11,... | collective-permute-start | bytes 4718600 | tf_op jit(solution)/shard_map/ppermute | solution.py:434
  7.7 4.2 %held.1 = (f32[4,6,32,8,128]{4,3,2,1,0:T(8,128)}, f32[4,6,8,8,128]{4,3,2,1,0:T(8,128)}) custom-call(f32[6,32,8,8,1,128]{5,4,3,2,1,0:T(1,128)} %bitcast.12, f32[2,6,32,8,128]{4,3,2,1,0:T(8,128)} %near.1.after), custom_call_target="tpu_custom_call" | custom-call | bytes 1000 | tf_op jit(solution)/shard_map/held/pallas_call | solution.py:66
  11.9 0.0 collective-permute-done.1.near
  11.9 14.3 %collective-permute-done.far = f32[2,6,32,8,128]{4,3,2,1,0:T(8,128)S(1)} collective-permute-done((f32[2,6,32,8,128]{4,3,2,1,0:T(8,128)S(1)}, f32[2,6,32,8,128]{4,3,2,1,0:T(8,128)S(1)}, u32[]{:S(2)}, u32[]{:S(2)}) %collective-permute-start) | collective-permute-done | bytes 1572896 | tf_op jit(solution)/shard_map/ppermute | solution.py:434
  26.2 0.0 copy-done.2
  26.2 1.1 %copy-done.1 = f32[4,6,8,8,128]{4,3,2,1,0:T(8,128)S(1)} copy-done((f32[4,6,8,8,128]{4,3,2,1,0:T(8,128)S(1)}, f32[4,6,8,8,128]{4,3,2,1,0:T(8,128)}, u32[]{:S(2)}) %copy-start.1) | copy-done | bytes 786456
  27.3 2.6 %edges.1 = (f32[6,2,4,8,128]{4,3,2,1,0:T(8,128)S(1)}, f32[6,2,4,8,128]{4,3,2,1,0:T(8,128)S(1)}, f32[6,2,32,128]{3,2,1,0:T(8,128)S(1)}, f32[6,2,32,128]{3,2,1,0:T(8,128)S(1)}) custom-call(s32[512]{0:T(512)S(1)} %copy-done.2, f32[4,6,8,8,128]{4,3,2,1,0:T(8,128)S(1)} %copy-done.1, f32[2,6,32,8,128]{4,3,2,1,0:T(8,128)S(1)} %collective-permute-done.far, ...), custom_call_target="tpu_custom_call" | custom-call | bytes 6000000 | tf_op jit(solution)/shard_map/edges/pallas_call | solution.py:165
  29.9 1.0 %collective-permute-start.2 = (f32[6,2,4,8,128]{4,3,2,1,0:T(8,128)S(1)}, f32[6,2,4,8,128]{4,3,2,1,0:T(8,128)S(1)}, u32[]{:S(2)}, u32[]{:S(2)}) collective-permute-start(f32[6,2,4,8,128]{4,3,2,1,0:T(8,128)S(1)} %get-tuple-element.13), channel_id=1, source_target_pairs={{0,32},{32,0},{64,96},{96,64},{1,33},{33,1},{65,97},{97,65},{2,34}... | collective-permute-start | bytes 589832 | tf_op jit(solution)/shard_map/ppermute | solution.py:434
  30.9 1.9 %collective-permute-start.3 = (f32[6,2,4,8,128]{4,3,2,1,0:T(8,128)S(1)}, f32[6,2,4,8,128]{4,3,2,1,0:T(8,128)S(1)}, u32[]{:S(2)}, u32[]{:S(2)}) collective-permute-start(f32[6,2,4,8,128]{4,3,2,1,0:T(8,128)S(1)} %get-tuple-element.14), channel_id=1, source_target_pairs={{32,64},{64,32},{33,65},{65,33},{34,66},{66,34},{35,67},{67,35},{3... | collective-permute-start | bytes 589832 | tf_op jit(solution)/shard_map/ppermute | solution.py:434
  32.8 7.0 %collective-permute-start.4 = (f32[6,2,32,128]{3,2,1,0:T(8,128)S(1)}, f32[6,2,32,128]{3,2,1,0:T(8,128)S(1)}, u32[]{:S(2)}, u32[]{:S(2)}) collective-permute-start(f32[6,2,32,128]{3,2,1,0:T(8,128)S(1)} %get-tuple-element.15), channel_id=1, source_target_pairs={{0,1},{1,0},{2,3},{3,2},{4,5},{5,4},{6,7},{7,6},{8,9},{9,8},{10,11... | collective-permute-start | bytes 589832 | tf_op jit(solution)/shard_map/ppermute | solution.py:434
  39.8 1.9 %collective-permute-start.5 = (f32[6,2,32,128]{3,2,1,0:T(8,128)S(1)}, f32[6,2,32,128]{3,2,1,0:T(8,128)S(1)}, u32[]{:S(2)}, u32[]{:S(2)}) collective-permute-start(f32[6,2,32,128]{3,2,1,0:T(8,128)S(1)} %get-tuple-element.16), channel_id=1, source_target_pairs={{1,2},{2,1},{3,4},{4,3},{5,6},{6,5},{7,8},{8,7},{9,10},{10,9},{11,... | collective-permute-start | bytes 589832 | tf_op jit(solution)/shard_map/ppermute | solution.py:434
  41.7 0.0 collective-permute-done.2.z_pair
  41.7 0.0 collective-permute-done.3.z_cross
  41.7 0.0 collective-permute-done.4.y_near
  41.8 5.0 %collective-permute-done.5.y_far = f32[6,2,32,128]{3,2,1,0:T(8,128)S(1)} collective-permute-done((f32[6,2,32,128]{3,2,1,0:T(8,128)S(1)}, f32[6,2,32,128]{3,2,1,0:T(8,128)S(1)}, u32[]{:S(2)}, u32[]{:S(2)}) %collective-permute-start.5) | collective-permute-done | bytes 196640 | tf_op jit(solution)/shard_map/ppermute | solution.py:434
  46.8 0.0 copy-done
  46.8 0.0 copy-done.3
  46.8 15.0 %step.1 = f32[6,32,8,4,1,128]{5,4,3,2,1,0:T(1,128)} custom-call(s32[512]{0:T(512)S(1)} %copy-done.2, f32[6]{0:T(128)S(1)} %copy-done.3, f32[4,6,32,8,128]{4,3,2,1,0:T(8,128)S(1)} %copy-done, f32[2,6,32,8,128]{4,3,2,1,0:T(8,128)S(1)} %collective-permute-done.far, f32[2,6,32,8,128]{4,3,2,1,0:T(8,128)S(1)} %collective-permute-done.1.near, ...), custom_call_target="tpu_custom_call" | custom-call | bytes 40000000 | tf_op jit(solution)/shard_map/step/pallas_call | solution.py:393
  (3 shorter events, 0.0 us)
Async XLA Ops:
  2.5 3.5 %copy-start.4 = (f32[2,6,32,8,128]{4,3,2,1,0:T(8,128)S(1)}, f32[2,6,32,8,128]{4,3,2,1,0:T(8,128)}, u32[]{:S(2)}) copy-start(f32[2,6,32,8,128]{4,3,2,1,0:T(8,128)} %far.1.after) | copy-start | bytes 4718596
  5.2 20.9 %copy-start.2 = (s32[512]{0:T(512)S(1)}, s32[512]{0:T(512)}, u32[]{:S(2)}) copy-start(s32[512]{0:T(512)} %owner.3) | copy-start | bytes 6148
  5.3 6.7 %collective-permute-start.1 = (f32[2,6,32,8,128]{4,3,2,1,0:T(8,128)}, f32[2,6,32,8,128]{4,3,2,1,0:T(8,128)S(1)}, u32[]{:S(2)}, u32[]{:S(2)}) collective-permute-start(f32[2,6,32,8,128]{4,3,2,1,0:T(8,128)} %near.1.after), channel_id=1, source_target_pairs={{0,1},{1,0},{2,3},{3,2},{4,5},{5,4},{6,7},{7,6},{8,9},{9,8},{10,11... | collective-permute-start | bytes 4718600 | tf_op jit(solution)/shard_map/ppermute | solution.py:434
  6.0 20.1 %collective-permute-start = (f32[2,6,32,8,128]{4,3,2,1,0:T(8,128)S(1)}, f32[2,6,32,8,128]{4,3,2,1,0:T(8,128)S(1)}, u32[]{:S(2)}, u32[]{:S(2)}) collective-permute-start(f32[2,6,32,8,128]{4,3,2,1,0:T(8,128)S(1)} %copy-done.4), channel_id=1, source_target_pairs={{1,2},{2,1},{3,4},{4,3},{5,6},{6,5},{7,8},{8,7},{9,10},{10,9},{11,... | collective-permute-start | bytes 4718600 | tf_op jit(solution)/shard_map/ppermute | solution.py:434
  26.2 1.1 %copy-start.1 = (f32[4,6,8,8,128]{4,3,2,1,0:T(8,128)S(1)}, f32[4,6,8,8,128]{4,3,2,1,0:T(8,128)}, u32[]{:S(2)}) copy-start(f32[4,6,8,8,128]{4,3,2,1,0:T(8,128)} %get-tuple-element.12.rim) | copy-start | bytes 2359300
  27.3 19.5 %copy-start = (f32[4,6,32,8,128]{4,3,2,1,0:T(8,128)S(1)}, f32[4,6,32,8,128]{4,3,2,1,0:T(8,128)}, u32[]{:S(2)}) copy-start(f32[4,6,32,8,128]{4,3,2,1,0:T(8,128)} %get-tuple-element.11.hold) | copy-start | bytes 9437188
  27.3 19.5 %copy-start.3 = (f32[6]{0:T(128)S(1)}, f32[6]{0:T(128)}, u32[]{:S(2)}) copy-start(f32[6]{0:T(128)} %spread.1) | copy-start | bytes 76
  29.9 11.8 %collective-permute-start.2 = (f32[6,2,4,8,128]{4,3,2,1,0:T(8,128)S(1)}, f32[6,2,4,8,128]{4,3,2,1,0:T(8,128)S(1)}, u32[]{:S(2)}, u32[]{:S(2)}) collective-permute-start(f32[6,2,4,8,128]{4,3,2,1,0:T(8,128)S(1)} %get-tuple-element.13), channel_id=1, source_target_pairs={{0,32},{32,0},{64,96},{96,64},{1,33},{33,1},{65,97},{97,65},{2,34}... | collective-permute-start | bytes 589832 | tf_op jit(solution)/shard_map/ppermute | solution.py:434
  30.9 10.8 %collective-permute-start.3 = (f32[6,2,4,8,128]{4,3,2,1,0:T(8,128)S(1)}, f32[6,2,4,8,128]{4,3,2,1,0:T(8,128)S(1)}, u32[]{:S(2)}, u32[]{:S(2)}) collective-permute-start(f32[6,2,4,8,128]{4,3,2,1,0:T(8,128)S(1)} %get-tuple-element.14), channel_id=1, source_target_pairs={{32,64},{64,32},{33,65},{65,33},{34,66},{66,34},{35,67},{67,35},{3... | collective-permute-start | bytes 589832 | tf_op jit(solution)/shard_map/ppermute | solution.py:434
  32.8 8.9 %collective-permute-start.4 = (f32[6,2,32,128]{3,2,1,0:T(8,128)S(1)}, f32[6,2,32,128]{3,2,1,0:T(8,128)S(1)}, u32[]{:S(2)}, u32[]{:S(2)}) collective-permute-start(f32[6,2,32,128]{3,2,1,0:T(8,128)S(1)} %get-tuple-element.15), channel_id=1, source_target_pairs={{0,1},{1,0},{2,3},{3,2},{4,5},{5,4},{6,7},{7,6},{8,9},{9,8},{10,11... | collective-permute-start | bytes 589832 | tf_op jit(solution)/shard_map/ppermute | solution.py:434
  39.8 7.0 %collective-permute-start.5 = (f32[6,2,32,128]{3,2,1,0:T(8,128)S(1)}, f32[6,2,32,128]{3,2,1,0:T(8,128)S(1)}, u32[]{:S(2)}, u32[]{:S(2)}) collective-permute-start(f32[6,2,32,128]{3,2,1,0:T(8,128)S(1)} %get-tuple-element.16), channel_id=1, source_target_pairs={{1,2},{2,1},{3,4},{4,3},{5,6},{6,5},{7,8},{8,7},{9,10},{10,9},{11,... | collective-permute-start | bytes 589832 | tf_op jit(solution)/shard_map/ppermute | solution.py:434

commit v4 on v3

v4 whole, which is shorter than its diff:
```python
import functools

import jax
import jax.numpy as jnp
from jax import lax
from jax.experimental import pallas as pl
from jax.experimental.pallas import tpu as pltpu
from jax.sharding import PartitionSpec as P

B = 32
F = 6
CAP = 4
PARTS = 4
HALF = 16
ROWS = 8
LANES = 128
AXES = ("gx", "gy")
F32 = jnp.float32
HBM = pl.BlockSpec(memory_space=pl.ANY)
VMEM = pl.BlockSpec(memory_space=pltpu.VMEM)
SMEM = pl.BlockSpec(memory_space=pltpu.SMEM)
WIDE = 56 << 20


def run_all(copies):
    for copy in copies:
        copy.start()
    for copy in copies:
        copy.wait()


def odd(axis):
    return lax.axis_index(axis) % 2 == 1


def leaving_copies(x, near, target, planes, sem):
    first = jnp.where(odd("gy"), 0, 6) if near else jnp.where(odd("gy"), 6, 0)
    return [
        pltpu.make_async_copy(x.at[:, planes, :, first + j, 0], target.at[j], sem.at[j])
        for j in range(2)
    ]


def far_body(x, low, high, sem):
    run_all(
        leaving_copies(x, False, low, slice(0, HALF), sem.at[0])
        + leaving_copies(x, False, high, slice(HALF, B), sem.at[1])
    )


def near_body(x, after, *rest):
    nears, (hold_low, hold_high, sem) = rest[:PARTS], rest[PARTS:]
    copies = []
    for k, near in enumerate(nears):
        copies += leaving_copies(x, True, near, slice(8 * k, 8 * k + 8), sem.at[2 + k])
    for k, hold in enumerate((hold_low, hold_high)):
        for c in range(CAP):
            planes = slice(HALF * k, HALF * k + HALF)
            copies.append(
                pltpu.make_async_copy(
                    x.at[:, planes, :, 2 + c, 0], hold.at[c], sem.at[k, c]
                )
            )
    run_all(copies)


def from_slots(body, name, arrays, shapes, sems):
    shapes = tuple(jax.ShapeDtypeStruct(shape, F32) for shape in shapes)
    return pl.pallas_call(
        body,
        name=name,
        out_shape=shapes,
        in_specs=[HBM] * len(arrays),
        out_specs=(VMEM,) * len(shapes),
        scratch_shapes=[pltpu.SemaphoreType.DMA(sems)],
        compiler_params=pltpu.CompilerParams(vmem_limit_bytes=WIDE),
        cost_estimate=pl.CostEstimate(flops=0, bytes_accessed=1000, transcendentals=0),
    )(*arrays)


def far_boxes(x):
    return from_slots(far_body, "far", [x], [(2, F, HALF, ROWS, LANES)] * 2, (2, 2))


def near_boxes(x, after):
    half = (CAP, F, HALF, ROWS, LANES)
    part = (2, F, B // PARTS, ROWS, LANES)
    return from_slots(
        near_body, "near", [x, after], [part] * PARTS + [half, half], (2 + PARTS, CAP)
    )


def device_number():
    return lax.axis_index("gx") * lax.axis_size("gy") + lax.axis_index("gy")


def kept_flags(owner):
    device = device_number()
    return [owner[device * CAP + c] == device for c in range(CAP)]


def arrived(kept, here, c, far, near):
    from_far = odd("gy") if c >= 2 else jnp.logical_not(odd("gy"))
    return jnp.where(kept, here, jnp.where(from_far, far, near))


def swap_64(a, b, lane):
    low = lane < 64
    m = pltpu.roll(jnp.where(low, b, a), 64, 1)
    return jnp.where(low, a, m), jnp.where(low, m, b)


def swap_32(a, b, lane):
    even = (lane & 32) == 0
    m = jnp.where(even, b, a)
    return jnp.where(even, a, pltpu.roll(m, 32, 1)), jnp.where(even, pltpu.roll(m, 96, 1), b)


def turned_to_layers(v, lane):
    a, c = swap_64(v[0], v[2], lane)
    b, d = swap_64(v[1], v[3], lane)
    return *swap_32(a, b, lane), *swap_32(c, d, lane)


def turn_half(kept, hold, nears, far, target, index):
    lane = lax.broadcasted_iota(jnp.int32, (8, LANES), 1)
    for near, z0 in ((nears[0], 0), (nears[1], 8)):

        def group(g, _):
            for z in (2 * g, 2 * g + 1):
                for f in range(F):
                    v = [
                        arrived(
                            kept[c], hold[c, f, z0 + z], c, far[c % 2, f, z0 + z], near[c % 2, f, z]
                        )
                        for c in range(CAP)
                    ]
                    for j, value in enumerate(turned_to_layers(v, lane)):
                        target[f, index + z0 + z, j] = value
            return 0

        lax.fori_loop(0, 4, group, 0)


def turn_low_body(owner, hold, near_0, near_1, far, q):
    turn_half(kept_flags(owner), hold, (near_0, near_1), far, q, 3)
    for f in range(F):
        q[f, 0] = q[f, 3]
        q[f, 1] = q[f, 3]
        q[f, 2] = q[f, 3]


def turn_high_body(
    owner, hold, near_0, near_1, far, q_low, after, q, z_own, y_own, z_pair, z_cross, y_near, y_far
):
    turn_half(kept_flags(owner), hold, (near_0, near_1), far, q, 5)
    odd_z, odd_y = odd("gx"), odd("gy")
    for f in range(F):
        for k in range(5):
            q[f, k] = q_low[f, k + 14]
        q[f, 21] = q[f, 20]
        q[f, 22] = q[f, 20]
        ends = [q_low[f, 3], q_low[f, 4], q[f, 19], q[f, 20]]
        for k in range(4):
            z_own[f, k] = ends[k]
        for k in range(2):
            z_pair[f, k] = jnp.where(odd_z, ends[k], ends[2 + k])
            z_cross[f, k] = jnp.where(odd_z, ends[2 + k], ends[k])
        for b in range(4):
            span = slice(8 * b, 8 * b + 8)
            source, z = (q_low, 8 * b + 3) if b < 2 else (q, 8 * b - 11)
            ends = [source[f, z : z + 8, j, 0 if j < 2 else 7, :] for j in range(4)]
            for k in range(4):
                y_own[f, k, span, :] = ends[k]
            for k in range(2):
                y_near[f, k, span, :] = jnp.where(odd_y, ends[k], ends[2 + k])
                y_far[f, k, span, :] = jnp.where(odd_y, ends[2 + k], ends[k])


def turn(body, name, planes, owner, arrays, others, after=()):
    shapes = [(F, planes, 4, ROWS, LANES)] + others
    return pl.pallas_call(
        body,
        name=name,
        out_shape=tuple(jax.ShapeDtypeStruct(shape, F32) for shape in shapes),
        in_specs=[SMEM] + [VMEM] * len(arrays) + [HBM] * len(after),
        out_specs=(VMEM,) * len(shapes),
        compiler_params=pltpu.CompilerParams(vmem_limit_bytes=24 << 20),
        cost_estimate=pl.CostEstimate(flops=0, bytes_accessed=6000000, transcendentals=0),
    )(owner, *arrays, *after)


def turn_low(owner, *arrays):
    return turn(turn_low_body, "turn_low", LOW + 10, owner, arrays, [])[0]


def turn_high(owner, after, *arrays):
    z_own, y_own = (F, 4, 4, ROWS, LANES), (F, 4, B, LANES)
    z_half, y_half = (F, 2, 4, ROWS, LANES), (F, 2, B, LANES)
    others = [z_own, y_own, z_half, z_half, y_half, y_half]
    return turn(turn_high_body, "turn_high", B - LOW + 10, owner, arrays, others, (after,))


def minmod(a, b):
    return jnp.maximum(jnp.minimum(a, b), jnp.minimum(jnp.maximum(a, b), 0.0))


def conduction(v):
    return jnp.exp(0.5 * jnp.tanh(v))


LEAD = 5
J = range(4)
LOW = 14


def step_body(
    first, count, chunk, spread, q, *rest,
):
    (
        out, result, carry_p, carry_n, carry_c, dx, dx_old, cx, cx_old, px, mx, nx, done, turned, sem_out,
    ) = rest[-15:]
    lane = lax.broadcasted_iota(jnp.int32, (8, LANES), 1)
    sub = lax.broadcasted_iota(jnp.int32, (8, LANES), 0)
    scale = [0.5 * spread[f] for f in range(F)]

    def y_next(value, end):
        return jnp.where(sub == 7, end, pltpu.roll(value, 7, 0))

    def y_last(value, end):
        return jnp.where(sub == 0, end, pltpu.roll(value, 1, 0))

    def leaving(k):
        z = chunk * k
        return [
            pltpu.make_async_copy(
                result.at[c, :, pl.ds(z + LEAD, chunk)],
                out.at[:, pl.ds(first + z, chunk), :, c, 0],
                sem_out.at[k, c],
            )
            for c in range(CAP)
        ]

    def plane(i, _):
        for f in range(F):
            for j in (0, 2):
                result[j, f, i], result[j + 1, f, i] = swap_32(turned[f, j], turned[f, j + 1], lane)
        for f in range(F):
            for j in (0, 1):
                turned[f, j], turned[f, j + 2] = swap_64(done[f, j], done[f, j + 2], lane)

        here = [carry_c[j] for j in J]
        above = [conduction(q[5, i + 1, j]) for j in J]
        cond_z = [a + b for a, b in zip(here, above)]
        for j in J:
            carry_c[j] = above[j]
        beyond = here[1:] + [y_next(here[0], here[3])]
        cond_y = [a + b for a, b in zip(here, beyond)]
        v = [q[1, i, j] for j in J]
        beyond = v[1:] + [y_next(v[0], v[3])]
        weight_y = [0.0625 * (a + b) for a, b in zip(v, beyond)]
        weight_z = [0.0625 * (q[2, i, j] + q[2, i + 1, j]) for j in J]
        edge_y = -0.125 * v[0]
        edge_x = [-0.125 * q[0, i, j] for j in J]
        for f in range(F):
            value = [q[f, i, j] for j in J]
            twice = [a + a for a in value]
            total = []
            for j in J:
                after = q[f, i + 1, j]
                d = after - value[j]
                slope = minmod(d, q[f, i + 2, j] - after)
                double = after + after
                state = jnp.where(weight_z[j] > 0.0, carry_p[f, j], double - slope)
                carry_p[f, j] = double + slope
                net = (scale[f] * cond_z[j]) * d - weight_z[j] * state
                total.append(value[j] + (net - carry_n[f, j]))
                carry_n[f, j] = net
            beyond = value[1:] + [y_next(value[0], value[3])]
            d = [b - a for a, b in zip(value, beyond)]
            before = [y_last(d[3], 0.0)] + d[:3]
            slope = [minmod(a, b) for a, b in zip(before, d)]
            right = [a - b for a, b in zip(twice, slope)]
            right = right[1:] + [y_next(right[0], twice[3])]
            net = []
            for j in J:
                state = jnp.where(weight_y[j] > 0.0, twice[j] + slope[j], right[j])
                net.append((scale[f] * cond_y[j]) * d[j] - weight_y[j] * state)
            before = [y_last(net[3], edge_y * twice[0])] + net[:3]
            for j in J:
                n = nx[f, j]
                t = total[j] + (net[j] - before[j])
                before_x = jnp.where(lane == 0, edge_x[j] * twice[j], pltpu.roll(n, 1, 1))
                done[f, j] = t + (n - before_x)
        for j in J:
            u = q[0, i + 1, j]
            weight = 0.0625 * ((u + u) + dx_old[0, j])
            from_left = (weight > 0.0) | (lane == 127)
            cond = cx_old[j]
            for f in range(F):
                state = jnp.where(from_left, px[f, j], pltpu.roll(mx[f, j], 127, 1))
                nx[f, j] = (scale[f] * cond) * dx_old[f, j] - weight * state
        for j in J:
            cx_old[j] = cx[j]
            for f in range(F):
                a, d = q[f, i + 2, j], dx[f, j]
                slope = minmod(pltpu.roll(d, 1, 1), d)
                px[f, j], mx[f, j] = (a + a) + slope, (a + a) - slope
                dx_old[f, j] = d
        for j in J:
            c = conduction(q[5, i + 3, j])
            cx[j] = c + jnp.where(lane == 127, c, pltpu.roll(c, 127, 1))
            for f in range(F):
                a = q[f, i + 3, j]
                dx[f, j] = jnp.where(lane == 127, 0.0, pltpu.roll(a, 127, 1) - a)

        @pl.when((i >= chunk + 4) & ((i - 4) % chunk == 0))
        def _():
            for copy in leaving((i - 4) // chunk - 1):
                copy.start()

        return 0

    lax.fori_loop(0, count + LEAD, plane, 0)
    for k in range(count // chunk):
        for copy in leaving(k):
            copy.wait()


def step(first, count, chunk, spread, q, out=None):
    planes = lambda *lead: pltpu.VMEM((*lead, ROWS, LANES), F32)
    return pl.pallas_call(
        functools.partial(step_body, first, count, chunk),
        name="step",
        out_shape=jax.ShapeDtypeStruct((F, B, ROWS, CAP, 1, LANES), F32),
        in_specs=[SMEM, VMEM] + ([] if out is None else [HBM]),
        out_specs=HBM,
        input_output_aliases={} if out is None else {2: 0},
        scratch_shapes=[
            planes(CAP, F, count + LEAD),
            planes(F, 4),
            planes(F, 4),
            planes(4),
            planes(F, 4),
            planes(F, 4),
            planes(4),
            planes(4),
            planes(F, 4),
            planes(F, 4),
            planes(F, 4),
            planes(F, 4),
            planes(F, 4),
            pltpu.SemaphoreType.DMA((count // chunk, CAP)),
        ],
        compiler_params=pltpu.CompilerParams(vmem_limit_bytes=24 << 20),
        cost_estimate=pl.CostEstimate(flops=0, bytes_accessed=20000000, transcendentals=0),
    )(spread, q, *(() if out is None else (out,)))


def change(far, out_1, in_0, in_1, u_out, u_0, u_1, c_out, c_0, scale):
    d = in_0 - out_1
    slope = minmod(d, in_1 - in_0)
    inner = -jnp.maximum(0.0625 * (u_0 + u_1), 0.0) * slope
    weight = 0.0625 * (u_out + u_0)
    left = (out_1 + out_1) + minmod(out_1 - far, d)
    right = (in_0 + in_0) - slope
    net = (scale * (c_out + c_0)) * d - weight * jnp.where(weight > 0.0, left, right)
    outer = net + (0.125 * u_0) * (in_0 + in_0)
    return inner - outer, -inner


def both_ends(below, own, above, velocity, has_below, has_above, scale):
    u = [below(velocity, 1)] + [own(velocity, k) for k in range(4)] + [above(velocity, 0)]
    c = [conduction(v) for v in (below(5, 1), own(5, 0), own(5, 3), above(5, 0))]
    result = []
    for f in range(F):
        layers = [own(f, k) for k in range(4)]
        a, b = change(
            below(f, 0), below(f, 1), layers[0], layers[1], u[0], u[1], u[2], c[0], c[1], scale[f]
        )
        e, d = change(
            above(f, 1), above(f, 0), layers[3], layers[2], -u[5], -u[4], -u[3], c[3], c[2], scale[f]
        )
        a, b = jnp.where(has_below, a, 0.0), jnp.where(has_below, b, 0.0)
        d, e = jnp.where(has_above, d, 0.0), jnp.where(has_above, e, 0.0)
        result.append([a, b, d, e])
    return result


def ends_body(
    spread, z_own, y_own, z_pair, z_cross, y_near, y_far, before, out,
    z_add, y_add, planes, first, last, sem, sem_in, sem_out,
):
    gx, gy = lax.axis_index("gx"), lax.axis_index("gy")
    odd_z, odd_y = odd("gx"), odd("gy")
    lane = lax.broadcasted_iota(jnp.int32, (8, LANES), 1)
    sub = lax.broadcasted_iota(jnp.int32, (8, LANES), 0)
    scale = [0.5 * spread[f] for f in range(F)]

    def moves(inward):
        rows, whole = [], []
        for c in range(CAP):
            parts = [
                (out.at[:, :, 0, c, 0], first.at[c], rows),
                (out.at[:, :, 7, c, 0], last.at[c], rows),
                (out.at[:, 0:2, :, c, 0], planes.at[c, :, 0:2], whole),
                (out.at[:, 30:32, :, c, 0], planes.at[c, :, 2:4], whole),
            ]
            for k, (there, here, kind) in enumerate(parts):
                source, target = (there, here) if inward else (here, there)
                kind.append(
                    pltpu.make_async_copy(source, target, (sem_in if inward else sem_out).at[c, k])
                )
        return rows, whole

    rows, whole = moves(True)
    for copy in rows + whole:
        copy.start()

    for j in range(4):
        changes = both_ends(
            lambda f, k: jnp.where(odd_z, z_pair[f, k, j], z_cross[f, k, j]),
            lambda f, k: z_own[f, k, j],
            lambda f, k: jnp.where(odd_z, z_cross[f, k, j], z_pair[f, k, j]),
            2, gx > 0, gx < lax.axis_size("gx") - 1, scale,
        )
        for f in range(F):
            for k in range(4):
                z_add[f, k, j] = changes[f][k]
    for b in range(4):
        span = slice(8 * b, 8 * b + 8)
        changes = both_ends(
            lambda f, k: jnp.where(odd_y, y_near[f, k, span, :], y_far[f, k, span, :]),
            lambda f, k: y_own[f, k, span, :],
            lambda f, k: jnp.where(odd_y, y_far[f, k, span, :], y_near[f, k, span, :]),
            1, gy > 0, gy < lax.axis_size("gy") - 1, scale,
        )
        for f in range(F):
            for c, value in enumerate(turned_to_layers(changes[f], lane)):
                y_add[c, f, span, :] = value

    for copy in rows + whole:
        copy.wait()
    corner = ((sub == 0) & (lane < 64)) | ((sub == 7) & (lane >= 64))
    for f in range(F):
        for c in range(CAP):
            for b in range(4):
                span = slice(8 * b, 8 * b + 8)
                value = y_add[c, f, span, :]
                first[c, f, span, :] += jnp.where(lane < 64, value, 0.0)
                last[c, f, span, :] += jnp.where(lane >= 64, value, 0.0)
        for k, z in enumerate((0, 1, 30, 31)):
            values = turned_to_layers([z_add[f, k, j] for j in range(4)], lane)
            for c in range(CAP):
                planes[c, f, k] += values[c] + jnp.where(corner, y_add[c, f, z : z + 1, :], 0.0)
    rows, whole = moves(False)
    run_all(rows)
    run_all(whole)


def ends(spread, *arrays):
    rows = pltpu.VMEM((CAP, F, B, LANES), F32)
    planes = pltpu.VMEM((CAP, F, 4, ROWS, LANES), F32)
    return pl.pallas_call(
        ends_body,
        name="ends",
        out_shape=jax.ShapeDtypeStruct((F, B, ROWS, CAP, 1, LANES), F32),
        in_specs=[SMEM] + [VMEM] * (len(arrays) - 1) + [HBM],
        out_specs=HBM,
        input_output_aliases={len(arrays): 0},
        scratch_shapes=[
            pltpu.VMEM((F, 4, 4, ROWS, LANES), F32),
            rows,
            planes,
            rows,
            rows,
            pltpu.SemaphoreType.DMA((1,)),
            pltpu.SemaphoreType.DMA((CAP, 4)),
            pltpu.SemaphoreType.DMA((CAP, 4)),
        ],
        compiler_params=pltpu.CompilerParams(vmem_limit_bytes=24 << 20),
        cost_estimate=pl.CostEstimate(flops=0, bytes_accessed=6000000, transcendentals=0),
    )(spread, *arrays)


def exchange(block, axes, first, wrap=False):
    count = lax.axis_size(axes)
    pairs = []
    for i in range(first, count, 2):
        j = (i + 1) % count
        if i + 1 < count or wrap:
            pairs += [(i, j), (j, i)]
    return lax.ppermute(block, axes, pairs)


def local(old_state, old_owner, old_slot, diffusivity):
    x = old_state.reshape(8, F, B, ROWS, LANES).transpose(1, 2, 3, 0, 4)[..., None, :]
    far_low, far_high = far_boxes(x)
    *nears, hold_low, hold_high = near_boxes(x, far_low)
    far_low = exchange(far_low, AXES, 1, wrap=True)
    far_high = exchange(far_high, AXES, 1, wrap=True)
    nears = [exchange(near, AXES, 0) for near in nears]
    q_low = turn_low(old_owner, hold_low, *nears[:2], far_low)
    out = step(0, LOW, 7, diffusivity, q_low)
    q_high, z_own, y_own, z_pair, z_cross, y_near, y_far = turn_high(
        old_owner, out, hold_high, *nears[2:], far_high, q_low
    )
    y_near = exchange(y_near, "gy", 0)
    y_far = exchange(y_far, "gy", 1)
    z_pair = exchange(z_pair, "gx", 0)
    z_cross = exchange(z_cross, "gx", 1)
    out = step(LOW, B - LOW, 9, diffusivity, q_high, out)
    out = ends(diffusivity, z_own, y_own, z_pair, z_cross, y_near, y_far, out)
    return out[..., 0, :].transpose(3, 0, 1, 2, 4).reshape(CAP, F, B * B * B)


def solution(mesh):
    placed = (P(AXES, None, None), P(), P(), P())
    return jax.shard_map(
        local, mesh=mesh, in_specs=placed, out_specs=P(AXES, None, None), check_vma=False
    )
```

time: 62 us -> 56.3 us (0.908)
  the two profiles are of different devices: /device:TPU:5 before, /device:TPU:91 now
where the time goes in v4:
time: 56.3 us; the launch traced here: 56 us
  Pallas kernels  32.4 us (58%)
  starting transfers between devices  15.7 us (28%)
  waiting for transfers between devices  4.41 us (8%)
  local copies, waits for them, and re-layouts  3.31 us (6%)
    pallas_call x2, Pallas kernels, step(): pl.pallas_call(functools.partial(step_body, first, count, chunk), name='s...  16 us
    ppermute x10, starting transfers between devices, exchange(): return lax.ppermute(block, axes, pairs)  15.7 us
    pallas_call x2, Pallas kernels, from_slots(): pl.pallas_call(body, name=name, out_shape=shapes, in_specs=[HBM] * len(ar...  7.36 us
    pallas_call x2, Pallas kernels, turn(): pl.pallas_call(body, name=name, out_shape=tuple((jax.ShapeDtypeStruct(sha...  4.83 us
    ppermute x10, waiting for transfers between devices, exchange(): return lax.ppermute(block, axes, pairs)  4.41 us
    pallas_call x1, Pallas kernels, ends(): pl.pallas_call(ends_body, name='ends', out_shape=jax.ShapeDtypeStruct((F,...  4.24 us
    unnamed x12, local copies, waits for them, and re-layouts  3.31 us
  transfers between devices with their start and end apart: 10, of which 3 were waited for; matrix products, arithmetic and copies ran while one was open for 0% of the time, Pallas kernels for 41%

profile of v4, /device:TPU:91, one launch (start us, length us, event | category | flops | bytes accessed | tf_op | source)
XLA Modules:
  0.0 56.0 jit_solution(2913042685374546526)
XLA Ops:
  0.0 2.5 %far.1 = (f32[2,6,16,8,128]{4,3,2,1,0:T(8,128)}, f32[2,6,16,8,128]{4,3,2,1,0:T(8,128)}) custom-call(f32[6,32,8,8,1,128]{5,4,3,2,1,0:T(1,128)} %bitcast.10), custom_call_target="tpu_custom_call" | custom-call | bytes 1000 | tf_op jit(solution)/shard_map/far/pallas_call | solution.py:69
  2.5 0.0 copy-start.3
  2.6 2.0 %collective-permute-start.5 = (f32[2,6,16,8,128]{4,3,2,1,0:T(8,128)}, f32[2,6,16,8,128]{4,3,2,1,0:T(8,128)S(1)}, u32[]{:S(2)}, u32[]{:S(2)}) collective-permute-start(f32[2,6,16,8,128]{4,3,2,1,0:T(8,128)} %get-tuple-element.20.after), channel_id=1, source_target_pairs={{1,2},{2,1},{3,4},{4,3},{5,6},{6,5},{7,8},{8,7},{9,10},{10,9},{11,... | collective-permute-start | bytes 2359304 | tf_op jit(solution)/shard_map/ppermute | solution.py:493
  4.6 4.8 %near.1 = (f32[2,6,8,8,128]{4,3,2,1,0:T(8,128)}, f32[2,6,8,8,128]{4,3,2,1,0:T(8,128)}, f32[2,6,8,8,128]{4,3,2,1,0:T(8,128)}, f32[2,6,8,8,128]{4,3,2,1,0:T(8,128)...) custom-call(f32[6,32,8,8,1,128]{5,4,3,2,1,0:T(1,128)} %bitcast.11, ...), custom_call_target="tpu_custom_call" | custom-call | bytes 1000 | tf_op jit(solution)/shard_map/near/pallas_call | solution.py:69
  9.4 0.0 copy-start.4
  9.4 0.1 collective-permute-start.3
  9.6 0.2 collective-permute-start.2
  9.7 0.4 collective-permute-start.4
  10.2 0.1 collective-permute-start
  10.2 1.2 %collective-permute-done.3.near_0 = f32[2,6,8,8,128]{4,3,2,1,0:T(8,128)S(1)} collective-permute-done((f32[2,6,8,8,128]{4,3,2,1,0:T(8,128)}, f32[2,6,8,8,128]{4,3,2,1,0:T(8,128)S(1)}, u32[]{:S(2)}, u32[]{:S(2)}) %collective-permute-start.3) | collective-permute-done | bytes 393248 | tf_op jit(solution)/shard_map/ppermute | solution.py:493
  11.5 0.1 collective-permute-start.1
  11.6 0.4 collective-permute-done.4.near_1
  12.0 2.7 %collective-permute-done.5.far = f32[2,6,16,8,128]{4,3,2,1,0:T(8,128)S(1)} collective-permute-done((f32[2,6,16,8,128]{4,3,2,1,0:T(8,128)}, f32[2,6,16,8,128]{4,3,2,1,0:T(8,128)S(1)}, u32[]{:S(2)}, u32[]{:S(2)}) %collective-permute-start.5) | collective-permute-done | bytes 786464 | tf_op jit(solution)/shard_map/ppermute | solution.py:493
  14.8 1.4 %copy-done.2 = f32[4,6,16,8,128]{4,3,2,1,0:T(8,128)S(1)} copy-done((f32[4,6,16,8,128]{4,3,2,1,0:T(8,128)S(1)}, f32[4,6,16,8,128]{4,3,2,1,0:T(8,128)}, u32[]{:S(2)}) %copy-start.2) | copy-done | bytes 1572888
  16.2 2.2 %turn_low.1.q.q_low = f32[6,24,4,8,128]{4,3,2,1,0:T(8,128)S(1)} custom-call(s32[512]{0:T(512)S(1)} %copy-done.3, f32[4,6,16,8,128]{4,3,2,1,0:T(8,128)S(1)} %copy-done.2, f32[2,6,8,8,128]{4,3,2,1,0:T(8,128)S(1)} %collective-permute-done.3.near_0, f32[2,6,8,8,128]{4,3,2,1,0:T(8,128)S(1)} %collective-permute-done.4.near_1, ...), custom_call_target="tpu_custom_call" | custom-call | bytes 6000000 | tf_op jit(solution)/shard_map/turn_low/pallas_call | solution.py:182
  18.4 7.3 %step.2.after.rest_0_ = f32[6,32,8,4,1,128]{5,4,3,2,1,0:T(1,128)} custom-call(f32[6]{0:T(128)S(1)} %copy-done.4, f32[6,24,4,8,128]{4,3,2,1,0:T(8,128)S(1)} %turn_low.1.q.q_low), custom_call_target="tpu_custom_call" | custom-call | bytes 20000000 | tf_op jit(solution)/shard_map/step/pallas_call | solution.py:332
  25.8 1.9 %copy-done = f32[6,32,8,4,1,128]{5,4,3,2,1,0:T(1,128)S(1)} copy-done((f32[6,32,8,4,1,128]{5,4,3,2,1,0:T(1,128)S(1)}, f32[6,32,8,4,1,128]{5,4,3,2,1,0:T(1,128)}, u32[]{:S(2)}) %copy-start) | copy-done | bytes 3145752
  27.7 2.7 %turn_high.1 = (f32[6,28,4,8,128]{4,3,2,1,0:T(8,128)S(1)}, f32[6,4,4,8,128]{4,3,2,1,0:T(8,128)S(1)}, f32[6,4,32,128]{3,2,1,0:T(8,128)S(1)}, f32[6,2,4,8,128]{4,3...) custom-call(s32[512]{0:T(512)S(1)} %copy-done.3, ...), custom_call_target="tpu_custom_call" | custom-call | bytes 6000000 | tf_op jit(solution)/shard_map/turn_high/pallas_call | solution.py:182
  30.3 0.3 collective-permute-start.6
  30.7 3.8 %collective-permute-start.7 = (f32[6,2,4,8,128]{4,3,2,1,0:T(8,128)S(1)}, f32[6,2,4,8,128]{4,3,2,1,0:T(8,128)S(1)}, u32[]{:S(2)}, u32[]{:S(2)}) collective-permute-start(f32[6,2,4,8,128]{4,3,2,1,0:T(8,128)S(1)} %get-tuple-element.31), channel_id=1, source_target_pairs={{32,64},{64,32},{33,65},{65,33},{34,66},{66,34},{35,67},{67,35},{3... | collective-permute-start | bytes 589832 | tf_op jit(solution)/shard_map/ppermute | solution.py:493
  34.5 0.9 %collective-permute-start.8 = (f32[6,2,32,128]{3,2,1,0:T(8,128)S(1)}, f32[6,2,32,128]{3,2,1,0:T(8,128)S(1)}, u32[]{:S(2)}, u32[]{:S(2)}) collective-permute-start(f32[6,2,32,128]{3,2,1,0:T(8,128)S(1)} %get-tuple-element.32), channel_id=1, source_target_pairs={{0,1},{1,0},{2,3},{3,2},{4,5},{5,4},{6,7},{7,6},{8,9},{9,8},{10,11... | collective-permute-start | bytes 589832 | tf_op jit(solution)/shard_map/ppermute | solution.py:493
  35.3 7.8 %collective-permute-start.9 = (f32[6,2,32,128]{3,2,1,0:T(8,128)S(1)}, f32[6,2,32,128]{3,2,1,0:T(8,128)S(1)}, u32[]{:S(2)}, u32[]{:S(2)}) collective-permute-start(f32[6,2,32,128]{3,2,1,0:T(8,128)S(1)} %get-tuple-element.33), channel_id=1, source_target_pairs={{1,2},{2,1},{3,4},{4,3},{5,6},{6,5},{7,8},{8,7},{9,10},{10,9},{11,... | collective-permute-start | bytes 589832 | tf_op jit(solution)/shard_map/ppermute | solution.py:493
  43.1 8.7 %step.3.before = f32[6,32,8,4,1,128]{5,4,3,2,1,0:T(1,128)} custom-call(f32[6]{0:T(128)S(1)} %copy-done.4, f32[6,28,4,8,128]{4,3,2,1,0:T(8,128)S(1)} %get-tuple-element.34.q, f32[6,32,8,4,1,128]{5,4,3,2,1,0:T(1,128)} %step.2.after.rest_0_), custom_call_target="tpu_custom_call", output_to_operand_aliasing={{}: (2, {})} | custom-call | bytes 20000000 | tf_op jit(solution)/shard_map/step/pallas_call | solution.py:332
  51.8 4.2 %ends.1 = f32[6,32,8,4,1,128]{5,4,3,2,1,0:T(1,128)} custom-call(f32[6]{0:T(128)S(1)} %copy-done.4, f32[6,4,4,8,128]{4,3,2,1,0:T(8,128)S(1)} %get-tuple-element.28.z_own, f32[6,4,32,128]{3,2,1,0:T(8,128)S(1)} %get-tuple-element.29.y_own, f32[6,2,4,8,128]{4,3,2,1,0:T(8,128)S(1)} %collective-permute-done.6.z_pair, ...), custom_call_target="tpu_custom_call", output_to_operand_aliasing={{}: (7, {})} | custom-call | bytes 6000000 | tf_op jit(solution)/shard_map/ends/pallas_call | solution.py:464
  (15 shorter events, 0.0 us)
Async XLA Ops:
  2.5 7.0 %copy-start.5 = (f32[2,6,16,8,128]{4,3,2,1,0:T(8,128)S(1)}, f32[2,6,16,8,128]{4,3,2,1,0:T(8,128)}, u32[]{:S(2)}) copy-start(f32[2,6,16,8,128]{4,3,2,1,0:T(8,128)} %get-tuple-element.24) | copy-start | bytes 2359300
  2.5 12.2 %copy-start.3 = (s32[512]{0:T(512)S(1)}, s32[512]{0:T(512)}, u32[]{:S(2)}) copy-start(s32[512]{0:T(512)} %owner.3) | copy-start | bytes 6148
  2.6 12.2 %collective-permute-start.5 = (f32[2,6,16,8,128]{4,3,2,1,0:T(8,128)}, f32[2,6,16,8,128]{4,3,2,1,0:T(8,128)S(1)}, u32[]{:S(2)}, u32[]{:S(2)}) collective-permute-start(f32[2,6,16,8,128]{4,3,2,1,0:T(8,128)} %get-tuple-element.20.after), channel_id=1, source_target_pairs={{1,2},{2,1},{3,4},{4,3},{5,6},{6,5},{7,8},{8,7},{9,10},{10,9},{11,... | collective-permute-start | bytes 2359304 | tf_op jit(solution)/shard_map/ppermute | solution.py:493
  9.4 8.9 %copy-start.4 = (f32[6]{0:T(128)S(1)}, f32[6]{0:T(128)}, u32[]{:S(2)}) copy-start(f32[6]{0:T(128)} %spread.5) | copy-start | bytes 76
  9.4 2.0 %collective-permute-start.3 = (f32[2,6,8,8,128]{4,3,2,1,0:T(8,128)}, f32[2,6,8,8,128]{4,3,2,1,0:T(8,128)S(1)}, u32[]{:S(2)}, u32[]{:S(2)}) collective-permute-start(f32[2,6,8,8,128]{4,3,2,1,0:T(8,128)} %get-tuple-element.26), channel_id=1, source_target_pairs={{0,1},{1,0},{2,3},{3,2},{4,5},{5,4},{6,7},{7,6},{8,9},{9,8},{10,11... | collective-permute-start | bytes 1179656 | tf_op jit(solution)/shard_map/ppermute | solution.py:493
  9.6 16.2 %collective-permute-start.2 = (f32[2,6,16,8,128]{4,3,2,1,0:T(8,128)S(1)}, f32[2,6,16,8,128]{4,3,2,1,0:T(8,128)S(1)}, u32[]{:S(2)}, u32[]{:S(2)}) collective-permute-start(f32[2,6,16,8,128]{4,3,2,1,0:T(8,128)S(1)} %copy-done.5), channel_id=1, source_target_pairs={{1,2},{2,1},{3,4},{4,3},{5,6},{6,5},{7,8},{8,7},{9,10},{10,9},{11,... | collective-permute-start | bytes 2359304 | tf_op jit(solution)/shard_map/ppermute | solution.py:493
  9.7 2.3 %collective-permute-start.4 = (f32[2,6,8,8,128]{4,3,2,1,0:T(8,128)}, f32[2,6,8,8,128]{4,3,2,1,0:T(8,128)S(1)}, u32[]{:S(2)}, u32[]{:S(2)}) collective-permute-start(f32[2,6,8,8,128]{4,3,2,1,0:T(8,128)} %get-tuple-element.27), channel_id=1, source_target_pairs={{0,1},{1,0},{2,3},{3,2},{4,5},{5,4},{6,7},{7,6},{8,9},{9,8},{10,11... | collective-permute-start | bytes 1179656 | tf_op jit(solution)/shard_map/ppermute | solution.py:493
  10.2 15.6 %collective-permute-start = (f32[2,6,8,8,128]{4,3,2,1,0:T(8,128)}, f32[2,6,8,8,128]{4,3,2,1,0:T(8,128)S(1)}, u32[]{:S(2)}, u32[]{:S(2)}) collective-permute-start(f32[2,6,8,8,128]{4,3,2,1,0:T(8,128)} %get-tuple-element.22), channel_id=1, source_target_pairs={{0,1},{1,0},{2,3},{3,2},{4,5},{5,4},{6,7},{7,6},{8,9},{9,8},{10,11... | collective-permute-start | bytes 1179656 | tf_op jit(solution)/shard_map/ppermute | solution.py:493
  11.5 14.3 %collective-permute-start.1 = (f32[2,6,8,8,128]{4,3,2,1,0:T(8,128)}, f32[2,6,8,8,128]{4,3,2,1,0:T(8,128)S(1)}, u32[]{:S(2)}, u32[]{:S(2)}) collective-permute-start(f32[2,6,8,8,128]{4,3,2,1,0:T(8,128)} %get-tuple-element.23), channel_id=1, source_target_pairs={{0,1},{1,0},{2,3},{3,2},{4,5},{5,4},{6,7},{7,6},{8,9},{9,8},{10,11... | collective-permute-start | bytes 1179656 | tf_op jit(solution)/shard_map/ppermute | solution.py:493
  14.8 1.4 %copy-start.2 = (f32[4,6,16,8,128]{4,3,2,1,0:T(8,128)S(1)}, f32[4,6,16,8,128]{4,3,2,1,0:T(8,128)}, u32[]{:S(2)}) copy-start(f32[4,6,16,8,128]{4,3,2,1,0:T(8,128)} %get-tuple-element.25.hold) | copy-start | bytes 4718596
  18.4 7.4 %copy-start.1 = (f32[4,6,16,8,128]{4,3,2,1,0:T(8,128)S(1)}, f32[4,6,16,8,128]{4,3,2,1,0:T(8,128)}, u32[]{:S(2)}) copy-start(f32[4,6,16,8,128]{4,3,2,1,0:T(8,128)} %get-tuple-element.21.hold) | copy-start | bytes 4718596
  25.8 1.9 %copy-start = (f32[6,32,8,4,1,128]{5,4,3,2,1,0:T(1,128)S(1)}, f32[6,32,8,4,1,128]{5,4,3,2,1,0:T(1,128)}, u32[]{:S(2)}) copy-start(f32[6,32,8,4,1,128]{5,4,3,2,1,0:T(1,128)} %step.2.after.rest_0_) | copy-start | bytes 9437188
  30.3 21.4 %collective-permute-start.6 = (f32[6,2,4,8,128]{4,3,2,1,0:T(8,128)S(1)}, f32[6,2,4,8,128]{4,3,2,1,0:T(8,128)S(1)}, u32[]{:S(2)}, u32[]{:S(2)}) collective-permute-start(f32[6,2,4,8,128]{4,3,2,1,0:T(8,128)S(1)} %get-tuple-element.30), channel_id=1, source_target_pairs={{0,32},{32,0},{64,96},{96,64},{1,33},{33,1},{65,97},{97,65},{2,34}... | collective-permute-start | bytes 589832 | tf_op jit(solution)/shard_map/ppermute | solution.py:493
  30.7 21.1 %collective-permute-start.7 = (f32[6,2,4,8,128]{4,3,2,1,0:T(8,128)S(1)}, f32[6,2,4,8,128]{4,3,2,1,0:T(8,128)S(1)}, u32[]{:S(2)}, u32[]{:S(2)}) collective-permute-start(f32[6,2,4,8,128]{4,3,2,1,0:T(8,128)S(1)} %get-tuple-element.31), channel_id=1, source_target_pairs={{32,64},{64,32},{33,65},{65,33},{34,66},{66,34},{35,67},{67,35},{3... | collective-permute-start | bytes 589832 | tf_op jit(solution)/shard_map/ppermute | solution.py:493
  34.5 17.3 %collective-permute-start.8 = (f32[6,2,32,128]{3,2,1,0:T(8,128)S(1)}, f32[6,2,32,128]{3,2,1,0:T(8,128)S(1)}, u32[]{:S(2)}, u32[]{:S(2)}) collective-permute-start(f32[6,2,32,128]{3,2,1,0:T(8,128)S(1)} %get-tuple-element.32), channel_id=1, source_target_pairs={{0,1},{1,0},{2,3},{3,2},{4,5},{5,4},{6,7},{7,6},{8,9},{9,8},{10,11... | collective-permute-start | bytes 589832 | tf_op jit(solution)/shard_map/ppermute | solution.py:493
  35.3 16.5 %collective-permute-start.9 = (f32[6,2,32,128]{3,2,1,0:T(8,128)S(1)}, f32[6,2,32,128]{3,2,1,0:T(8,128)S(1)}, u32[]{:S(2)}, u32[]{:S(2)}) collective-permute-start(f32[6,2,32,128]{3,2,1,0:T(8,128)S(1)} %get-tuple-element.33), channel_id=1, source_target_pairs={{1,2},{2,1},{3,4},{4,3},{5,6},{6,5},{7,8},{8,7},{9,10},{10,9},{11,... | collective-permute-start | bytes 589832 | tf_op jit(solution)/shard_map/ppermute | solution.py:493

commit v5 on v4

--- a/solution.py
+++ b/solution.py
@@ -41,30 +41,26 @@
     ]
 
 
-def far_body(x, low, high, sem):
-    run_all(
-        leaving_copies(x, False, low, slice(0, HALF), sem.at[0])
-        + leaving_copies(x, False, high, slice(HALF, B), sem.at[1])
-    )
-
-
-def near_body(x, after, *rest):
+def far_body(x, low, token, sem):
+    token[...] = jnp.zeros_like(token)
+    run_all(leaving_copies(x, False, low, slice(0, HALF), sem))
+
+
+def near_body(x, after, high, *rest):
     nears, (hold_low, hold_high, sem) = rest[:PARTS], rest[PARTS:]
-    copies = []
+    copies = leaving_copies(x, False, high, slice(HALF, B), sem.at[2 + PARTS])
     for k, near in enumerate(nears):
         copies += leaving_copies(x, True, near, slice(8 * k, 8 * k + 8), sem.at[2 + k])
     for k, hold in enumerate((hold_low, hold_high)):
         for c in range(CAP):
             planes = slice(HALF * k, HALF * k + HALF)
             copies.append(
-                pltpu.make_async_copy(
-                    x.at[:, planes, :, 2 + c, 0], hold.at[c], sem.at[k, c]
-                )
+                pltpu.make_async_copy(x.at[:, planes, :, 2 + c, 0], hold.at[c], sem.at[k, c])
             )
     run_all(copies)
 
 
-def from_slots(body, name, arrays, shapes, sems):
+def from_slots(body, name, arrays, shapes, sems, limit):
     shapes = tuple(jax.ShapeDtypeStruct(shape, F32) for shape in shapes)
     return pl.pallas_call(
         body,
@@ -73,21 +69,20 @@
         in_specs=[HBM] * len(arrays),
         out_specs=(VMEM,) * len(shapes),
         scratch_shapes=[pltpu.SemaphoreType.DMA(sems)],
-        compiler_params=pltpu.CompilerParams(vmem_limit_bytes=WIDE),
+        compiler_params=pltpu.CompilerParams(vmem_limit_bytes=limit),
         cost_estimate=pl.CostEstimate(flops=0, bytes_accessed=1000, transcendentals=0),
     )(*arrays)
 
 
 def far_boxes(x):
-    return from_slots(far_body, "far", [x], [(2, F, HALF, ROWS, LANES)] * 2, (2, 2))
+    return from_slots(far_body, "far", [x], [(2, F, HALF, ROWS, LANES), (ROWS, LANES)], (2,), WIDE)
 
 
 def near_boxes(x, after):
+    part = (2, F, B // PARTS, ROWS, LANES)
     half = (CAP, F, HALF, ROWS, LANES)
-    part = (2, F, B // PARTS, ROWS, LANES)
-    return from_slots(
-        near_body, "near", [x, after], [part] * PARTS + [half, half], (2 + PARTS, CAP)
-    )
+    shapes = [(2, F, HALF, ROWS, LANES)] + [part] * PARTS + [half, half]
+    return from_slots(near_body, "near", [x, after], shapes, (3 + PARTS, CAP), 24 << 20)
 
 
 def device_number():
@@ -122,28 +117,34 @@
     return *swap_32(a, b, lane), *swap_32(c, d, lane)
 
 
-def turn_half(kept, hold, nears, far, target, index):
+def turn_half(kept, hold, nears, far, target, index, half):
     lane = lax.broadcasted_iota(jnp.int32, (8, LANES), 1)
-    for near, z0 in ((nears[0], 0), (nears[1], 8)):
-
-        def group(g, _):
-            for z in (2 * g, 2 * g + 1):
-                for f in range(F):
-                    v = [
-                        arrived(
-                            kept[c], hold[c, f, z0 + z], c, far[c % 2, f, z0 + z], near[c % 2, f, z]
-                        )
-                        for c in range(CAP)
-                    ]
-                    for j, value in enumerate(turned_to_layers(v, lane)):
-                        target[f, index + z0 + z, j] = value
-            return 0
-
-        lax.fori_loop(0, 4, group, 0)
-
-
-def turn_low_body(owner, hold, near_0, near_1, far, q):
-    turn_half(kept_flags(owner), hold, (near_0, near_1), far, q, 3)
+
+    def first_half(z):
+        near = nears[z // 8]
+        for f in range(F):
+            v = [
+                arrived(kept[c], hold[c, f, z], c, far[c % 2, f, z], near[c % 2, f, z % 8])
+                for c in range(CAP)
+            ]
+            half[z % 8, f, 0], half[z % 8, f, 2] = swap_64(v[0], v[2], lane)
+            half[z % 8, f, 1], half[z % 8, f, 3] = swap_64(v[1], v[3], lane)
+
+    def second_half(z):
+        for f in range(F):
+            a, b, c, d = [half[z % 8, f, j] for j in range(4)]
+            target[f, index + z, 0], target[f, index + z, 1] = swap_32(a, b, lane)
+            target[f, index + z, 2], target[f, index + z, 3] = swap_32(c, d, lane)
+
+    for z in range(HALF + 4):
+        if z < HALF:
+            first_half(z)
+        if z >= 4:
+            second_half(z - 4)
+
+
+def turn_low_body(owner, hold, near_0, near_1, far, q, half):
+    turn_half(kept_flags(owner), hold, (near_0, near_1), far, q, 3, half)
     for f in range(F):
         q[f, 0] = q[f, 3]
         q[f, 1] = q[f, 3]
@@ -151,9 +152,9 @@
 
 
 def turn_high_body(
-    owner, hold, near_0, near_1, far, q_low, after, q, z_own, y_own, z_pair, z_cross, y_near, y_far
+    owner, hold, near_0, near_1, far, q_low, after, q, z_own, y_own, z_pair, z_cross, y_near, y_far, half
 ):
-    turn_half(kept_flags(owner), hold, (near_0, near_1), far, q, 5)
+    turn_half(kept_flags(owner), hold, (near_0, near_1), far, q, 5, half)
     odd_z, odd_y = odd("gx"), odd("gy")
     for f in range(F):
         for k in range(5):
@@ -183,8 +184,9 @@
         body,
         name=name,
         out_shape=tuple(jax.ShapeDtypeStruct(shape, F32) for shape in shapes),
-        in_specs=[SMEM] + [VMEM] * len(arrays) + [HBM] * len(after),
+        in_specs=[SMEM] + [VMEM] * (len(arrays) + len(after)),
         out_specs=(VMEM,) * len(shapes),
+        scratch_shapes=[pltpu.VMEM((8, F, 4, ROWS, LANES), F32)],
         compiler_params=pltpu.CompilerParams(vmem_limit_bytes=24 << 20),
         cost_estimate=pl.CostEstimate(flops=0, bytes_accessed=6000000, transcendentals=0),
     )(owner, *arrays, *after)
@@ -218,8 +220,9 @@
     first, count, chunk, spread, q, *rest,
 ):
     (
-        out, result, carry_p, carry_n, carry_c, dx, dx_old, cx, cx_old, px, mx, nx, done, turned, sem_out,
-    ) = rest[-15:]
+        out, token, result, carry_p, carry_n, carry_c, dx, dx_old, cx, cx_old, px, mx, nx, done, turned, sem_out,
+    ) = rest[-16:]
+    token[...] = jnp.zeros_like(token)
     lane = lax.broadcasted_iota(jnp.int32, (8, LANES), 1)
     sub = lax.broadcasted_iota(jnp.int32, (8, LANES), 0)
     scale = [0.5 * spread[f] for f in range(F)]
@@ -332,9 +335,12 @@
     return pl.pallas_call(
         functools.partial(step_body, first, count, chunk),
         name="step",
-        out_shape=jax.ShapeDtypeStruct((F, B, ROWS, CAP, 1, LANES), F32),
+        out_shape=(
+            jax.ShapeDtypeStruct((F, B, ROWS, CAP, 1, LANES), F32),
+            jax.ShapeDtypeStruct((ROWS, LANES), F32),
+        ),
         in_specs=[SMEM, VMEM] + ([] if out is None else [HBM]),
-        out_specs=HBM,
+        out_specs=(HBM, VMEM),
         input_output_aliases={} if out is None else {2: 0},
         scratch_shapes=[
             planes(CAP, F, count + LEAD),
@@ -441,21 +447,25 @@
 
     for copy in rows + whole:
         copy.wait()
-    corner = ((sub == 0) & (lane < 64)) | ((sub == 7) & (lane >= 64))
-    for f in range(F):
-        for c in range(CAP):
+    rows_out, whole_out = moves(False)
+    for c in range(CAP):
+        for f in range(F):
             for b in range(4):
                 span = slice(8 * b, 8 * b + 8)
                 value = y_add[c, f, span, :]
                 first[c, f, span, :] += jnp.where(lane < 64, value, 0.0)
                 last[c, f, span, :] += jnp.where(lane >= 64, value, 0.0)
+        rows_out[2 * c].start()
+        rows_out[2 * c + 1].start()
+    corner = ((sub == 0) & (lane < 64)) | ((sub == 7) & (lane >= 64))
+    for f in range(F):
         for k, z in enumerate((0, 1, 30, 31)):
             values = turned_to_layers([z_add[f, k, j] for j in range(4)], lane)
             for c in range(CAP):
                 planes[c, f, k] += values[c] + jnp.where(corner, y_add[c, f, z : z + 1, :], 0.0)
-    rows, whole = moves(False)
-    run_all(rows)
-    run_all(whole)
+    for copy in rows_out:
+        copy.wait()
+    run_all(whole_out)
 
 
 def ends(spread, *arrays):
@@ -495,21 +505,21 @@
 
 def local(old_state, old_owner, old_slot, diffusivity):
     x = old_state.reshape(8, F, B, ROWS, LANES).transpose(1, 2, 3, 0, 4)[..., None, :]
-    far_low, far_high = far_boxes(x)
-    *nears, hold_low, hold_high = near_boxes(x, far_low)
+    far_low, token = far_boxes(x)
+    far_high, *nears, hold_low, hold_high = near_boxes(x, token)
     far_low = exchange(far_low, AXES, 1, wrap=True)
     far_high = exchange(far_high, AXES, 1, wrap=True)
     nears = [exchange(near, AXES, 0) for near in nears]
     q_low = turn_low(old_owner, hold_low, *nears[:2], far_low)
-    out = step(0, LOW, 7, diffusivity, q_low)
+    out, token = step(0, LOW, 7, diffusivity, q_low)
     q_high, z_own, y_own, z_pair, z_cross, y_near, y_far = turn_high(
-        old_owner, out, hold_high, *nears[2:], far_high, q_low
+        old_owner, token, hold_high, *nears[2:], far_high, q_low
     )
     y_near = exchange(y_near, "gy", 0)
     y_far = exchange(y_far, "gy", 1)
     z_pair = exchange(z_pair, "gx", 0)
     z_cross = exchange(z_cross, "gx", 1)
-    out = step(LOW, B - LOW, 9, diffusivity, q_high, out)
+    out, _ = step(LOW, B - LOW, 9, diffusivity, q_high, out)
     out = ends(diffusivity, z_own, y_own, z_pair, z_cross, y_near, y_far, out)
     return out[..., 0, :].transpose(3, 0, 1, 2, 4).reshape(CAP, F, B * B * B)
 

time: 56.3 us -> 53.2 us (0.945)
  the two profiles are of different devices: /device:TPU:91 before, /device:TPU:5 now
where the time goes in v5:
time: 53.2 us; the launch traced here: 53 us
  Pallas kernels  29.9 us (56%)
  starting transfers between devices  21.4 us (40%)
  waiting for transfers between devices  0.86 us (2%)
  local copies, waits for them, and re-layouts  0.69 us (1%)
    ppermute x10, starting transfers between devices, exchange(): return lax.ppermute(block, axes, pairs)  21.4 us
    pallas_call x2, Pallas kernels, step(): pl.pallas_call(functools.partial(step_body, first, count, chunk), name='s...  16.4 us
    pallas_call x2, Pallas kernels, from_slots(): pl.pallas_call(body, name=name, out_shape=shapes, in_specs=[HBM] * len(ar...  6.23 us
    pallas_call x1, Pallas kernels, ends(): pl.pallas_call(ends_body, name='ends', out_shape=jax.ShapeDtypeStruct((F,...  4.17 us
    pallas_call x2, Pallas kernels, turn(): pl.pallas_call(body, name=name, out_shape=tuple((jax.ShapeDtypeStruct(sha...  3.13 us
  transfers between devices with their start and end apart: 10, of which 1 were waited for; matrix products, arithmetic and copies ran while one was open for 0% of the time, Pallas kernels for 41%

profile of v5, /device:TPU:5, one launch (start us, length us, event | category | flops | bytes accessed | tf_op | source)
XLA Modules:
  0.0 53.0 jit_solution(509320672975125986)
XLA Ops:
  0.0 2.2 %far.1 = (f32[2,6,16,8,128]{4,3,2,1,0:T(8,128)}, f32[8,128]{1,0:T(8,128)}) custom-call(f32[6,32,8,8,1,128]{5,4,3,2,1,0:T(1,128)} %bitcast.10), custom_call_target="tpu_custom_call" | custom-call | bytes 1000 | tf_op jit(solution)/shard_map/far/pallas_call | solution.py:65
  2.2 2.3 %collective-permute-start.5 = (f32[2,6,16,8,128]{4,3,2,1,0:T(8,128)}, f32[2,6,16,8,128]{4,3,2,1,0:T(8,128)S(1)}, u32[]{:S(2)}, u32[]{:S(2)}) collective-permute-start(f32[2,6,16,8,128]{4,3,2,1,0:T(8,128)} %get-tuple-element.32), channel_id=1, source_target_pairs={{1,2},{2,1},{3,4},{4,3},{5,6},{6,5},{7,8},{8,7},{9,10},{10,9},{11,... | collective-permute-start | bytes 2359304 | tf_op jit(solution)/shard_map/ppermute | solution.py:503
  4.5 0.7 %copy-done.3 = f32[8,128]{1,0:T(8,128)S(1)} copy-done((f32[8,128]{1,0:T(8,128)S(1)}, f32[8,128]{1,0:T(8,128)}, u32[]{:S(2)}) %copy-start.3) | copy-done | bytes 4120
  5.1 4.1 %near.1 = (f32[2,6,16,8,128]{4,3,2,1,0:T(8,128)S(1)}, f32[2,6,8,8,128]{4,3,2,1,0:T(8,128)S(1)}, f32[2,6,8,8,128]{4,3,2,1,0:T(8,128)S(1)}, f32[2,6,8,8,128]{4,3,2...) custom-call(f32[6,32,8,8,1,128]{5,4,3,2,1,0:T(1,128)S(1)} %bitcast.1, ...), custom_call_target="tpu_custom_call" | custom-call | bytes 1000 | tf_op jit(solution)/shard_map/near/pallas_call | solution.py:65
  9.2 0.0 copy-start.2
  9.2 4.5 %collective-permute-start.3 = (f32[2,6,8,8,128]{4,3,2,1,0:T(8,128)S(1)}, f32[2,6,8,8,128]{4,3,2,1,0:T(8,128)S(1)}, u32[]{:S(2)}, u32[]{:S(2)}) collective-permute-start(f32[2,6,8,8,128]{4,3,2,1,0:T(8,128)S(1)} %get-tuple-element.30), channel_id=1, source_target_pairs={{0,1},{1,0},{2,3},{3,2},{4,5},{5,4},{6,7},{7,6},{8,9},{9,8},{10,11... | collective-permute-start | bytes 1179656 | tf_op jit(solution)/shard_map/ppermute | solution.py:503
  13.7 1.7 %collective-permute-start.4 = (f32[2,6,8,8,128]{4,3,2,1,0:T(8,128)S(1)}, f32[2,6,8,8,128]{4,3,2,1,0:T(8,128)S(1)}, u32[]{:S(2)}, u32[]{:S(2)}) collective-permute-start(f32[2,6,8,8,128]{4,3,2,1,0:T(8,128)S(1)} %get-tuple-element.31), channel_id=1, source_target_pairs={{0,1},{1,0},{2,3},{3,2},{4,5},{5,4},{6,7},{7,6},{8,9},{9,8},{10,11... | collective-permute-start | bytes 1179656 | tf_op jit(solution)/shard_map/ppermute | solution.py:503
  15.4 0.0 collective-permute-start
  15.4 0.0 collective-permute-done.3.near_0
  15.4 0.5 collective-permute-start.1
  15.9 0.8 %collective-permute-done.4.near_1 = f32[2,6,8,8,128]{4,3,2,1,0:T(8,128)S(1)} collective-permute-done((f32[2,6,8,8,128]{4,3,2,1,0:T(8,128)S(1)}, f32[2,6,8,8,128]{4,3,2,1,0:T(8,128)S(1)}, u32[]{:S(2)}, u32[]{:S(2)}) %collective-permute-start.4) | collective-permute-done | bytes 393248 | tf_op jit(solution)/shard_map/ppermute | solution.py:503
  16.8 0.0 collective-permute-done.5.far
  16.8 1.3 %turn_low.1.q.q_low = f32[6,24,4,8,128]{4,3,2,1,0:T(8,128)S(1)} custom-call(s32[512]{0:T(512)S(1)} %copy-done.1, f32[4,6,16,8,128]{4,3,2,1,0:T(8,128)S(1)} %get-tuple-element.29.hold, f32[2,6,8,8,128]{4,3,2,1,0:T(8,128)S(1)} %collective-permute-done.3.near_0, f32[2,6,8,8,128]{4,3,2,1,0:T(8,128)S(1)} %collective-permute-done.4.near_1, ...), custom_call_target="tpu_custom_call" | custom-call | bytes 6000000 | tf_op jit(solution)/shard_map/turn_low/pallas_call | solution.py:183
  18.1 7.3 %step.2 = (f32[6,32,8,4,1,128]{5,4,3,2,1,0:T(1,128)}, f32[8,128]{1,0:T(8,128)S(1)}) custom-call(f32[6]{0:T(128)S(1)} %copy-done.2, f32[6,24,4,8,128]{4,3,2,1,0:T(8,128)S(1)} %turn_low.1.q.q_low), custom_call_target="tpu_custom_call" | custom-call | bytes 20000000 | tf_op jit(solution)/shard_map/step/pallas_call | solution.py:335
  25.5 0.0 collective-permute-done.2.far
  25.5 1.8 %turn_high.1 = (f32[6,28,4,8,128]{4,3,2,1,0:T(8,128)S(1)}, f32[6,4,4,8,128]{4,3,2,1,0:T(8,128)S(1)}, f32[6,4,32,128]{3,2,1,0:T(8,128)S(1)}, f32[6,2,4,8,128]{4,3...) custom-call(s32[512]{0:T(512)S(1)} %copy-done.1, ...), custom_call_target="tpu_custom_call" | custom-call | bytes 6000000 | tf_op jit(solution)/shard_map/turn_high/pallas_call | solution.py:183
  27.3 1.3 %collective-permute-start.6 = (f32[6,2,4,8,128]{4,3,2,1,0:T(8,128)S(1)}, f32[6,2,4,8,128]{4,3,2,1,0:T(8,128)S(1)}, u32[]{:S(2)}, u32[]{:S(2)}) collective-permute-start(f32[6,2,4,8,128]{4,3,2,1,0:T(8,128)S(1)} %get-tuple-element.36), channel_id=1, source_target_pairs={{0,32},{32,0},{64,96},{96,64},{1,33},{33,1},{65,97},{97,65},{2,34}... | collective-permute-start | bytes 589832 | tf_op jit(solution)/shard_map/ppermute | solution.py:503
  28.6 3.4 %collective-permute-start.7 = (f32[6,2,4,8,128]{4,3,2,1,0:T(8,128)S(1)}, f32[6,2,4,8,128]{4,3,2,1,0:T(8,128)S(1)}, u32[]{:S(2)}, u32[]{:S(2)}) collective-permute-start(f32[6,2,4,8,128]{4,3,2,1,0:T(8,128)S(1)} %get-tuple-element.37), channel_id=1, source_target_pairs={{32,64},{64,32},{33,65},{65,33},{34,66},{66,34},{35,67},{67,35},{3... | collective-permute-start | bytes 589832 | tf_op jit(solution)/shard_map/ppermute | solution.py:503
  32.0 5.8 %collective-permute-start.8 = (f32[6,2,32,128]{3,2,1,0:T(8,128)S(1)}, f32[6,2,32,128]{3,2,1,0:T(8,128)S(1)}, u32[]{:S(2)}, u32[]{:S(2)}) collective-permute-start(f32[6,2,32,128]{3,2,1,0:T(8,128)S(1)} %get-tuple-element.38), channel_id=1, source_target_pairs={{0,1},{1,0},{2,3},{3,2},{4,5},{5,4},{6,7},{7,6},{8,9},{9,8},{10,11... | collective-permute-start | bytes 589832 | tf_op jit(solution)/shard_map/ppermute | solution.py:503
  37.8 1.9 %collective-permute-start.9 = (f32[6,2,32,128]{3,2,1,0:T(8,128)S(1)}, f32[6,2,32,128]{3,2,1,0:T(8,128)S(1)}, u32[]{:S(2)}, u32[]{:S(2)}) collective-permute-start(f32[6,2,32,128]{3,2,1,0:T(8,128)S(1)} %get-tuple-element.39), channel_id=1, source_target_pairs={{1,2},{2,1},{3,4},{4,3},{5,6},{6,5},{7,8},{8,7},{9,10},{10,9},{11,... | collective-permute-start | bytes 589832 | tf_op jit(solution)/shard_map/ppermute | solution.py:503
  39.7 9.1 %step.3 = (f32[6,32,8,4,1,128]{5,4,3,2,1,0:T(1,128)}, f32[8,128]{1,0:T(8,128)}) custom-call(f32[6]{0:T(128)S(1)} %copy-done.2, f32[6,28,4,8,128]{4,3,2,1,0:T(8,128)S(1)} %get-tuple-element.40.q, f32[6,32,8,4,1,128]{5,4,3,2,1,0:T(1,128)} %get-tuple-element.41.rest_0_), custom_call_target="tpu_custom_call", output_to_operand_aliasing={{0}: (2, {})} | custom-call | bytes 20000000 | tf_op jit(solution)/shard_map/step/pallas_call | solution.py:335
  48.8 0.0 collective-permute-done.8.y_near
  48.8 0.0 collective-permute-done.9.y_far
  48.8 4.2 %ends.1 = f32[6,32,8,4,1,128]{5,4,3,2,1,0:T(1,128)} custom-call(f32[6]{0:T(128)S(1)} %copy-done.2, f32[6,4,4,8,128]{4,3,2,1,0:T(8,128)S(1)} %get-tuple-element.34.z_own, f32[6,4,32,128]{3,2,1,0:T(8,128)S(1)} %get-tuple-element.35.y_own, f32[6,2,4,8,128]{4,3,2,1,0:T(8,128)S(1)} %collective-permute-done.6.z_pair, ...), custom_call_target="tpu_custom_call", output_to_operand_aliasing={{}: (7, {})} | custom-call | bytes 6000000 | tf_op jit(solution)/shard_map/ends/pallas_call | solution.py:474
  (11 shorter events, 0.0 us)
Async XLA Ops:
  0.0 4.5 %copy-start = (f32[8,6,32768]{2,0,1:T(8,128)S(1)}, f32[8,6,32768]{2,0,1:T(8,128)}, u32[]{:S(2)}) copy-start(f32[8,6,32768]{2,0,1:T(8,128)} %param.4) | copy-start | bytes 18874372
  2.2 14.6 %collective-permute-start.5 = (f32[2,6,16,8,128]{4,3,2,1,0:T(8,128)}, f32[2,6,16,8,128]{4,3,2,1,0:T(8,128)S(1)}, u32[]{:S(2)}, u32[]{:S(2)}) collective-permute-start(f32[2,6,16,8,128]{4,3,2,1,0:T(8,128)} %get-tuple-element.32), channel_id=1, source_target_pairs={{1,2},{2,1},{3,4},{4,3},{5,6},{6,5},{7,8},{8,7},{9,10},{10,9},{11,... | collective-permute-start | bytes 2359304 | tf_op jit(solution)/shard_map/ppermute | solution.py:503
  4.5 0.7 %copy-start.3 = (f32[8,128]{1,0:T(8,128)S(1)}, f32[8,128]{1,0:T(8,128)}, u32[]{:S(2)}) copy-start(f32[8,128]{1,0:T(8,128)} %get-tuple-element.24.after) | copy-start | bytes 12292
  5.1 11.6 %copy-start.1 = (s32[512]{0:T(512)S(1)}, s32[512]{0:T(512)}, u32[]{:S(2)}) copy-start(s32[512]{0:T(512)} %owner.3) | copy-start | bytes 6148
  9.2 8.9 %copy-start.2 = (f32[6]{0:T(128)S(1)}, f32[6]{0:T(128)}, u32[]{:S(2)}) copy-start(f32[6]{0:T(128)} %spread.5) | copy-start | bytes 76
  9.2 6.2 %collective-permute-start.3 = (f32[2,6,8,8,128]{4,3,2,1,0:T(8,128)S(1)}, f32[2,6,8,8,128]{4,3,2,1,0:T(8,128)S(1)}, u32[]{:S(2)}, u32[]{:S(2)}) collective-permute-start(f32[2,6,8,8,128]{4,3,2,1,0:T(8,128)S(1)} %get-tuple-element.30), channel_id=1, source_target_pairs={{0,1},{1,0},{2,3},{3,2},{4,5},{5,4},{6,7},{7,6},{8,9},{9,8},{10,11... | collective-permute-start | bytes 1179656 | tf_op jit(solution)/shard_map/ppermute | solution.py:503
  13.7 11.8 %collective-permute-start.2 = (f32[2,6,16,8,128]{4,3,2,1,0:T(8,128)S(1)}, f32[2,6,16,8,128]{4,3,2,1,0:T(8,128)S(1)}, u32[]{:S(2)}, u32[]{:S(2)}) collective-permute-start(f32[2,6,16,8,128]{4,3,2,1,0:T(8,128)S(1)} %get-tuple-element.28), channel_id=1, source_target_pairs={{1,2},{2,1},{3,4},{4,3},{5,6},{6,5},{7,8},{8,7},{9,10},{10,9},{11,... | collective-permute-start | bytes 2359304 | tf_op jit(solution)/shard_map/ppermute | solution.py:503
  13.7 3.1 %collective-permute-start.4 = (f32[2,6,8,8,128]{4,3,2,1,0:T(8,128)S(1)}, f32[2,6,8,8,128]{4,3,2,1,0:T(8,128)S(1)}, u32[]{:S(2)}, u32[]{:S(2)}) collective-permute-start(f32[2,6,8,8,128]{4,3,2,1,0:T(8,128)S(1)} %get-tuple-element.31), channel_id=1, source_target_pairs={{0,1},{1,0},{2,3},{3,2},{4,5},{5,4},{6,7},{7,6},{8,9},{9,8},{10,11... | collective-permute-start | bytes 1179656 | tf_op jit(solution)/shard_map/ppermute | solution.py:503
  15.4 10.0 %collective-permute-start = (f32[2,6,8,8,128]{4,3,2,1,0:T(8,128)S(1)}, f32[2,6,8,8,128]{4,3,2,1,0:T(8,128)S(1)}, u32[]{:S(2)}, u32[]{:S(2)}) collective-permute-start(f32[2,6,8,8,128]{4,3,2,1,0:T(8,128)S(1)} %get-tuple-element.26), channel_id=1, source_target_pairs={{0,1},{1,0},{2,3},{3,2},{4,5},{5,4},{6,7},{7,6},{8,9},{9,8},{10,11... | collective-permute-start | bytes 1179656 | tf_op jit(solution)/shard_map/ppermute | solution.py:503
  15.4 10.0 %collective-permute-start.1 = (f32[2,6,8,8,128]{4,3,2,1,0:T(8,128)S(1)}, f32[2,6,8,8,128]{4,3,2,1,0:T(8,128)S(1)}, u32[]{:S(2)}, u32[]{:S(2)}) collective-permute-start(f32[2,6,8,8,128]{4,3,2,1,0:T(8,128)S(1)} %get-tuple-element.27), channel_id=1, source_target_pairs={{0,1},{1,0},{2,3},{3,2},{4,5},{5,4},{6,7},{7,6},{8,9},{9,8},{10,11... | collective-permute-start | bytes 1179656 | tf_op jit(solution)/shard_map/ppermute | solution.py:503
  27.3 21.5 %collective-permute-start.6 = (f32[6,2,4,8,128]{4,3,2,1,0:T(8,128)S(1)}, f32[6,2,4,8,128]{4,3,2,1,0:T(8,128)S(1)}, u32[]{:S(2)}, u32[]{:S(2)}) collective-permute-start(f32[6,2,4,8,128]{4,3,2,1,0:T(8,128)S(1)} %get-tuple-element.36), channel_id=1, source_target_pairs={{0,32},{32,0},{64,96},{96,64},{1,33},{33,1},{65,97},{97,65},{2,34}... | collective-permute-start | bytes 589832 | tf_op jit(solution)/shard_map/ppermute | solution.py:503
  28.6 20.2 %collective-permute-start.7 = (f32[6,2,4,8,128]{4,3,2,1,0:T(8,128)S(1)}, f32[6,2,4,8,128]{4,3,2,1,0:T(8,128)S(1)}, u32[]{:S(2)}, u32[]{:S(2)}) collective-permute-start(f32[6,2,4,8,128]{4,3,2,1,0:T(8,128)S(1)} %get-tuple-element.37), channel_id=1, source_target_pairs={{32,64},{64,32},{33,65},{65,33},{34,66},{66,34},{35,67},{67,35},{3... | collective-permute-start | bytes 589832 | tf_op jit(solution)/shard_map/ppermute | solution.py:503
  32.0 16.8 %collective-permute-start.8 = (f32[6,2,32,128]{3,2,1,0:T(8,128)S(1)}, f32[6,2,32,128]{3,2,1,0:T(8,128)S(1)}, u32[]{:S(2)}, u32[]{:S(2)}) collective-permute-start(f32[6,2,32,128]{3,2,1,0:T(8,128)S(1)} %get-tuple-element.38), channel_id=1, source_target_pairs={{0,1},{1,0},{2,3},{3,2},{4,5},{5,4},{6,7},{7,6},{8,9},{9,8},{10,11... | collective-permute-start | bytes 589832 | tf_op jit(solution)/shard_map/ppermute | solution.py:503
  37.8 11.1 %collective-permute-start.9 = (f32[6,2,32,128]{3,2,1,0:T(8,128)S(1)}, f32[6,2,32,128]{3,2,1,0:T(8,128)S(1)}, u32[]{:S(2)}, u32[]{:S(2)}) collective-permute-start(f32[6,2,32,128]{3,2,1,0:T(8,128)S(1)} %get-tuple-element.39), channel_id=1, source_target_pairs={{1,2},{2,1},{3,4},{4,3},{5,6},{6,5},{7,8},{8,7},{9,10},{10,9},{11,... | collective-permute-start | bytes 589832 | tf_op jit(solution)/shard_map/ppermute | solution.py:503

commit v6 on v5

--- a/solution.py
+++ b/solution.py
@@ -220,8 +220,8 @@
     first, count, chunk, spread, q, *rest,
 ):
     (
-        out, token, result, carry_p, carry_n, carry_c, dx, dx_old, cx, cx_old, px, mx, nx, done, turned, sem_out,
-    ) = rest[-16:]
+        out, token, result, carry_p, carry_n, carry_c, dx, cx, px, mx, nx, done, turned, sem_out,
+    ) = rest[-14:]
     token[...] = jnp.zeros_like(token)
     lane = lax.broadcasted_iota(jnp.int32, (8, LANES), 1)
     sub = lax.broadcasted_iota(jnp.int32, (8, LANES), 0)
@@ -244,7 +244,7 @@
             for c in range(CAP)
         ]
 
-    def plane(i, _):
+    def late(i):
         for f in range(F):
             for j in (0, 2):
                 result[j, f, i], result[j + 1, f, i] = swap_32(turned[f, j], turned[f, j + 1], lane)
@@ -252,6 +252,7 @@
             for j in (0, 1):
                 turned[f, j], turned[f, j + 2] = swap_64(done[f, j], done[f, j + 2], lane)
 
+    def middle(i):
         here = [carry_c[j] for j in J]
         above = [conduction(q[5, i + 1, j]) for j in J]
         cond_z = [a + b for a, b in zip(here, above)]
@@ -295,27 +296,36 @@
                 t = total[j] + (net[j] - before[j])
                 before_x = jnp.where(lane == 0, edge_x[j] * twice[j], pltpu.roll(n, 1, 1))
                 done[f, j] = t + (n - before_x)
+    def early(i):
+        here, there = i & 1, (i + 1) & 1
         for j in J:
             u = q[0, i + 1, j]
-            weight = 0.0625 * ((u + u) + dx_old[0, j])
+            weight = 0.0625 * ((u + u) + dx[here, 0, j])
             from_left = (weight > 0.0) | (lane == 127)
-            cond = cx_old[j]
+            cond = cx[here, j]
             for f in range(F):
                 state = jnp.where(from_left, px[f, j], pltpu.roll(mx[f, j], 127, 1))
-                nx[f, j] = (scale[f] * cond) * dx_old[f, j] - weight * state
+                nx[f, j] = (scale[f] * cond) * dx[here, f, j] - weight * state
         for j in J:
-            cx_old[j] = cx[j]
             for f in range(F):
-                a, d = q[f, i + 2, j], dx[f, j]
+                a, d = q[f, i + 2, j], dx[there, f, j]
                 slope = minmod(pltpu.roll(d, 1, 1), d)
                 px[f, j], mx[f, j] = (a + a) + slope, (a + a) - slope
-                dx_old[f, j] = d
         for j in J:
             c = conduction(q[5, i + 3, j])
-            cx[j] = c + jnp.where(lane == 127, c, pltpu.roll(c, 127, 1))
+            cx[here, j] = c + jnp.where(lane == 127, c, pltpu.roll(c, 127, 1))
             for f in range(F):
                 a = q[f, i + 3, j]
-                dx[f, j] = jnp.where(lane == 127, 0.0, pltpu.roll(a, 127, 1) - a)
+                dx[here, f, j] = jnp.where(lane == 127, 0.0, pltpu.roll(a, 127, 1) - a)
+
+    def starting(i, _):
+        early(i)
+        return 0
+
+    def plane(i, _):
+        late(i)
+        middle(i)
+        early(i)
 
         @pl.when((i >= chunk + 4) & ((i - 4) % chunk == 0))
         def _():
@@ -324,7 +334,27 @@
 
         return 0
 
-    lax.fori_loop(0, count + LEAD, plane, 0)
+    def ending(i, _):
+        late(i)
+        return 0
+
+    for j in J:
+        carry_c[j] = conduction(q[5, 3, j])
+        cond = conduction(q[5, 2, j]) + carry_c[j]
+        weight = 0.0625 * (q[2, 2, j] + q[2, 3, j])
+        for f in range(F):
+            a, b, c, d = [q[f, k, j] for k in range(1, 5)]
+            across = c - b
+            left = (b + b) + minmod(b - a, across)
+            slope = minmod(across, d - c)
+            state = jnp.where(weight > 0.0, left, (c + c) - slope)
+            carry_p[f, j] = (c + c) + slope
+            carry_n[f, j] = (scale[f] * cond) * across - weight * state
+    lax.fori_loop(0, 3, starting, 0)
+    lax.fori_loop(3, count + 3, plane, 0)
+    lax.fori_loop(count + 3, count + LEAD, ending, 0)
+    for copy in leaving(count // chunk - 1):
+        copy.start()
     for k in range(count // chunk):
         for copy in leaving(k):
             copy.wait()
@@ -347,10 +377,8 @@
             planes(F, 4),
             planes(F, 4),
             planes(4),
-            planes(F, 4),
-            planes(F, 4),
-            planes(4),
-            planes(4),
+            planes(2, F, 4),
+            planes(2, 4),
             planes(F, 4),
             planes(F, 4),
             planes(F, 4),
@@ -519,7 +547,7 @@
     y_far = exchange(y_far, "gy", 1)
     z_pair = exchange(z_pair, "gx", 0)
     z_cross = exchange(z_cross, "gx", 1)
-    out, _ = step(LOW, B - LOW, 9, diffusivity, q_high, out)
+    out, _ = step(LOW, B - LOW, 6, diffusivity, q_high, out)
     out = ends(diffusivity, z_own, y_own, z_pair, z_cross, y_near, y_far, out)
     return out[..., 0, :].transpose(3, 0, 1, 2, 4).reshape(CAP, F, B * B * B)
 

time: 53.2 us -> 52.3 us (0.983)
  Pallas kernels: 29.9 us -> 28.2 us
  waiting for transfers between devices: 0.86 us -> 1.65 us
    pallas_call x2, Pallas kernels: 16.4 us -> 14.6 us  [step(): pl.pallas_call(functools.partial(step_body, first, count, chunk), name='s...]
    ppermute x10, waiting for transfers between devices: 0.86 us -> 1.65 us  [exchange(): return lax.ppermute(block, axes, pairs)]
  transfers between devices with their start and end apart: 10 -> 10, of which waited for: 1 -> 2; matrix products, arithmetic and copies ran while one was open for 0% -> 0% of each run, Pallas kernels for 41% -> 38%
where the time goes in v6:
time: 52.3 us; the launch traced here: 52.1 us
  Pallas kernels  28.2 us (54%)
  starting transfers between devices  21.5 us (41%)
  waiting for transfers between devices  1.65 us (3%)
  local copies, waits for them, and re-layouts  0.69 us (1%)
    ppermute x10, starting transfers between devices, exchange(): return lax.ppermute(block, axes, pairs)  21.5 us
    pallas_call x2, Pallas kernels, step(): pl.pallas_call(functools.partial(step_body, first, count, chunk), name='s...  14.6 us
    pallas_call x2, Pallas kernels, from_slots(): pl.pallas_call(body, name=name, out_shape=shapes, in_specs=[HBM] * len(ar...  6.23 us
    pallas_call x1, Pallas kernels, ends(): pl.pallas_call(ends_body, name='ends', out_shape=jax.ShapeDtypeStruct((F,...  4.17 us
    pallas_call x2, Pallas kernels, turn(): pl.pallas_call(body, name=name, out_shape=tuple((jax.ShapeDtypeStruct(sha...  3.13 us
    ppermute x10, waiting for transfers between devices, exchange(): return lax.ppermute(block, axes, pairs)  1.65 us
  transfers between devices with their start and end apart: 10, of which 2 were waited for; matrix products, arithmetic and copies ran while one was open for 0% of the time, Pallas kernels for 38%

profile of v6, /device:TPU:5, one launch (start us, length us, event | category | flops | bytes accessed | tf_op | source)
XLA Modules:
  0.0 52.1 jit_solution(10789315931582971310)
XLA Ops:
  0.0 2.2 %far.1 = (f32[2,6,16,8,128]{4,3,2,1,0:T(8,128)}, f32[8,128]{1,0:T(8,128)}) custom-call(f32[6,32,8,8,1,128]{5,4,3,2,1,0:T(1,128)} %bitcast.10), custom_call_target="tpu_custom_call" | custom-call | bytes 1000 | tf_op jit(solution)/shard_map/far/pallas_call | solution.py:65
  2.2 2.3 %collective-permute-start.5 = (f32[2,6,16,8,128]{4,3,2,1,0:T(8,128)}, f32[2,6,16,8,128]{4,3,2,1,0:T(8,128)S(1)}, u32[]{:S(2)}, u32[]{:S(2)}) collective-permute-start(f32[2,6,16,8,128]{4,3,2,1,0:T(8,128)} %get-tuple-element.32), channel_id=1, source_target_pairs={{1,2},{2,1},{3,4},{4,3},{5,6},{6,5},{7,8},{8,7},{9,10},{10,9},{11,... | collective-permute-start | bytes 2359304 | tf_op jit(solution)/shard_map/ppermute | solution.py:531
  4.5 0.7 %copy-done.3 = f32[8,128]{1,0:T(8,128)S(1)} copy-done((f32[8,128]{1,0:T(8,128)S(1)}, f32[8,128]{1,0:T(8,128)}, u32[]{:S(2)}) %copy-start.3) | copy-done | bytes 4120
  5.1 4.1 %near.1 = (f32[2,6,16,8,128]{4,3,2,1,0:T(8,128)S(1)}, f32[2,6,8,8,128]{4,3,2,1,0:T(8,128)S(1)}, f32[2,6,8,8,128]{4,3,2,1,0:T(8,128)S(1)}, f32[2,6,8,8,128]{4,3,2...) custom-call(f32[6,32,8,8,1,128]{5,4,3,2,1,0:T(1,128)S(1)} %bitcast.1, ...), custom_call_target="tpu_custom_call" | custom-call | bytes 1000 | tf_op jit(solution)/shard_map/near/pallas_call | solution.py:65
  9.2 0.0 copy-start.2
  9.2 4.5 %collective-permute-start.3 = (f32[2,6,8,8,128]{4,3,2,1,0:T(8,128)S(1)}, f32[2,6,8,8,128]{4,3,2,1,0:T(8,128)S(1)}, u32[]{:S(2)}, u32[]{:S(2)}) collective-permute-start(f32[2,6,8,8,128]{4,3,2,1,0:T(8,128)S(1)} %get-tuple-element.30), channel_id=1, source_target_pairs={{0,1},{1,0},{2,3},{3,2},{4,5},{5,4},{6,7},{7,6},{8,9},{9,8},{10,11... | collective-permute-start | bytes 1179656 | tf_op jit(solution)/shard_map/ppermute | solution.py:531
  13.7 1.7 %collective-permute-start.4 = (f32[2,6,8,8,128]{4,3,2,1,0:T(8,128)S(1)}, f32[2,6,8,8,128]{4,3,2,1,0:T(8,128)S(1)}, u32[]{:S(2)}, u32[]{:S(2)}) collective-permute-start(f32[2,6,8,8,128]{4,3,2,1,0:T(8,128)S(1)} %get-tuple-element.31), channel_id=1, source_target_pairs={{0,1},{1,0},{2,3},{3,2},{4,5},{5,4},{6,7},{7,6},{8,9},{9,8},{10,11... | collective-permute-start | bytes 1179656 | tf_op jit(solution)/shard_map/ppermute | solution.py:531
  15.4 0.0 collective-permute-start
  15.4 0.0 collective-permute-done.3.near_0
  15.4 0.5 collective-permute-start.1
  15.9 0.8 %collective-permute-done.4.near_1 = f32[2,6,8,8,128]{4,3,2,1,0:T(8,128)S(1)} collective-permute-done((f32[2,6,8,8,128]{4,3,2,1,0:T(8,128)S(1)}, f32[2,6,8,8,128]{4,3,2,1,0:T(8,128)S(1)}, u32[]{:S(2)}, u32[]{:S(2)}) %collective-permute-start.4) | collective-permute-done | bytes 393248 | tf_op jit(solution)/shard_map/ppermute | solution.py:531
  16.8 0.0 collective-permute-done.5.far
  16.8 1.3 %turn_low.1.q.q_low = f32[6,24,4,8,128]{4,3,2,1,0:T(8,128)S(1)} custom-call(s32[512]{0:T(512)S(1)} %copy-done.1, f32[4,6,16,8,128]{4,3,2,1,0:T(8,128)S(1)} %get-tuple-element.29.hold, f32[2,6,8,8,128]{4,3,2,1,0:T(8,128)S(1)} %collective-permute-done.3.near_0, f32[2,6,8,8,128]{4,3,2,1,0:T(8,128)S(1)} %collective-permute-done.4.near_1, ...), custom_call_target="tpu_custom_call" | custom-call | bytes 6000000 | tf_op jit(solution)/shard_map/turn_low/pallas_call | solution.py:183
  18.1 6.4 %step.2 = (f32[6,32,8,4,1,128]{5,4,3,2,1,0:T(1,128)}, f32[8,128]{1,0:T(8,128)S(1)}) custom-call(f32[6]{0:T(128)S(1)} %copy-done.2, f32[6,24,4,8,128]{4,3,2,1,0:T(8,128)S(1)} %turn_low.1.q.q_low), custom_call_target="tpu_custom_call" | custom-call | bytes 20000000 | tf_op jit(solution)/shard_map/step/pallas_call | solution.py:365
  24.6 0.0 collective-permute-done.1.near_1
  24.6 0.8 %collective-permute-done.2.far = f32[2,6,16,8,128]{4,3,2,1,0:T(8,128)S(1)} collective-permute-done((f32[2,6,16,8,128]{4,3,2,1,0:T(8,128)S(1)}, f32[2,6,16,8,128]{4,3,2,1,0:T(8,128)S(1)}, u32[]{:S(2)}, u32[]{:S(2)}) %collective-permute-start.2) | collective-permute-done | bytes 786464 | tf_op jit(solution)/shard_map/ppermute | solution.py:531
  25.4 1.8 %turn_high.1 = (f32[6,28,4,8,128]{4,3,2,1,0:T(8,128)S(1)}, f32[6,4,4,8,128]{4,3,2,1,0:T(8,128)S(1)}, f32[6,4,32,128]{3,2,1,0:T(8,128)S(1)}, f32[6,2,4,8,128]{4,3...) custom-call(s32[512]{0:T(512)S(1)} %copy-done.1, ...), custom_call_target="tpu_custom_call" | custom-call | bytes 6000000 | tf_op jit(solution)/shard_map/turn_high/pallas_call | solution.py:183
  27.2 1.3 %collective-permute-start.6 = (f32[6,2,4,8,128]{4,3,2,1,0:T(8,128)S(1)}, f32[6,2,4,8,128]{4,3,2,1,0:T(8,128)S(1)}, u32[]{:S(2)}, u32[]{:S(2)}) collective-permute-start(f32[6,2,4,8,128]{4,3,2,1,0:T(8,128)S(1)} %get-tuple-element.36), channel_id=1, source_target_pairs={{0,32},{32,0},{64,96},{96,64},{1,33},{33,1},{65,97},{97,65},{2,34}... | collective-permute-start | bytes 589832 | tf_op jit(solution)/shard_map/ppermute | solution.py:531
  28.5 3.4 %collective-permute-start.7 = (f32[6,2,4,8,128]{4,3,2,1,0:T(8,128)S(1)}, f32[6,2,4,8,128]{4,3,2,1,0:T(8,128)S(1)}, u32[]{:S(2)}, u32[]{:S(2)}) collective-permute-start(f32[6,2,4,8,128]{4,3,2,1,0:T(8,128)S(1)} %get-tuple-element.37), channel_id=1, source_target_pairs={{32,64},{64,32},{33,65},{65,33},{34,66},{66,34},{35,67},{67,35},{3... | collective-permute-start | bytes 589832 | tf_op jit(solution)/shard_map/ppermute | solution.py:531
  31.9 5.9 %collective-permute-start.8 = (f32[6,2,32,128]{3,2,1,0:T(8,128)S(1)}, f32[6,2,32,128]{3,2,1,0:T(8,128)S(1)}, u32[]{:S(2)}, u32[]{:S(2)}) collective-permute-start(f32[6,2,32,128]{3,2,1,0:T(8,128)S(1)} %get-tuple-element.38), channel_id=1, source_target_pairs={{0,1},{1,0},{2,3},{3,2},{4,5},{5,4},{6,7},{7,6},{8,9},{9,8},{10,11... | collective-permute-start | bytes 589832 | tf_op jit(solution)/shard_map/ppermute | solution.py:531
  37.8 1.9 %collective-permute-start.9 = (f32[6,2,32,128]{3,2,1,0:T(8,128)S(1)}, f32[6,2,32,128]{3,2,1,0:T(8,128)S(1)}, u32[]{:S(2)}, u32[]{:S(2)}) collective-permute-start(f32[6,2,32,128]{3,2,1,0:T(8,128)S(1)} %get-tuple-element.39), channel_id=1, source_target_pairs={{1,2},{2,1},{3,4},{4,3},{5,6},{6,5},{7,8},{8,7},{9,10},{10,9},{11,... | collective-permute-start | bytes 589832 | tf_op jit(solution)/shard_map/ppermute | solution.py:531
  39.7 8.2 %step.3 = (f32[6,32,8,4,1,128]{5,4,3,2,1,0:T(1,128)}, f32[8,128]{1,0:T(8,128)}) custom-call(f32[6]{0:T(128)S(1)} %copy-done.2, f32[6,28,4,8,128]{4,3,2,1,0:T(8,128)S(1)} %get-tuple-element.40.q, f32[6,32,8,4,1,128]{5,4,3,2,1,0:T(1,128)} %get-tuple-element.41.rest_0_), custom_call_target="tpu_custom_call", output_to_operand_aliasing={{0}: (2, {})} | custom-call | bytes 20000000 | tf_op jit(solution)/shard_map/step/pallas_call | solution.py:365
  47.9 0.0 collective-permute-done.7.z_cross
  47.9 4.2 %ends.1 = f32[6,32,8,4,1,128]{5,4,3,2,1,0:T(1,128)} custom-call(f32[6]{0:T(128)S(1)} %copy-done.2, f32[6,4,4,8,128]{4,3,2,1,0:T(8,128)S(1)} %get-tuple-element.34.z_own, f32[6,4,32,128]{3,2,1,0:T(8,128)S(1)} %get-tuple-element.35.y_own, f32[6,2,4,8,128]{4,3,2,1,0:T(8,128)S(1)} %collective-permute-done.6.z_pair, ...), custom_call_target="tpu_custom_call", output_to_operand_aliasing={{}: (7, {})} | custom-call | bytes 6000000 | tf_op jit(solution)/shard_map/ends/pallas_call | solution.py:502
  (11 shorter events, 0.0 us)
Async XLA Ops:
  0.0 4.5 %copy-start = (f32[8,6,32768]{2,0,1:T(8,128)S(1)}, f32[8,6,32768]{2,0,1:T(8,128)}, u32[]{:S(2)}) copy-start(f32[8,6,32768]{2,0,1:T(8,128)} %param.4) | copy-start | bytes 18874372
  2.2 14.6 %collective-permute-start.5 = (f32[2,6,16,8,128]{4,3,2,1,0:T(8,128)}, f32[2,6,16,8,128]{4,3,2,1,0:T(8,128)S(1)}, u32[]{:S(2)}, u32[]{:S(2)}) collective-permute-start(f32[2,6,16,8,128]{4,3,2,1,0:T(8,128)} %get-tuple-element.32), channel_id=1, source_target_pairs={{1,2},{2,1},{3,4},{4,3},{5,6},{6,5},{7,8},{8,7},{9,10},{10,9},{11,... | collective-permute-start | bytes 2359304 | tf_op jit(solution)/shard_map/ppermute | solution.py:531
  4.5 0.7 %copy-start.3 = (f32[8,128]{1,0:T(8,128)S(1)}, f32[8,128]{1,0:T(8,128)}, u32[]{:S(2)}) copy-start(f32[8,128]{1,0:T(8,128)} %get-tuple-element.24.after) | copy-start | bytes 12292
  5.1 11.6 %copy-start.1 = (s32[512]{0:T(512)S(1)}, s32[512]{0:T(512)}, u32[]{:S(2)}) copy-start(s32[512]{0:T(512)} %owner.3) | copy-start | bytes 6148
  9.2 8.9 %copy-start.2 = (f32[6]{0:T(128)S(1)}, f32[6]{0:T(128)}, u32[]{:S(2)}) copy-start(f32[6]{0:T(128)} %spread.5) | copy-start | bytes 76
  9.2 6.2 %collective-permute-start.3 = (f32[2,6,8,8,128]{4,3,2,1,0:T(8,128)S(1)}, f32[2,6,8,8,128]{4,3,2,1,0:T(8,128)S(1)}, u32[]{:S(2)}, u32[]{:S(2)}) collective-permute-start(f32[2,6,8,8,128]{4,3,2,1,0:T(8,128)S(1)} %get-tuple-element.30), channel_id=1, source_target_pairs={{0,1},{1,0},{2,3},{3,2},{4,5},{5,4},{6,7},{7,6},{8,9},{9,8},{10,11... | collective-permute-start | bytes 1179656 | tf_op jit(solution)/shard_map/ppermute | solution.py:531
  13.7 11.7 %collective-permute-start.2 = (f32[2,6,16,8,128]{4,3,2,1,0:T(8,128)S(1)}, f32[2,6,16,8,128]{4,3,2,1,0:T(8,128)S(1)}, u32[]{:S(2)}, u32[]{:S(2)}) collective-permute-start(f32[2,6,16,8,128]{4,3,2,1,0:T(8,128)S(1)} %get-tuple-element.28), channel_id=1, source_target_pairs={{1,2},{2,1},{3,4},{4,3},{5,6},{6,5},{7,8},{8,7},{9,10},{10,9},{11,... | collective-permute-start | bytes 2359304 | tf_op jit(solution)/shard_map/ppermute | solution.py:531
  13.7 3.1 %collective-permute-start.4 = (f32[2,6,8,8,128]{4,3,2,1,0:T(8,128)S(1)}, f32[2,6,8,8,128]{4,3,2,1,0:T(8,128)S(1)}, u32[]{:S(2)}, u32[]{:S(2)}) collective-permute-start(f32[2,6,8,8,128]{4,3,2,1,0:T(8,128)S(1)} %get-tuple-element.31), channel_id=1, source_target_pairs={{0,1},{1,0},{2,3},{3,2},{4,5},{5,4},{6,7},{7,6},{8,9},{9,8},{10,11... | collective-permute-start | bytes 1179656 | tf_op jit(solution)/shard_map/ppermute | solution.py:531
  15.4 9.2 %collective-permute-start = (f32[2,6,8,8,128]{4,3,2,1,0:T(8,128)S(1)}, f32[2,6,8,8,128]{4,3,2,1,0:T(8,128)S(1)}, u32[]{:S(2)}, u32[]{:S(2)}) collective-permute-start(f32[2,6,8,8,128]{4,3,2,1,0:T(8,128)S(1)} %get-tuple-element.26), channel_id=1, source_target_pairs={{0,1},{1,0},{2,3},{3,2},{4,5},{5,4},{6,7},{7,6},{8,9},{9,8},{10,11... | collective-permute-start | bytes 1179656 | tf_op jit(solution)/shard_map/ppermute | solution.py:531
  15.4 9.2 %collective-permute-start.1 = (f32[2,6,8,8,128]{4,3,2,1,0:T(8,128)S(1)}, f32[2,6,8,8,128]{4,3,2,1,0:T(8,128)S(1)}, u32[]{:S(2)}, u32[]{:S(2)}) collective-permute-start(f32[2,6,8,8,128]{4,3,2,1,0:T(8,128)S(1)} %get-tuple-element.27), channel_id=1, source_target_pairs={{0,1},{1,0},{2,3},{3,2},{4,5},{5,4},{6,7},{7,6},{8,9},{9,8},{10,11... | collective-permute-start | bytes 1179656 | tf_op jit(solution)/shard_map/ppermute | solution.py:531
  27.2 20.7 %collective-permute-start.6 = (f32[6,2,4,8,128]{4,3,2,1,0:T(8,128)S(1)}, f32[6,2,4,8,128]{4,3,2,1,0:T(8,128)S(1)}, u32[]{:S(2)}, u32[]{:S(2)}) collective-permute-start(f32[6,2,4,8,128]{4,3,2,1,0:T(8,128)S(1)} %get-tuple-element.36), channel_id=1, source_target_pairs={{0,32},{32,0},{64,96},{96,64},{1,33},{33,1},{65,97},{97,65},{2,34}... | collective-permute-start | bytes 589832 | tf_op jit(solution)/shard_map/ppermute | solution.py:531
  28.5 19.4 %collective-permute-start.7 = (f32[6,2,4,8,128]{4,3,2,1,0:T(8,128)S(1)}, f32[6,2,4,8,128]{4,3,2,1,0:T(8,128)S(1)}, u32[]{:S(2)}, u32[]{:S(2)}) collective-permute-start(f32[6,2,4,8,128]{4,3,2,1,0:T(8,128)S(1)} %get-tuple-element.37), channel_id=1, source_target_pairs={{32,64},{64,32},{33,65},{65,33},{34,66},{66,34},{35,67},{67,35},{3... | collective-permute-start | bytes 589832 | tf_op jit(solution)/shard_map/ppermute | solution.py:531
  31.9 16.0 %collective-permute-start.8 = (f32[6,2,32,128]{3,2,1,0:T(8,128)S(1)}, f32[6,2,32,128]{3,2,1,0:T(8,128)S(1)}, u32[]{:S(2)}, u32[]{:S(2)}) collective-permute-start(f32[6,2,32,128]{3,2,1,0:T(8,128)S(1)} %get-tuple-element.38), channel_id=1, source_target_pairs={{0,1},{1,0},{2,3},{3,2},{4,5},{5,4},{6,7},{7,6},{8,9},{9,8},{10,11... | collective-permute-start | bytes 589832 | tf_op jit(solution)/shard_map/ppermute | solution.py:531
  37.8 10.2 %collective-permute-start.9 = (f32[6,2,32,128]{3,2,1,0:T(8,128)S(1)}, f32[6,2,32,128]{3,2,1,0:T(8,128)S(1)}, u32[]{:S(2)}, u32[]{:S(2)}) collective-permute-start(f32[6,2,32,128]{3,2,1,0:T(8,128)S(1)} %get-tuple-element.39), channel_id=1, source_target_pairs={{1,2},{2,1},{3,4},{4,3},{5,6},{6,5},{7,8},{8,7},{9,10},{10,9},{11,... | collective-permute-start | bytes 589832 | tf_op jit(solution)/shard_map/ppermute | solution.py:531

commit v7 on v6

--- a/solution.py
+++ b/solution.py
@@ -10,8 +10,9 @@
 B = 32
 F = 6
 CAP = 4
-PARTS = 4
-HALF = 16
+HALF = 20
+LOW = HALF - 2
+PARTS = ((0, HALF // 2), (HALF // 2, HALF), (HALF, (HALF + B) // 2), ((HALF + B) // 2, B))
 ROWS = 8
 LANES = 128
 AXES = ("gx", "gy")
@@ -47,13 +48,13 @@
 
 
 def near_body(x, after, high, *rest):
-    nears, (hold_low, hold_high, sem) = rest[:PARTS], rest[PARTS:]
-    copies = leaving_copies(x, False, high, slice(HALF, B), sem.at[2 + PARTS])
+    nears, (hold_low, hold_high, sem) = rest[: len(PARTS)], rest[len(PARTS) :]
+    copies = leaving_copies(x, False, high, slice(HALF, B), sem.at[2 + len(PARTS)])
     for k, near in enumerate(nears):
-        copies += leaving_copies(x, True, near, slice(8 * k, 8 * k + 8), sem.at[2 + k])
+        copies += leaving_copies(x, True, near, slice(*PARTS[k]), sem.at[2 + k])
     for k, hold in enumerate((hold_low, hold_high)):
         for c in range(CAP):
-            planes = slice(HALF * k, HALF * k + HALF)
+            planes = slice(HALF, B) if k else slice(0, HALF)
             copies.append(
                 pltpu.make_async_copy(x.at[:, planes, :, 2 + c, 0], hold.at[c], sem.at[k, c])
             )
@@ -79,10 +80,10 @@
 
 
 def near_boxes(x, after):
-    part = (2, F, B // PARTS, ROWS, LANES)
-    half = (CAP, F, HALF, ROWS, LANES)
-    shapes = [(2, F, HALF, ROWS, LANES)] + [part] * PARTS + [half, half]
-    return from_slots(near_body, "near", [x, after], shapes, (3 + PARTS, CAP), 24 << 20)
+    boxes = lambda count, planes: (count, F, planes, ROWS, LANES)
+    shapes = [boxes(2, B - HALF)] + [boxes(2, end - start) for start, end in PARTS]
+    shapes += [boxes(CAP, HALF), boxes(CAP, B - HALF)]
+    return from_slots(near_body, "near", [x, after], shapes, (3 + len(PARTS), CAP), 24 << 20)
 
 
 def device_number():
@@ -117,14 +118,14 @@
     return *swap_32(a, b, lane), *swap_32(c, d, lane)
 
 
-def turn_half(kept, hold, nears, far, target, index, half):
+def turn_part(kept, count, hold, nears, far, target, index, half):
     lane = lax.broadcasted_iota(jnp.int32, (8, LANES), 1)
 
     def first_half(z):
-        near = nears[z // 8]
+        near = nears[z // (count // 2)]
         for f in range(F):
             v = [
-                arrived(kept[c], hold[c, f, z], c, far[c % 2, f, z], near[c % 2, f, z % 8])
+                arrived(kept[c], hold[c, f, z], c, far[c % 2, f, z], near[c % 2, f, z % (count // 2)])
                 for c in range(CAP)
             ]
             half[z % 8, f, 0], half[z % 8, f, 2] = swap_64(v[0], v[2], lane)
@@ -136,15 +137,15 @@
             target[f, index + z, 0], target[f, index + z, 1] = swap_32(a, b, lane)
             target[f, index + z, 2], target[f, index + z, 3] = swap_32(c, d, lane)
 
-    for z in range(HALF + 4):
-        if z < HALF:
+    for z in range(count + 4):
+        if z < count:
             first_half(z)
         if z >= 4:
             second_half(z - 4)
 
 
 def turn_low_body(owner, hold, near_0, near_1, far, q, half):
-    turn_half(kept_flags(owner), hold, (near_0, near_1), far, q, 3, half)
+    turn_part(kept_flags(owner), HALF, hold, (near_0, near_1), far, q, 3, half)
     for f in range(F):
         q[f, 0] = q[f, 3]
         q[f, 1] = q[f, 3]
@@ -154,14 +155,15 @@
 def turn_high_body(
     owner, hold, near_0, near_1, far, q_low, after, q, z_own, y_own, z_pair, z_cross, y_near, y_far, half
 ):
-    turn_half(kept_flags(owner), hold, (near_0, near_1), far, q, 5, half)
+    turn_part(kept_flags(owner), B - HALF, hold, (near_0, near_1), far, q, 5, half)
     odd_z, odd_y = odd("gx"), odd("gy")
     for f in range(F):
         for k in range(5):
-            q[f, k] = q_low[f, k + 14]
-        q[f, 21] = q[f, 20]
-        q[f, 22] = q[f, 20]
-        ends = [q_low[f, 3], q_low[f, 4], q[f, 19], q[f, 20]]
+            q[f, k] = q_low[f, k + LOW]
+        top = B + 2 - LOW
+        q[f, top + 1] = q[f, top]
+        q[f, top + 2] = q[f, top]
+        ends = [q_low[f, 3], q_low[f, 4], q[f, top - 1], q[f, top]]
         for k in range(4):
             z_own[f, k] = ends[k]
         for k in range(2):
@@ -169,7 +171,7 @@
             z_cross[f, k] = jnp.where(odd_z, ends[2 + k], ends[k])
         for b in range(4):
             span = slice(8 * b, 8 * b + 8)
-            source, z = (q_low, 8 * b + 3) if b < 2 else (q, 8 * b - 11)
+            source, z = (q_low, 8 * b + 3) if b < 2 else (q, 8 * b + 3 - LOW)
             ends = [source[f, z : z + 8, j, 0 if j < 2 else 7, :] for j in range(4)]
             for k in range(4):
                 y_own[f, k, span, :] = ends[k]
@@ -213,7 +215,6 @@
 
 LEAD = 5
 J = range(4)
-LOW = 14
 
 
 def step_body(
@@ -539,7 +540,7 @@
     far_high = exchange(far_high, AXES, 1, wrap=True)
     nears = [exchange(near, AXES, 0) for near in nears]
     q_low = turn_low(old_owner, hold_low, *nears[:2], far_low)
-    out, token = step(0, LOW, 7, diffusivity, q_low)
+    out, token = step(0, LOW, 9, diffusivity, q_low)
     q_high, z_own, y_own, z_pair, z_cross, y_near, y_far = turn_high(
         old_owner, token, hold_high, *nears[2:], far_high, q_low
     )
@@ -547,7 +548,7 @@
     y_far = exchange(y_far, "gy", 1)
     z_pair = exchange(z_pair, "gx", 0)
     z_cross = exchange(z_cross, "gx", 1)
-    out, _ = step(LOW, B - LOW, 6, diffusivity, q_high, out)
+    out, _ = step(LOW, B - LOW, 7, diffusivity, q_high, out)
     out = ends(diffusivity, z_own, y_own, z_pair, z_cross, y_near, y_far, out)
     return out[..., 0, :].transpose(3, 0, 1, 2, 4).reshape(CAP, F, B * B * B)
 

time: 52.3 us -> 51.7 us (0.989)
  the two profiles are of different devices: /device:TPU:5 before, /device:TPU:91 now
where the time goes in v7:
time: 51.7 us; the launch traced here: 51.5 us
  Pallas kernels  28.2 us (55%)
  starting transfers between devices  16.6 us (32%)
  waiting for transfers between devices  5.81 us (11%)
  local copies, waits for them, and re-layouts  0.69 us (1%)
    ppermute x10, starting transfers between devices, exchange(): return lax.ppermute(block, axes, pairs)  16.6 us
    pallas_call x2, Pallas kernels, step(): pl.pallas_call(functools.partial(step_body, first, count, chunk), name='s...  14.7 us
    pallas_call x2, Pallas kernels, from_slots(): pl.pallas_call(body, name=name, out_shape=shapes, in_specs=[HBM] * len(ar...  6.22 us
    ppermute x10, waiting for transfers between devices, exchange(): return lax.ppermute(block, axes, pairs)  5.81 us
    pallas_call x1, Pallas kernels, ends(): pl.pallas_call(ends_body, name='ends', out_shape=jax.ShapeDtypeStruct((F,...  4.17 us
    pallas_call x2, Pallas kernels, turn(): pl.pallas_call(body, name=name, out_shape=tuple((jax.ShapeDtypeStruct(sha...  3.08 us
  transfers between devices with their start and end apart: 10, of which 3 were waited for; matrix products, arithmetic and copies ran while one was open for 0% of the time, Pallas kernels for 39%

profile of v7, /device:TPU:91, one launch (start us, length us, event | category | flops | bytes accessed | tf_op | source)
XLA Modules:
  0.0 51.5 jit_solution(11691244295987643231)
XLA Ops:
  0.0 2.3 %far.1 = (f32[2,6,20,8,128]{4,3,2,1,0:T(8,128)}, f32[8,128]{1,0:T(8,128)}) custom-call(f32[6,32,8,8,1,128]{5,4,3,2,1,0:T(1,128)} %bitcast.10), custom_call_target="tpu_custom_call" | custom-call | bytes 1000 | tf_op jit(solution)/shard_map/far/pallas_call | solution.py:66
  2.3 2.0 %collective-permute-start.5 = (f32[2,6,20,8,128]{4,3,2,1,0:T(8,128)}, f32[2,6,20,8,128]{4,3,2,1,0:T(8,128)S(1)}, u32[]{:S(2)}, u32[]{:S(2)}) collective-permute-start(f32[2,6,20,8,128]{4,3,2,1,0:T(8,128)} %get-tuple-element.32), channel_id=1, source_target_pairs={{1,2},{2,1},{3,4},{4,3},{5,6},{6,5},{7,8},{8,7},{9,10},{10,9},{11,... | collective-permute-start | bytes 2949128 | tf_op jit(solution)/shard_map/ppermute | solution.py:532
  4.3 0.7 %copy-done.3 = f32[8,128]{1,0:T(8,128)S(1)} copy-done((f32[8,128]{1,0:T(8,128)S(1)}, f32[8,128]{1,0:T(8,128)}, u32[]{:S(2)}) %copy-start.3) | copy-done | bytes 4120
  5.0 3.9 %near.1 = (f32[2,6,12,8,128]{4,3,2,1,0:T(8,128)S(1)}, f32[2,6,10,8,128]{4,3,2,1,0:T(8,128)S(1)}, f32[2,6,10,8,128]{4,3,2,1,0:T(8,128)S(1)}, f32[2,6,6,8,128]{4,3...) custom-call(f32[6,32,8,8,1,128]{5,4,3,2,1,0:T(1,128)S(1)} %bitcast.1, ...), custom_call_target="tpu_custom_call" | custom-call | bytes 1000 | tf_op jit(solution)/shard_map/near/pallas_call | solution.py:66
  8.9 0.1 collective-permute-start.3
  9.0 1.1 %collective-permute-start.2 = (f32[2,6,12,8,128]{4,3,2,1,0:T(8,128)S(1)}, f32[2,6,12,8,128]{4,3,2,1,0:T(8,128)S(1)}, u32[]{:S(2)}, u32[]{:S(2)}) collective-permute-start(f32[2,6,12,8,128]{4,3,2,1,0:T(8,128)S(1)} %get-tuple-element.28), channel_id=1, source_target_pairs={{1,2},{2,1},{3,4},{4,3},{5,6},{6,5},{7,8},{8,7},{9,10},{10,9},{11,... | collective-permute-start | bytes 1769480 | tf_op jit(solution)/shard_map/ppermute | solution.py:532
  10.1 0.5 collective-permute-start
  10.6 0.2 collective-permute-done.3.near_0
  10.9 0.1 collective-permute-start.1
  11.0 1.0 %collective-permute-done.4.near_1 = f32[2,6,10,8,128]{4,3,2,1,0:T(8,128)S(1)} collective-permute-done((f32[2,6,10,8,128]{4,3,2,1,0:T(8,128)S(1)}, f32[2,6,10,8,128]{4,3,2,1,0:T(8,128)S(1)}, u32[]{:S(2)}, u32[]{:S(2)}) %collective-permute-start.4) | collective-permute-done | bytes 491552 | tf_op jit(solution)/shard_map/ppermute | solution.py:532
  12.0 4.6 %collective-permute-done.5.far = f32[2,6,20,8,128]{4,3,2,1,0:T(8,128)S(1)} collective-permute-done((f32[2,6,20,8,128]{4,3,2,1,0:T(8,128)}, f32[2,6,20,8,128]{4,3,2,1,0:T(8,128)S(1)}, u32[]{:S(2)}, u32[]{:S(2)}) %collective-permute-start.5) | collective-permute-done | bytes 983072 | tf_op jit(solution)/shard_map/ppermute | solution.py:532
  16.6 1.5 %turn_low.1.q.q_low = f32[6,28,4,8,128]{4,3,2,1,0:T(8,128)S(1)} custom-call(s32[512]{0:T(512)S(1)} %copy-done.1, f32[4,6,20,8,128]{4,3,2,1,0:T(8,128)S(1)} %get-tuple-element.29.hold, f32[2,6,10,8,128]{4,3,2,1,0:T(8,128)S(1)} %collective-permute-done.3.near_0, f32[2,6,10,8,128]{4,3,2,1,0:T(8,128)S(1)} %collective-permute-done.4.near_1, ...), custom_call_target="tpu_custom_call" | custom-call | bytes 6000000 | tf_op jit(solution)/shard_map/turn_low/pallas_call | solution.py:185
  18.1 7.7 %step.2 = (f32[6,32,8,4,1,128]{5,4,3,2,1,0:T(1,128)}, f32[8,128]{1,0:T(8,128)S(1)}) custom-call(f32[6]{0:T(128)S(1)} %copy-done.2, f32[6,28,4,8,128]{4,3,2,1,0:T(8,128)S(1)} %turn_low.1.q.q_low), custom_call_target="tpu_custom_call" | custom-call | bytes 20000000 | tf_op jit(solution)/shard_map/step/pallas_call | solution.py:366
  25.8 0.0 collective-permute-done.1.near_1
  25.8 0.0 collective-permute-done.2.far
  25.8 1.6 %turn_high.1 = (f32[6,24,4,8,128]{4,3,2,1,0:T(8,128)S(1)}, f32[6,4,4,8,128]{4,3,2,1,0:T(8,128)S(1)}, f32[6,4,32,128]{3,2,1,0:T(8,128)S(1)}, f32[6,2,4,8,128]{4,3...) custom-call(s32[512]{0:T(512)S(1)} %copy-done.1, ...), custom_call_target="tpu_custom_call" | custom-call | bytes 6000000 | tf_op jit(solution)/shard_map/turn_high/pallas_call | solution.py:185
  27.4 0.3 collective-permute-start.6
  27.7 3.8 %collective-permute-start.7 = (f32[6,2,4,8,128]{4,3,2,1,0:T(8,128)S(1)}, f32[6,2,4,8,128]{4,3,2,1,0:T(8,128)S(1)}, u32[]{:S(2)}, u32[]{:S(2)}) collective-permute-start(f32[6,2,4,8,128]{4,3,2,1,0:T(8,128)S(1)} %get-tuple-element.37), channel_id=1, source_target_pairs={{32,64},{64,32},{33,65},{65,33},{34,66},{66,34},{35,67},{67,35},{3... | collective-permute-start | bytes 589832 | tf_op jit(solution)/shard_map/ppermute | solution.py:532
  31.5 0.9 %collective-permute-start.8 = (f32[6,2,32,128]{3,2,1,0:T(8,128)S(1)}, f32[6,2,32,128]{3,2,1,0:T(8,128)S(1)}, u32[]{:S(2)}, u32[]{:S(2)}) collective-permute-start(f32[6,2,32,128]{3,2,1,0:T(8,128)S(1)} %get-tuple-element.38), channel_id=1, source_target_pairs={{0,1},{1,0},{2,3},{3,2},{4,5},{5,4},{6,7},{7,6},{8,9},{9,8},{10,11... | collective-permute-start | bytes 589832 | tf_op jit(solution)/shard_map/ppermute | solution.py:532
  32.4 7.8 %collective-permute-start.9 = (f32[6,2,32,128]{3,2,1,0:T(8,128)S(1)}, f32[6,2,32,128]{3,2,1,0:T(8,128)S(1)}, u32[]{:S(2)}, u32[]{:S(2)}) collective-permute-start(f32[6,2,32,128]{3,2,1,0:T(8,128)S(1)} %get-tuple-element.39), channel_id=1, source_target_pairs={{1,2},{2,1},{3,4},{4,3},{5,6},{6,5},{7,8},{8,7},{9,10},{10,9},{11,... | collective-permute-start | bytes 589832 | tf_op jit(solution)/shard_map/ppermute | solution.py:532
  40.2 7.0 %step.3 = (f32[6,32,8,4,1,128]{5,4,3,2,1,0:T(1,128)}, f32[8,128]{1,0:T(8,128)}) custom-call(f32[6]{0:T(128)S(1)} %copy-done.2, f32[6,24,4,8,128]{4,3,2,1,0:T(8,128)S(1)} %get-tuple-element.40.q, f32[6,32,8,4,1,128]{5,4,3,2,1,0:T(1,128)} %get-tuple-element.41.rest_0_), custom_call_target="tpu_custom_call", output_to_operand_aliasing={{0}: (2, {})} | custom-call | bytes 20000000 | tf_op jit(solution)/shard_map/step/pallas_call | solution.py:366
  47.2 0.0 collective-permute-done.6.z_pair
  47.3 0.0 collective-permute-done.7.z_cross
  47.3 4.2 %ends.1 = f32[6,32,8,4,1,128]{5,4,3,2,1,0:T(1,128)} custom-call(f32[6]{0:T(128)S(1)} %copy-done.2, f32[6,4,4,8,128]{4,3,2,1,0:T(8,128)S(1)} %get-tuple-element.34.z_own, f32[6,4,32,128]{3,2,1,0:T(8,128)S(1)} %get-tuple-element.35.y_own, f32[6,2,4,8,128]{4,3,2,1,0:T(8,128)S(1)} %collective-permute-done.6.z_pair, ...), custom_call_target="tpu_custom_call", output_to_operand_aliasing={{}: (7, {})} | custom-call | bytes 6000000 | tf_op jit(solution)/shard_map/ends/pallas_call | solution.py:503
  (11 shorter events, 0.0 us)
Async XLA Ops:
  0.0 4.3 %copy-start = (f32[8,6,32768]{2,0,1:T(8,128)S(1)}, f32[8,6,32768]{2,0,1:T(8,128)}, u32[]{:S(2)}) copy-start(f32[8,6,32768]{2,0,1:T(8,128)} %param.4) | copy-start | bytes 18874372
  2.3 14.3 %collective-permute-start.5 = (f32[2,6,20,8,128]{4,3,2,1,0:T(8,128)}, f32[2,6,20,8,128]{4,3,2,1,0:T(8,128)S(1)}, u32[]{:S(2)}, u32[]{:S(2)}) collective-permute-start(f32[2,6,20,8,128]{4,3,2,1,0:T(8,128)} %get-tuple-element.32), channel_id=1, source_target_pairs={{1,2},{2,1},{3,4},{4,3},{5,6},{6,5},{7,8},{8,7},{9,10},{10,9},{11,... | collective-permute-start | bytes 2949128 | tf_op jit(solution)/shard_map/ppermute | solution.py:532
  4.3 0.7 %copy-start.3 = (f32[8,128]{1,0:T(8,128)S(1)}, f32[8,128]{1,0:T(8,128)}, u32[]{:S(2)}) copy-start(f32[8,128]{1,0:T(8,128)} %get-tuple-element.24.after) | copy-start | bytes 12292
  5.0 11.6 %copy-start.1 = (s32[512]{0:T(512)S(1)}, s32[512]{0:T(512)}, u32[]{:S(2)}) copy-start(s32[512]{0:T(512)} %owner.3) | copy-start | bytes 6148
  8.9 1.9 %collective-permute-start.3 = (f32[2,6,10,8,128]{4,3,2,1,0:T(8,128)S(1)}, f32[2,6,10,8,128]{4,3,2,1,0:T(8,128)S(1)}, u32[]{:S(2)}, u32[]{:S(2)}) collective-permute-start(f32[2,6,10,8,128]{4,3,2,1,0:T(8,128)S(1)} %get-tuple-element.30), channel_id=1, source_target_pairs={{0,1},{1,0},{2,3},{3,2},{4,5},{5,4},{6,7},{7,6},{8,9},{9,8},{10,11... | collective-permute-start | bytes 1474568 | tf_op jit(solution)/shard_map/ppermute | solution.py:532
  9.0 16.8 %collective-permute-start.2 = (f32[2,6,12,8,128]{4,3,2,1,0:T(8,128)S(1)}, f32[2,6,12,8,128]{4,3,2,1,0:T(8,128)S(1)}, u32[]{:S(2)}, u32[]{:S(2)}) collective-permute-start(f32[2,6,12,8,128]{4,3,2,1,0:T(8,128)S(1)} %get-tuple-element.28), channel_id=1, source_target_pairs={{1,2},{2,1},{3,4},{4,3},{5,6},{6,5},{7,8},{8,7},{9,10},{10,9},{11,... | collective-permute-start | bytes 1769480 | tf_op jit(solution)/shard_map/ppermute | solution.py:532
  10.1 1.9 %collective-permute-start.4 = (f32[2,6,10,8,128]{4,3,2,1,0:T(8,128)S(1)}, f32[2,6,10,8,128]{4,3,2,1,0:T(8,128)S(1)}, u32[]{:S(2)}, u32[]{:S(2)}) collective-permute-start(f32[2,6,10,8,128]{4,3,2,1,0:T(8,128)S(1)} %get-tuple-element.31), channel_id=1, source_target_pairs={{0,1},{1,0},{2,3},{3,2},{4,5},{5,4},{6,7},{7,6},{8,9},{9,8},{10,11... | collective-permute-start | bytes 1474568 | tf_op jit(solution)/shard_map/ppermute | solution.py:532
  10.1 15.6 %collective-permute-start = (f32[2,6,6,8,128]{4,3,2,1,0:T(8,128)S(1)}, f32[2,6,6,8,128]{4,3,2,1,0:T(8,128)S(1)}, u32[]{:S(2)}, u32[]{:S(2)}) collective-permute-start(f32[2,6,6,8,128]{4,3,2,1,0:T(8,128)S(1)} %get-tuple-element.26), channel_id=1, source_target_pairs={{0,1},{1,0},{2,3},{3,2},{4,5},{5,4},{6,7},{7,6},{8,9},{9,8},{10,11... | collective-permute-start | bytes 884744 | tf_op jit(solution)/shard_map/ppermute | solution.py:532
  10.9 14.9 %collective-permute-start.1 = (f32[2,6,6,8,128]{4,3,2,1,0:T(8,128)S(1)}, f32[2,6,6,8,128]{4,3,2,1,0:T(8,128)S(1)}, u32[]{:S(2)}, u32[]{:S(2)}) collective-permute-start(f32[2,6,6,8,128]{4,3,2,1,0:T(8,128)S(1)} %get-tuple-element.27), channel_id=1, source_target_pairs={{0,1},{1,0},{2,3},{3,2},{4,5},{5,4},{6,7},{7,6},{8,9},{9,8},{10,11... | collective-permute-start | bytes 884744 | tf_op jit(solution)/shard_map/ppermute | solution.py:532
  16.6 1.5 %copy-start.2 = (f32[6]{0:T(128)S(1)}, f32[6]{0:T(128)}, u32[]{:S(2)}) copy-start(f32[6]{0:T(128)} %spread.5) | copy-start | bytes 76
  27.4 19.8 %collective-permute-start.6 = (f32[6,2,4,8,128]{4,3,2,1,0:T(8,128)S(1)}, f32[6,2,4,8,128]{4,3,2,1,0:T(8,128)S(1)}, u32[]{:S(2)}, u32[]{:S(2)}) collective-permute-start(f32[6,2,4,8,128]{4,3,2,1,0:T(8,128)S(1)} %get-tuple-element.36), channel_id=1, source_target_pairs={{0,32},{32,0},{64,96},{96,64},{1,33},{33,1},{65,97},{97,65},{2,34}... | collective-permute-start | bytes 589832 | tf_op jit(solution)/shard_map/ppermute | solution.py:532
  27.7 19.5 %collective-permute-start.7 = (f32[6,2,4,8,128]{4,3,2,1,0:T(8,128)S(1)}, f32[6,2,4,8,128]{4,3,2,1,0:T(8,128)S(1)}, u32[]{:S(2)}, u32[]{:S(2)}) collective-permute-start(f32[6,2,4,8,128]{4,3,2,1,0:T(8,128)S(1)} %get-tuple-element.37), channel_id=1, source_target_pairs={{32,64},{64,32},{33,65},{65,33},{34,66},{66,34},{35,67},{67,35},{3... | collective-permute-start | bytes 589832 | tf_op jit(solution)/shard_map/ppermute | solution.py:532
  31.5 15.7 %collective-permute-start.8 = (f32[6,2,32,128]{3,2,1,0:T(8,128)S(1)}, f32[6,2,32,128]{3,2,1,0:T(8,128)S(1)}, u32[]{:S(2)}, u32[]{:S(2)}) collective-permute-start(f32[6,2,32,128]{3,2,1,0:T(8,128)S(1)} %get-tuple-element.38), channel_id=1, source_target_pairs={{0,1},{1,0},{2,3},{3,2},{4,5},{5,4},{6,7},{7,6},{8,9},{9,8},{10,11... | collective-permute-start | bytes 589832 | tf_op jit(solution)/shard_map/ppermute | solution.py:532
  32.4 14.9 %collective-permute-start.9 = (f32[6,2,32,128]{3,2,1,0:T(8,128)S(1)}, f32[6,2,32,128]{3,2,1,0:T(8,128)S(1)}, u32[]{:S(2)}, u32[]{:S(2)}) collective-permute-start(f32[6,2,32,128]{3,2,1,0:T(8,128)S(1)} %get-tuple-element.39), channel_id=1, source_target_pairs={{1,2},{2,1},{3,4},{4,3},{5,6},{6,5},{7,8},{8,7},{9,10},{10,9},{11,... | collective-permute-start | bytes 589832 | tf_op jit(solution)/shard_map/ppermute | solution.py:532

commit v8 on v7

--- a/solution.py
+++ b/solution.py
@@ -423,7 +423,7 @@
 
 
 def ends_body(
-    spread, z_own, y_own, z_pair, z_cross, y_near, y_far, before, out,
+    spread, z_own, y_own, y_far, z_pair, z_cross, y_near, before, out,
     z_add, y_add, planes, first, last, sem, sem_in, sem_out,
 ):
     gx, gy = lax.axis_index("gx"), lax.axis_index("gy")
@@ -549,7 +549,7 @@
     z_pair = exchange(z_pair, "gx", 0)
     z_cross = exchange(z_cross, "gx", 1)
     out, _ = step(LOW, B - LOW, 7, diffusivity, q_high, out)
-    out = ends(diffusivity, z_own, y_own, z_pair, z_cross, y_near, y_far, out)
+    out = ends(diffusivity, z_own, y_own, y_far, z_pair, z_cross, y_near, out)
     return out[..., 0, :].transpose(3, 0, 1, 2, 4).reshape(CAP, F, B * B * B)
 
 

time: 51.7 us -> 51.5 us (level)
  the two profiles are of different devices: /device:TPU:91 before, /device:TPU:27 now
where the time goes in v8:
time: 51.5 us; the launch traced here: 51.3 us
  Pallas kernels  28.2 us (55%)
  starting transfers between devices  19.1 us (37%)
  waiting for transfers between devices  3.23 us (6%)
  local copies, waits for them, and re-layouts  0.69 us (1%)
    ppermute x10, starting transfers between devices, exchange(): return lax.ppermute(block, axes, pairs)  19.1 us
    pallas_call x2, Pallas kernels, step(): pl.pallas_call(functools.partial(step_body, first, count, chunk), name='s...  14.7 us
    pallas_call x2, Pallas kernels, from_slots(): pl.pallas_call(body, name=name, out_shape=shapes, in_specs=[HBM] * len(ar...  6.22 us
    pallas_call x1, Pallas kernels, ends(): pl.pallas_call(ends_body, name='ends', out_shape=jax.ShapeDtypeStruct((F,...  4.17 us
    ppermute x10, waiting for transfers between devices, exchange(): return lax.ppermute(block, axes, pairs)  3.23 us
    pallas_call x2, Pallas kernels, turn(): pl.pallas_call(body, name=name, out_shape=tuple((jax.ShapeDtypeStruct(sha...  3.07 us
  transfers between devices with their start and end apart: 10, of which 2 were waited for; matrix products, arithmetic and copies ran while one was open for 0% of the time, Pallas kernels for 39%

profile of v8, /device:TPU:27, one launch (start us, length us, event | category | flops | bytes accessed | tf_op | source)
XLA Modules:
  0.0 51.3 jit_solution(8585480627013045011)
XLA Ops:
  0.0 2.3 %far.1 = (f32[2,6,20,8,128]{4,3,2,1,0:T(8,128)}, f32[8,128]{1,0:T(8,128)}) custom-call(f32[6,32,8,8,1,128]{5,4,3,2,1,0:T(1,128)} %bitcast.10), custom_call_target="tpu_custom_call" | custom-call | bytes 1000 | tf_op jit(solution)/shard_map/far/pallas_call | solution.py:66
  2.3 2.3 %collective-permute-start.5 = (f32[2,6,20,8,128]{4,3,2,1,0:T(8,128)}, f32[2,6,20,8,128]{4,3,2,1,0:T(8,128)S(1)}, u32[]{:S(2)}, u32[]{:S(2)}) collective-permute-start(f32[2,6,20,8,128]{4,3,2,1,0:T(8,128)} %get-tuple-element.32), channel_id=1, source_target_pairs={{1,2},{2,1},{3,4},{4,3},{5,6},{6,5},{7,8},{8,7},{9,10},{10,9},{11,... | collective-permute-start | bytes 2949128 | tf_op jit(solution)/shard_map/ppermute | solution.py:532
  4.6 0.7 %copy-done.3 = f32[8,128]{1,0:T(8,128)S(1)} copy-done((f32[8,128]{1,0:T(8,128)S(1)}, f32[8,128]{1,0:T(8,128)}, u32[]{:S(2)}) %copy-start.3) | copy-done | bytes 4120
  5.3 3.9 %near.1 = (f32[2,6,12,8,128]{4,3,2,1,0:T(8,128)S(1)}, f32[2,6,10,8,128]{4,3,2,1,0:T(8,128)S(1)}, f32[2,6,10,8,128]{4,3,2,1,0:T(8,128)S(1)}, f32[2,6,6,8,128]{4,3...) custom-call(f32[6,32,8,8,1,128]{5,4,3,2,1,0:T(1,128)S(1)} %bitcast.1, ...), custom_call_target="tpu_custom_call" | custom-call | bytes 1000 | tf_op jit(solution)/shard_map/near/pallas_call | solution.py:66
  9.2 2.2 %collective-permute-start.3 = (f32[2,6,10,8,128]{4,3,2,1,0:T(8,128)S(1)}, f32[2,6,10,8,128]{4,3,2,1,0:T(8,128)S(1)}, u32[]{:S(2)}, u32[]{:S(2)}) collective-permute-start(f32[2,6,10,8,128]{4,3,2,1,0:T(8,128)S(1)} %get-tuple-element.30), channel_id=1, source_target_pairs={{0,1},{1,0},{2,3},{3,2},{4,5},{5,4},{6,7},{7,6},{8,9},{9,8},{10,11... | collective-permute-start | bytes 1474568 | tf_op jit(solution)/shard_map/ppermute | solution.py:532
  11.4 1.7 %collective-permute-start.4 = (f32[2,6,10,8,128]{4,3,2,1,0:T(8,128)S(1)}, f32[2,6,10,8,128]{4,3,2,1,0:T(8,128)S(1)}, u32[]{:S(2)}, u32[]{:S(2)}) collective-permute-start(f32[2,6,10,8,128]{4,3,2,1,0:T(8,128)S(1)} %get-tuple-element.31), channel_id=1, source_target_pairs={{0,1},{1,0},{2,3},{3,2},{4,5},{5,4},{6,7},{7,6},{8,9},{9,8},{10,11... | collective-permute-start | bytes 1474568 | tf_op jit(solution)/shard_map/ppermute | solution.py:532
  13.1 0.0 collective-permute-start
  13.1 0.0 collective-permute-done.3.near_0
  13.2 0.5 collective-permute-start.1
  13.7 1.0 %collective-permute-done.4.near_1 = f32[2,6,10,8,128]{4,3,2,1,0:T(8,128)S(1)} collective-permute-done((f32[2,6,10,8,128]{4,3,2,1,0:T(8,128)S(1)}, f32[2,6,10,8,128]{4,3,2,1,0:T(8,128)S(1)}, u32[]{:S(2)}, u32[]{:S(2)}) %collective-permute-start.4) | collective-permute-done | bytes 491552 | tf_op jit(solution)/shard_map/ppermute | solution.py:532
  14.6 2.2 %collective-permute-done.5.far = f32[2,6,20,8,128]{4,3,2,1,0:T(8,128)S(1)} collective-permute-done((f32[2,6,20,8,128]{4,3,2,1,0:T(8,128)}, f32[2,6,20,8,128]{4,3,2,1,0:T(8,128)S(1)}, u32[]{:S(2)}, u32[]{:S(2)}) %collective-permute-start.5) | collective-permute-done | bytes 983072 | tf_op jit(solution)/shard_map/ppermute | solution.py:532
  16.9 1.5 %turn_low.1.q.q_low = f32[6,28,4,8,128]{4,3,2,1,0:T(8,128)S(1)} custom-call(s32[512]{0:T(512)S(1)} %copy-done.1, f32[4,6,20,8,128]{4,3,2,1,0:T(8,128)S(1)} %get-tuple-element.29.hold, f32[2,6,10,8,128]{4,3,2,1,0:T(8,128)S(1)} %collective-permute-done.3.near_0, f32[2,6,10,8,128]{4,3,2,1,0:T(8,128)S(1)} %collective-permute-done.4.near_1, ...), custom_call_target="tpu_custom_call" | custom-call | bytes 6000000 | tf_op jit(solution)/shard_map/turn_low/pallas_call | solution.py:185
  18.4 7.7 %step.2 = (f32[6,32,8,4,1,128]{5,4,3,2,1,0:T(1,128)}, f32[8,128]{1,0:T(8,128)S(1)}) custom-call(f32[6]{0:T(128)S(1)} %copy-done.2, f32[6,28,4,8,128]{4,3,2,1,0:T(8,128)S(1)} %turn_low.1.q.q_low), custom_call_target="tpu_custom_call" | custom-call | bytes 20000000 | tf_op jit(solution)/shard_map/step/pallas_call | solution.py:366
  26.1 0.0 collective-permute-done.near_0
  26.1 0.0 collective-permute-done.1.near_1
  26.1 1.6 %turn_high.1 = (f32[6,24,4,8,128]{4,3,2,1,0:T(8,128)S(1)}, f32[6,4,4,8,128]{4,3,2,1,0:T(8,128)S(1)}, f32[6,4,32,128]{3,2,1,0:T(8,128)S(1)}, f32[6,2,4,8,128]{4,3...) custom-call(s32[512]{0:T(512)S(1)} %copy-done.1, ...), custom_call_target="tpu_custom_call" | custom-call | bytes 6000000 | tf_op jit(solution)/shard_map/turn_high/pallas_call | solution.py:185
  27.7 3.4 %collective-permute-start.6 = (f32[6,2,32,128]{3,2,1,0:T(8,128)S(1)}, f32[6,2,32,128]{3,2,1,0:T(8,128)S(1)}, u32[]{:S(2)}, u32[]{:S(2)}) collective-permute-start(f32[6,2,32,128]{3,2,1,0:T(8,128)S(1)} %get-tuple-element.36), channel_id=1, source_target_pairs={{1,2},{2,1},{3,4},{4,3},{5,6},{6,5},{7,8},{8,7},{9,10},{10,9},{11,... | collective-permute-start | bytes 589832 | tf_op jit(solution)/shard_map/ppermute | solution.py:532
  31.1 0.3 collective-permute-start.7
  31.4 3.8 %collective-permute-start.8 = (f32[6,2,4,8,128]{4,3,2,1,0:T(8,128)S(1)}, f32[6,2,4,8,128]{4,3,2,1,0:T(8,128)S(1)}, u32[]{:S(2)}, u32[]{:S(2)}) collective-permute-start(f32[6,2,4,8,128]{4,3,2,1,0:T(8,128)S(1)} %get-tuple-element.38), channel_id=1, source_target_pairs={{32,64},{64,32},{33,65},{65,33},{34,66},{66,34},{35,67},{67,35},{3... | collective-permute-start | bytes 589832 | tf_op jit(solution)/shard_map/ppermute | solution.py:532
  35.2 4.9 %collective-permute-start.9 = (f32[6,2,32,128]{3,2,1,0:T(8,128)S(1)}, f32[6,2,32,128]{3,2,1,0:T(8,128)S(1)}, u32[]{:S(2)}, u32[]{:S(2)}) collective-permute-start(f32[6,2,32,128]{3,2,1,0:T(8,128)S(1)} %get-tuple-element.39), channel_id=1, source_target_pairs={{0,1},{1,0},{2,3},{3,2},{4,5},{5,4},{6,7},{7,6},{8,9},{9,8},{10,11... | collective-permute-start | bytes 589832 | tf_op jit(solution)/shard_map/ppermute | solution.py:532
  40.1 7.0 %step.3 = (f32[6,32,8,4,1,128]{5,4,3,2,1,0:T(1,128)}, f32[8,128]{1,0:T(8,128)}) custom-call(f32[6]{0:T(128)S(1)} %copy-done.2, f32[6,24,4,8,128]{4,3,2,1,0:T(8,128)S(1)} %get-tuple-element.40.q, f32[6,32,8,4,1,128]{5,4,3,2,1,0:T(1,128)} %get-tuple-element.41.rest_0_), custom_call_target="tpu_custom_call", output_to_operand_aliasing={{0}: (2, {})} | custom-call | bytes 20000000 | tf_op jit(solution)/shard_map/step/pallas_call | solution.py:366
  47.1 0.0 collective-permute-done.7.z_pair
  47.1 0.0 collective-permute-done.8.z_cross
  47.1 4.2 %ends.1 = f32[6,32,8,4,1,128]{5,4,3,2,1,0:T(1,128)} custom-call(f32[6]{0:T(128)S(1)} %copy-done.2, f32[6,4,4,8,128]{4,3,2,1,0:T(8,128)S(1)} %get-tuple-element.34.z_own, f32[6,4,32,128]{3,2,1,0:T(8,128)S(1)} %get-tuple-element.35.y_own, f32[6,2,32,128]{3,2,1,0:T(8,128)S(1)} %collective-permute-done.6.y_far, ...), custom_call_target="tpu_custom_call", output_to_operand_aliasing={{}: (7, {})} | custom-call | bytes 6000000 | tf_op jit(solution)/shard_map/ends/pallas_call | solution.py:503
  (11 shorter events, 0.0 us)
Async XLA Ops:
  0.0 4.6 %copy-start = (f32[8,6,32768]{2,0,1:T(8,128)S(1)}, f32[8,6,32768]{2,0,1:T(8,128)}, u32[]{:S(2)}) copy-start(f32[8,6,32768]{2,0,1:T(8,128)} %param.4) | copy-start | bytes 18874372
  2.3 14.6 %collective-permute-start.5 = (f32[2,6,20,8,128]{4,3,2,1,0:T(8,128)}, f32[2,6,20,8,128]{4,3,2,1,0:T(8,128)S(1)}, u32[]{:S(2)}, u32[]{:S(2)}) collective-permute-start(f32[2,6,20,8,128]{4,3,2,1,0:T(8,128)} %get-tuple-element.32), channel_id=1, source_target_pairs={{1,2},{2,1},{3,4},{4,3},{5,6},{6,5},{7,8},{8,7},{9,10},{10,9},{11,... | collective-permute-start | bytes 2949128 | tf_op jit(solution)/shard_map/ppermute | solution.py:532
  4.6 0.7 %copy-start.3 = (f32[8,128]{1,0:T(8,128)S(1)}, f32[8,128]{1,0:T(8,128)}, u32[]{:S(2)}) copy-start(f32[8,128]{1,0:T(8,128)} %get-tuple-element.24.after) | copy-start | bytes 12292
  5.3 11.6 %copy-start.1 = (s32[512]{0:T(512)S(1)}, s32[512]{0:T(512)}, u32[]{:S(2)}) copy-start(s32[512]{0:T(512)} %owner.3) | copy-start | bytes 6148
  9.2 4.0 %collective-permute-start.3 = (f32[2,6,10,8,128]{4,3,2,1,0:T(8,128)S(1)}, f32[2,6,10,8,128]{4,3,2,1,0:T(8,128)S(1)}, u32[]{:S(2)}, u32[]{:S(2)}) collective-permute-start(f32[2,6,10,8,128]{4,3,2,1,0:T(8,128)S(1)} %get-tuple-element.30), channel_id=1, source_target_pairs={{0,1},{1,0},{2,3},{3,2},{4,5},{5,4},{6,7},{7,6},{8,9},{9,8},{10,11... | collective-permute-start | bytes 1474568 | tf_op jit(solution)/shard_map/ppermute | solution.py:532
  11.4 14.7 %collective-permute-start.2 = (f32[2,6,12,8,128]{4,3,2,1,0:T(8,128)S(1)}, f32[2,6,12,8,128]{4,3,2,1,0:T(8,128)S(1)}, u32[]{:S(2)}, u32[]{:S(2)}) collective-permute-start(f32[2,6,12,8,128]{4,3,2,1,0:T(8,128)S(1)} %get-tuple-element.28), channel_id=1, source_target_pairs={{1,2},{2,1},{3,4},{4,3},{5,6},{6,5},{7,8},{8,7},{9,10},{10,9},{11,... | collective-permute-start | bytes 1769480 | tf_op jit(solution)/shard_map/ppermute | solution.py:532
  11.4 3.2 %collective-permute-start.4 = (f32[2,6,10,8,128]{4,3,2,1,0:T(8,128)S(1)}, f32[2,6,10,8,128]{4,3,2,1,0:T(8,128)S(1)}, u32[]{:S(2)}, u32[]{:S(2)}) collective-permute-start(f32[2,6,10,8,128]{4,3,2,1,0:T(8,128)S(1)} %get-tuple-element.31), channel_id=1, source_target_pairs={{0,1},{1,0},{2,3},{3,2},{4,5},{5,4},{6,7},{7,6},{8,9},{9,8},{10,11... | collective-permute-start | bytes 1474568 | tf_op jit(solution)/shard_map/ppermute | solution.py:532
  13.1 12.9 %collective-permute-start = (f32[2,6,6,8,128]{4,3,2,1,0:T(8,128)S(1)}, f32[2,6,6,8,128]{4,3,2,1,0:T(8,128)S(1)}, u32[]{:S(2)}, u32[]{:S(2)}) collective-permute-start(f32[2,6,6,8,128]{4,3,2,1,0:T(8,128)S(1)} %get-tuple-element.26), channel_id=1, source_target_pairs={{0,1},{1,0},{2,3},{3,2},{4,5},{5,4},{6,7},{7,6},{8,9},{9,8},{10,11... | collective-permute-start | bytes 884744 | tf_op jit(solution)/shard_map/ppermute | solution.py:532
  13.2 12.9 %collective-permute-start.1 = (f32[2,6,6,8,128]{4,3,2,1,0:T(8,128)S(1)}, f32[2,6,6,8,128]{4,3,2,1,0:T(8,128)S(1)}, u32[]{:S(2)}, u32[]{:S(2)}) collective-permute-start(f32[2,6,6,8,128]{4,3,2,1,0:T(8,128)S(1)} %get-tuple-element.27), channel_id=1, source_target_pairs={{0,1},{1,0},{2,3},{3,2},{4,5},{5,4},{6,7},{7,6},{8,9},{9,8},{10,11... | collective-permute-start | bytes 884744 | tf_op jit(solution)/shard_map/ppermute | solution.py:532
  16.9 1.5 %copy-start.2 = (f32[6]{0:T(128)S(1)}, f32[6]{0:T(128)}, u32[]{:S(2)}) copy-start(f32[6]{0:T(128)} %spread.5) | copy-start | bytes 76
  27.7 19.4 %collective-permute-start.6 = (f32[6,2,32,128]{3,2,1,0:T(8,128)S(1)}, f32[6,2,32,128]{3,2,1,0:T(8,128)S(1)}, u32[]{:S(2)}, u32[]{:S(2)}) collective-permute-start(f32[6,2,32,128]{3,2,1,0:T(8,128)S(1)} %get-tuple-element.36), channel_id=1, source_target_pairs={{1,2},{2,1},{3,4},{4,3},{5,6},{6,5},{7,8},{8,7},{9,10},{10,9},{11,... | collective-permute-start | bytes 589832 | tf_op jit(solution)/shard_map/ppermute | solution.py:532
  31.1 16.0 %collective-permute-start.7 = (f32[6,2,4,8,128]{4,3,2,1,0:T(8,128)S(1)}, f32[6,2,4,8,128]{4,3,2,1,0:T(8,128)S(1)}, u32[]{:S(2)}, u32[]{:S(2)}) collective-permute-start(f32[6,2,4,8,128]{4,3,2,1,0:T(8,128)S(1)} %get-tuple-element.37), channel_id=1, source_target_pairs={{0,32},{32,0},{64,96},{96,64},{1,33},{33,1},{65,97},{97,65},{2,34}... | collective-permute-start | bytes 589832 | tf_op jit(solution)/shard_map/ppermute | solution.py:532
  31.4 15.7 %collective-permute-start.8 = (f32[6,2,4,8,128]{4,3,2,1,0:T(8,128)S(1)}, f32[6,2,4,8,128]{4,3,2,1,0:T(8,128)S(1)}, u32[]{:S(2)}, u32[]{:S(2)}) collective-permute-start(f32[6,2,4,8,128]{4,3,2,1,0:T(8,128)S(1)} %get-tuple-element.38), channel_id=1, source_target_pairs={{32,64},{64,32},{33,65},{65,33},{34,66},{66,34},{35,67},{67,35},{3... | collective-permute-start | bytes 589832 | tf_op jit(solution)/shard_map/ppermute | solution.py:532
  35.2 11.9 %collective-permute-start.9 = (f32[6,2,32,128]{3,2,1,0:T(8,128)S(1)}, f32[6,2,32,128]{3,2,1,0:T(8,128)S(1)}, u32[]{:S(2)}, u32[]{:S(2)}) collective-permute-start(f32[6,2,32,128]{3,2,1,0:T(8,128)S(1)} %get-tuple-element.39), channel_id=1, source_target_pairs={{0,1},{1,0},{2,3},{3,2},{4,5},{5,4},{6,7},{7,6},{8,9},{9,8},{10,11... | collective-permute-start | bytes 589832 | tf_op jit(solution)/shard_map/ppermute | solution.py:532

commit v9 on v8

--- a/solution.py
+++ b/solution.py
@@ -10,7 +10,7 @@
 B = 32
 F = 6
 CAP = 4
-HALF = 20
+HALF = 18
 LOW = HALF - 2
 PARTS = ((0, HALF // 2), (HALF // 2, HALF), (HALF, (HALF + B) // 2), ((HALF + B) // 2, B))
 ROWS = 8
@@ -221,8 +221,8 @@
     first, count, chunk, spread, q, *rest,
 ):
     (
-        out, token, result, carry_p, carry_n, carry_c, dx, cx, px, mx, nx, done, turned, sem_out,
-    ) = rest[-14:]
+        out, token, firsts, lasts, ends, result, carry_p, carry_n, carry_c, dx, cx, px, mx, nx, done, turned, sem_out,
+    ) = rest[-17:]
     token[...] = jnp.zeros_like(token)
     lane = lax.broadcasted_iota(jnp.int32, (8, LANES), 1)
     sub = lax.broadcasted_iota(jnp.int32, (8, LANES), 0)
@@ -356,6 +356,14 @@
     lax.fori_loop(count + 3, count + LEAD, ending, 0)
     for copy in leaving(count // chunk - 1):
         copy.start()
+    for c in range(CAP):
+        for f in range(F):
+            for z in range(0, count, 8):
+                span = slice(LEAD + z, LEAD + z + 8)
+                firsts[c, f, z : z + 8, :] = result[c, f, span, 0, :]
+                lasts[c, f, z : z + 8, :] = result[c, f, span, 7, :]
+            for k in range(2):
+                ends[c, f, k] = result[c, f, LEAD + k + (count - 2 if first else 0)]
     for k in range(count // chunk):
         for copy in leaving(k):
             copy.wait()
@@ -369,9 +377,12 @@
         out_shape=(
             jax.ShapeDtypeStruct((F, B, ROWS, CAP, 1, LANES), F32),
             jax.ShapeDtypeStruct((ROWS, LANES), F32),
+            jax.ShapeDtypeStruct((CAP, F, count, LANES), F32),
+            jax.ShapeDtypeStruct((CAP, F, count, LANES), F32),
+            jax.ShapeDtypeStruct((CAP, F, 2, ROWS, LANES), F32),
         ),
         in_specs=[SMEM, VMEM] + ([] if out is None else [HBM]),
-        out_specs=(HBM, VMEM),
+        out_specs=(HBM,) + (VMEM,) * 4,
         input_output_aliases={} if out is None else {2: 0},
         scratch_shapes=[
             planes(CAP, F, count + LEAD),
@@ -423,8 +434,9 @@
 
 
 def ends_body(
-    spread, z_own, y_own, y_far, z_pair, z_cross, y_near, before, out,
-    z_add, y_add, planes, first, last, sem, sem_in, sem_out,
+    spread, z_own, y_own, y_far, z_pair, z_cross, y_near,
+    first_low, last_low, ends_low, first_high, last_high, ends_high, before, out,
+    z_add, y_add, planes, first, last, sem_out,
 ):
     gx, gy = lax.axis_index("gx"), lax.axis_index("gy")
     odd_z, odd_y = odd("gx"), odd("gy")
@@ -432,25 +444,14 @@
     sub = lax.broadcasted_iota(jnp.int32, (8, LANES), 0)
     scale = [0.5 * spread[f] for f in range(F)]
 
-    def moves(inward):
-        rows, whole = [], []
-        for c in range(CAP):
-            parts = [
-                (out.at[:, :, 0, c, 0], first.at[c], rows),
-                (out.at[:, :, 7, c, 0], last.at[c], rows),
-                (out.at[:, 0:2, :, c, 0], planes.at[c, :, 0:2], whole),
-                (out.at[:, 30:32, :, c, 0], planes.at[c, :, 2:4], whole),
-            ]
-            for k, (there, here, kind) in enumerate(parts):
-                source, target = (there, here) if inward else (here, there)
-                kind.append(
-                    pltpu.make_async_copy(source, target, (sem_in if inward else sem_out).at[c, k])
-                )
-        return rows, whole
-
-    rows, whole = moves(True)
-    for copy in rows + whole:
-        copy.start()
+    rows_out, whole_out = [], []
+    for c in range(CAP):
+        rows_out.append(pltpu.make_async_copy(first.at[c], out.at[:, :, 0, c, 0], sem_out.at[c, 0]))
+        rows_out.append(pltpu.make_async_copy(last.at[c], out.at[:, :, 7, c, 0], sem_out.at[c, 1]))
+        for k, z in enumerate((0, 30)):
+            there = out.at[:, z : z + 2, :, c, 0]
+            here = planes.at[c, :, 2 * k : 2 * k + 2]
+            whole_out.append(pltpu.make_async_copy(here, there, sem_out.at[c, 2 + k]))
 
     for j in range(4):
         changes = both_ends(
@@ -474,16 +475,16 @@
             for c, value in enumerate(turned_to_layers(changes[f], lane)):
                 y_add[c, f, span, :] = value
 
-    for copy in rows + whole:
-        copy.wait()
-    rows_out, whole_out = moves(False)
     for c in range(CAP):
         for f in range(F):
             for b in range(4):
                 span = slice(8 * b, 8 * b + 8)
                 value = y_add[c, f, span, :]
-                first[c, f, span, :] += jnp.where(lane < 64, value, 0.0)
-                last[c, f, span, :] += jnp.where(lane >= 64, value, 0.0)
+                part = slice(8 * (b % 2), 8 * (b % 2) + 8)
+                low = (first_low if b < 2 else first_high)[c, f, part, :]
+                high = (last_low if b < 2 else last_high)[c, f, part, :]
+                first[c, f, span, :] = low + jnp.where(lane < 64, value, 0.0)
+                last[c, f, span, :] = high + jnp.where(lane >= 64, value, 0.0)
         rows_out[2 * c].start()
         rows_out[2 * c + 1].start()
     corner = ((sub == 0) & (lane < 64)) | ((sub == 7) & (lane >= 64))
@@ -491,7 +492,9 @@
         for k, z in enumerate((0, 1, 30, 31)):
             values = turned_to_layers([z_add[f, k, j] for j in range(4)], lane)
             for c in range(CAP):
-                planes[c, f, k] += values[c] + jnp.where(corner, y_add[c, f, z : z + 1, :], 0.0)
+                plane = (ends_low if k < 2 else ends_high)[c, f, k % 2]
+                add = values[c] + jnp.where(corner, y_add[c, f, z : z + 1, :], 0.0)
+                planes[c, f, k] = plane + add
     for copy in rows_out:
         copy.wait()
     run_all(whole_out)
@@ -513,8 +516,6 @@
             planes,
             rows,
             rows,
-            pltpu.SemaphoreType.DMA((1,)),
-            pltpu.SemaphoreType.DMA((CAP, 4)),
             pltpu.SemaphoreType.DMA((CAP, 4)),
         ],
         compiler_params=pltpu.CompilerParams(vmem_limit_bytes=24 << 20),
@@ -540,7 +541,7 @@
     far_high = exchange(far_high, AXES, 1, wrap=True)
     nears = [exchange(near, AXES, 0) for near in nears]
     q_low = turn_low(old_owner, hold_low, *nears[:2], far_low)
-    out, token = step(0, LOW, 9, diffusivity, q_low)
+    out, token, *low_ends = step(0, LOW, 8, diffusivity, q_low)
     q_high, z_own, y_own, z_pair, z_cross, y_near, y_far = turn_high(
         old_owner, token, hold_high, *nears[2:], far_high, q_low
     )
@@ -548,8 +549,10 @@
     y_far = exchange(y_far, "gy", 1)
     z_pair = exchange(z_pair, "gx", 0)
     z_cross = exchange(z_cross, "gx", 1)
-    out, _ = step(LOW, B - LOW, 7, diffusivity, q_high, out)
-    out = ends(diffusivity, z_own, y_own, y_far, z_pair, z_cross, y_near, out)
+    out, _, *high_ends = step(LOW, B - LOW, 8, diffusivity, q_high, out)
+    out = ends(
+        diffusivity, z_own, y_own, y_far, z_pair, z_cross, y_near, *low_ends, *high_ends, out
+    )
     return out[..., 0, :].transpose(3, 0, 1, 2, 4).reshape(CAP, F, B * B * B)
 
 

time: 51.5 us -> 50 us (0.971)
  waiting for transfers between devices: 3.23 us -> 2.1 us
    ppermute x10, waiting for transfers between devices: 3.23 us -> 2.1 us  [exchange(): return lax.ppermute(block, axes, pairs)]
  transfers between devices with their start and end apart: 10 -> 10, of which waited for: 2 -> 2; matrix products, arithmetic and copies ran while one was open for 0% -> 0% of each run, Pallas kernels for 39% -> 40%
where the time goes in v9:
time: 50 us; the launch traced here: 49.8 us
  Pallas kernels  27.8 us (56%)
  starting transfers between devices  19.1 us (38%)
  waiting for transfers between devices  2.1 us (4%)
  local copies, waits for them, and re-layouts  0.69 us (1%)
    ppermute x10, starting transfers between devices, exchange(): return lax.ppermute(block, axes, pairs)  19.1 us
    pallas_call x2, Pallas kernels, step(): pl.pallas_call(functools.partial(step_body, first, count, chunk), name='s...  14.7 us
    pallas_call x2, Pallas kernels, from_slots(): pl.pallas_call(body, name=name, out_shape=shapes, in_specs=[HBM] * len(ar...  6.22 us
    pallas_call x1, Pallas kernels, ends(): pl.pallas_call(ends_body, name='ends', out_shape=jax.ShapeDtypeStruct((F,...  3.91 us
    pallas_call x2, Pallas kernels, turn(): pl.pallas_call(body, name=name, out_shape=tuple((jax.ShapeDtypeStruct(sha...  2.99 us
    ppermute x10, waiting for transfers between devices, exchange(): return lax.ppermute(block, axes, pairs)  2.1 us
  transfers between devices with their start and end apart: 10, of which 2 were waited for; matrix products, arithmetic and copies ran while one was open for 0% of the time, Pallas kernels for 40%

profile of v9, /device:TPU:27, one launch (start us, length us, event | category | flops | bytes accessed | tf_op | source)
XLA Modules:
  0.0 49.8 jit_solution(2013434868842723896)
XLA Ops:
  0.0 2.2 %far.1 = (f32[2,6,18,8,128]{4,3,2,1,0:T(8,128)}, f32[8,128]{1,0:T(8,128)}) custom-call(f32[6,32,8,8,1,128]{5,4,3,2,1,0:T(1,128)} %bitcast.10), custom_call_target="tpu_custom_call" | custom-call | bytes 1000 | tf_op jit(solution)/shard_map/far/pallas_call | solution.py:66
  2.2 2.3 %collective-permute-start.5 = (f32[2,6,18,8,128]{4,3,2,1,0:T(8,128)}, f32[2,6,18,8,128]{4,3,2,1,0:T(8,128)S(1)}, u32[]{:S(2)}, u32[]{:S(2)}) collective-permute-start(f32[2,6,18,8,128]{4,3,2,1,0:T(8,128)} %get-tuple-element.38), channel_id=1, source_target_pairs={{1,2},{2,1},{3,4},{4,3},{5,6},{6,5},{7,8},{8,7},{9,10},{10,9},{11,... | collective-permute-start | bytes 2654216 | tf_op jit(solution)/shard_map/ppermute | solution.py:533
  4.5 0.7 %copy-done.3 = f32[8,128]{1,0:T(8,128)S(1)} copy-done((f32[8,128]{1,0:T(8,128)S(1)}, f32[8,128]{1,0:T(8,128)}, u32[]{:S(2)}) %copy-start.3) | copy-done | bytes 4120
  5.2 4.0 %near.1 = (f32[2,6,14,8,128]{4,3,2,1,0:T(8,128)S(1)}, f32[2,6,9,8,128]{4,3,2,1,0:T(8,128)S(1)}, f32[2,6,9,8,128]{4,3,2,1,0:T(8,128)S(1)}, f32[2,6,7,8,128]{4,3,2...) custom-call(f32[6,32,8,8,1,128]{5,4,3,2,1,0:T(1,128)S(1)} %bitcast.1, ...), custom_call_target="tpu_custom_call" | custom-call | bytes 1000 | tf_op jit(solution)/shard_map/near/pallas_call | solution.py:66
  9.2 0.0 copy-start.2
  9.2 2.2 %collective-permute-start.3 = (f32[2,6,9,8,128]{4,3,2,1,0:T(8,128)S(1)}, f32[2,6,9,8,128]{4,3,2,1,0:T(8,128)S(1)}, u32[]{:S(2)}, u32[]{:S(2)}) collective-permute-start(f32[2,6,9,8,128]{4,3,2,1,0:T(8,128)S(1)} %get-tuple-element.36), channel_id=1, source_target_pairs={{0,1},{1,0},{2,3},{3,2},{4,5},{5,4},{6,7},{7,6},{8,9},{9,8},{10,11... | collective-permute-start | bytes 1327112 | tf_op jit(solution)/shard_map/ppermute | solution.py:533
  11.4 0.0 collective-permute-start.2
  11.4 1.7 %collective-permute-start.4 = (f32[2,6,9,8,128]{4,3,2,1,0:T(8,128)S(1)}, f32[2,6,9,8,128]{4,3,2,1,0:T(8,128)S(1)}, u32[]{:S(2)}, u32[]{:S(2)}) collective-permute-start(f32[2,6,9,8,128]{4,3,2,1,0:T(8,128)S(1)} %get-tuple-element.37), channel_id=1, source_target_pairs={{0,1},{1,0},{2,3},{3,2},{4,5},{5,4},{6,7},{7,6},{8,9},{9,8},{10,11... | collective-permute-start | bytes 1327112 | tf_op jit(solution)/shard_map/ppermute | solution.py:533
  13.2 0.0 collective-permute-start
  13.2 0.0 collective-permute-done.3.near_0
  13.2 0.5 %collective-permute-start.1 = (f32[2,6,7,8,128]{4,3,2,1,0:T(8,128)S(1)}, f32[2,6,7,8,128]{4,3,2,1,0:T(8,128)S(1)}, u32[]{:S(2)}, u32[]{:S(2)}) collective-permute-start(f32[2,6,7,8,128]{4,3,2,1,0:T(8,128)S(1)} %get-tuple-element.33), channel_id=1, source_target_pairs={{0,1},{1,0},{2,3},{3,2},{4,5},{5,4},{6,7},{7,6},{8,9},{9,8},{10,11... | collective-permute-start | bytes 1032200 | tf_op jit(solution)/shard_map/ppermute | solution.py:533
  13.7 0.9 %collective-permute-done.4.near_1 = f32[2,6,9,8,128]{4,3,2,1,0:T(8,128)S(1)} collective-permute-done((f32[2,6,9,8,128]{4,3,2,1,0:T(8,128)S(1)}, f32[2,6,9,8,128]{4,3,2,1,0:T(8,128)S(1)}, u32[]{:S(2)}, u32[]{:S(2)}) %collective-permute-start.4) | collective-permute-done | bytes 442400 | tf_op jit(solution)/shard_map/ppermute | solution.py:533
  14.6 1.2 %collective-permute-done.5.far = f32[2,6,18,8,128]{4,3,2,1,0:T(8,128)S(1)} collective-permute-done((f32[2,6,18,8,128]{4,3,2,1,0:T(8,128)}, f32[2,6,18,8,128]{4,3,2,1,0:T(8,128)S(1)}, u32[]{:S(2)}, u32[]{:S(2)}) %collective-permute-start.5) | collective-permute-done | bytes 884768 | tf_op jit(solution)/shard_map/ppermute | solution.py:533
  15.8 1.4 %turn_low.1.q.q_low = f32[6,26,4,8,128]{4,3,2,1,0:T(8,128)S(1)} custom-call(s32[512]{0:T(512)S(1)} %copy-done.1, f32[4,6,18,8,128]{4,3,2,1,0:T(8,128)S(1)} %get-tuple-element.35.hold, f32[2,6,9,8,128]{4,3,2,1,0:T(8,128)S(1)} %collective-permute-done.3.near_0, f32[2,6,9,8,128]{4,3,2,1,0:T(8,128)S(1)} %collective-permute-done.4.near_1, ...), custom_call_target="tpu_custom_call" | custom-call | bytes 6000000 | tf_op jit(solution)/shard_map/turn_low/pallas_call | solution.py:185
  17.1 7.0 %step.2 = (f32[6,32,8,4,1,128]{5,4,3,2,1,0:T(1,128)}, f32[8,128]{1,0:T(8,128)S(1)}, f32[4,6,16,128]{3,2,1,0:T(8,128)S(1)}, f32[4,6,16,128]{3,2,1,0:T(8,128)S(1)}, f32[4,6,2,8,128]{4,3,2,1,0:T(8,128)S(1)}) custom-call(f32[6]{0:T(128)S(1)} %copy-done.2, f32[6,26,4,8,128]{4,3,2,1,0:T(8,128)S(1)} %turn_low.1.q.q_low), custom_call_target="tpu_custom_call" | custom-call | bytes 20000000 | tf_op jit(solution)/shard_map/step/pallas_call | solution.py:374
  24.2 0.0 collective-permute-done.1.near_1
  24.2 0.0 collective-permute-done.2.far
  24.2 1.6 %turn_high.1 = (f32[6,26,4,8,128]{4,3,2,1,0:T(8,128)S(1)}, f32[6,4,4,8,128]{4,3,2,1,0:T(8,128)S(1)}, f32[6,4,32,128]{3,2,1,0:T(8,128)S(1)}, f32[6,2,4,8,128]{4,3...) custom-call(s32[512]{0:T(512)S(1)} %copy-done.1, ...), custom_call_target="tpu_custom_call" | custom-call | bytes 6000000 | tf_op jit(solution)/shard_map/turn_high/pallas_call | solution.py:185
  25.9 3.4 %collective-permute-start.6 = (f32[6,2,32,128]{3,2,1,0:T(8,128)S(1)}, f32[6,2,32,128]{3,2,1,0:T(8,128)S(1)}, u32[]{:S(2)}, u32[]{:S(2)}) collective-permute-start(f32[6,2,32,128]{3,2,1,0:T(8,128)S(1)} %get-tuple-element.42), channel_id=1, source_target_pairs={{1,2},{2,1},{3,4},{4,3},{5,6},{6,5},{7,8},{8,7},{9,10},{10,9},{11,... | collective-permute-start | bytes 589832 | tf_op jit(solution)/shard_map/ppermute | solution.py:533
  29.2 0.3 collective-permute-start.7
  29.6 3.8 %collective-permute-start.8 = (f32[6,2,4,8,128]{4,3,2,1,0:T(8,128)S(1)}, f32[6,2,4,8,128]{4,3,2,1,0:T(8,128)S(1)}, u32[]{:S(2)}, u32[]{:S(2)}) collective-permute-start(f32[6,2,4,8,128]{4,3,2,1,0:T(8,128)S(1)} %get-tuple-element.44), channel_id=1, source_target_pairs={{32,64},{64,32},{33,65},{65,33},{34,66},{66,34},{35,67},{67,35},{3... | collective-permute-start | bytes 589832 | tf_op jit(solution)/shard_map/ppermute | solution.py:533
  33.3 4.9 %collective-permute-start.9 = (f32[6,2,32,128]{3,2,1,0:T(8,128)S(1)}, f32[6,2,32,128]{3,2,1,0:T(8,128)S(1)}, u32[]{:S(2)}, u32[]{:S(2)}) collective-permute-start(f32[6,2,32,128]{3,2,1,0:T(8,128)S(1)} %get-tuple-element.45), channel_id=1, source_target_pairs={{0,1},{1,0},{2,3},{3,2},{4,5},{5,4},{6,7},{7,6},{8,9},{9,8},{10,11... | collective-permute-start | bytes 589832 | tf_op jit(solution)/shard_map/ppermute | solution.py:533
  38.2 7.6 %step.3 = (f32[6,32,8,4,1,128]{5,4,3,2,1,0:T(1,128)}, f32[8,128]{1,0:T(8,128)}, f32[4,6,16,128]{3,2,1,0:T(8,128)S(1)}, f32[4,6,16,128]{3,2,1,0:T(8,128)S(1)}, f32[4,6,2,8,128]{4,3,2,1,0:T(8,128)S(1)}) custom-call(f32[6]{0:T(128)S(1)} %copy-done.2, f32[6,26,4,8,128]{4,3,2,1,0:T(8,128)S(1)} %get-tuple-element.49.q, ...), custom_call_target="tpu_custom_call", output_to_operand_aliasing={{0}: (2, {})} | custom-call | bytes 20000000 | tf_op jit(solution)/shard_map/step/pallas_call | solution.py:374
  45.9 3.9 %ends.1 = f32[6,32,8,4,1,128]{5,4,3,2,1,0:T(1,128)} custom-call(f32[6]{0:T(128)S(1)} %copy-done.2, f32[6,4,4,8,128]{4,3,2,1,0:T(8,128)S(1)} %get-tuple-element.40.z_own, f32[6,4,32,128]{3,2,1,0:T(8,128)S(1)} %get-tuple-element.41.y_own, f32[6,2,32,128]{3,2,1,0:T(8,128)S(1)} %collective-permute-done.6.y_far, ...), custom_call_target="tpu_custom_call", output_to_operand_aliasing={{}: (13, {})} | custom-call | bytes 6000000 | tf_op jit(solution)/shard_map/ends/pallas_call | solution.py:506
  (11 shorter events, 0.0 us)
Async XLA Ops:
  0.0 4.5 %copy-start = (f32[8,6,32768]{2,0,1:T(8,128)S(1)}, f32[8,6,32768]{2,0,1:T(8,128)}, u32[]{:S(2)}) copy-start(f32[8,6,32768]{2,0,1:T(8,128)} %param.4) | copy-start | bytes 18874372
  2.2 13.5 %collective-permute-start.5 = (f32[2,6,18,8,128]{4,3,2,1,0:T(8,128)}, f32[2,6,18,8,128]{4,3,2,1,0:T(8,128)S(1)}, u32[]{:S(2)}, u32[]{:S(2)}) collective-permute-start(f32[2,6,18,8,128]{4,3,2,1,0:T(8,128)} %get-tuple-element.38), channel_id=1, source_target_pairs={{1,2},{2,1},{3,4},{4,3},{5,6},{6,5},{7,8},{8,7},{9,10},{10,9},{11,... | collective-permute-start | bytes 2654216 | tf_op jit(solution)/shard_map/ppermute | solution.py:533
  4.5 0.7 %copy-start.3 = (f32[8,128]{1,0:T(8,128)S(1)}, f32[8,128]{1,0:T(8,128)}, u32[]{:S(2)}) copy-start(f32[8,128]{1,0:T(8,128)} %get-tuple-element.30.after) | copy-start | bytes 12292
  5.2 10.6 %copy-start.1 = (s32[512]{0:T(512)S(1)}, s32[512]{0:T(512)}, u32[]{:S(2)}) copy-start(s32[512]{0:T(512)} %owner.3) | copy-start | bytes 6148
  9.2 7.9 %copy-start.2 = (f32[6]{0:T(128)S(1)}, f32[6]{0:T(128)}, u32[]{:S(2)}) copy-start(f32[6]{0:T(128)} %spread.5) | copy-start | bytes 76
  9.2 3.9 %collective-permute-start.3 = (f32[2,6,9,8,128]{4,3,2,1,0:T(8,128)S(1)}, f32[2,6,9,8,128]{4,3,2,1,0:T(8,128)S(1)}, u32[]{:S(2)}, u32[]{:S(2)}) collective-permute-start(f32[2,6,9,8,128]{4,3,2,1,0:T(8,128)S(1)} %get-tuple-element.36), channel_id=1, source_target_pairs={{0,1},{1,0},{2,3},{3,2},{4,5},{5,4},{6,7},{7,6},{8,9},{9,8},{10,11... | collective-permute-start | bytes 1327112 | tf_op jit(solution)/shard_map/ppermute | solution.py:533
  11.4 12.8 %collective-permute-start.2 = (f32[2,6,14,8,128]{4,3,2,1,0:T(8,128)S(1)}, f32[2,6,14,8,128]{4,3,2,1,0:T(8,128)S(1)}, u32[]{:S(2)}, u32[]{:S(2)}) collective-permute-start(f32[2,6,14,8,128]{4,3,2,1,0:T(8,128)S(1)} %get-tuple-element.34), channel_id=1, source_target_pairs={{1,2},{2,1},{3,4},{4,3},{5,6},{6,5},{7,8},{8,7},{9,10},{10,9},{11,... | collective-permute-start | bytes 2064392 | tf_op jit(solution)/shard_map/ppermute | solution.py:533
  11.4 3.1 %collective-permute-start.4 = (f32[2,6,9,8,128]{4,3,2,1,0:T(8,128)S(1)}, f32[2,6,9,8,128]{4,3,2,1,0:T(8,128)S(1)}, u32[]{:S(2)}, u32[]{:S(2)}) collective-permute-start(f32[2,6,9,8,128]{4,3,2,1,0:T(8,128)S(1)} %get-tuple-element.37), channel_id=1, source_target_pairs={{0,1},{1,0},{2,3},{3,2},{4,5},{5,4},{6,7},{7,6},{8,9},{9,8},{10,11... | collective-permute-start | bytes 1327112 | tf_op jit(solution)/shard_map/ppermute | solution.py:533
  13.2 11.0 %collective-permute-start = (f32[2,6,7,8,128]{4,3,2,1,0:T(8,128)S(1)}, f32[2,6,7,8,128]{4,3,2,1,0:T(8,128)S(1)}, u32[]{:S(2)}, u32[]{:S(2)}) collective-permute-start(f32[2,6,7,8,128]{4,3,2,1,0:T(8,128)S(1)} %get-tuple-element.32), channel_id=1, source_target_pairs={{0,1},{1,0},{2,3},{3,2},{4,5},{5,4},{6,7},{7,6},{8,9},{9,8},{10,11... | collective-permute-start | bytes 1032200 | tf_op jit(solution)/shard_map/ppermute | solution.py:533
  13.2 11.0 %collective-permute-start.1 = (f32[2,6,7,8,128]{4,3,2,1,0:T(8,128)S(1)}, f32[2,6,7,8,128]{4,3,2,1,0:T(8,128)S(1)}, u32[]{:S(2)}, u32[]{:S(2)}) collective-permute-start(f32[2,6,7,8,128]{4,3,2,1,0:T(8,128)S(1)} %get-tuple-element.33), channel_id=1, source_target_pairs={{0,1},{1,0},{2,3},{3,2},{4,5},{5,4},{6,7},{7,6},{8,9},{9,8},{10,11... | collective-permute-start | bytes 1032200 | tf_op jit(solution)/shard_map/ppermute | solution.py:533
  25.9 20.0 %collective-permute-start.6 = (f32[6,2,32,128]{3,2,1,0:T(8,128)S(1)}, f32[6,2,32,128]{3,2,1,0:T(8,128)S(1)}, u32[]{:S(2)}, u32[]{:S(2)}) collective-permute-start(f32[6,2,32,128]{3,2,1,0:T(8,128)S(1)} %get-tuple-element.42), channel_id=1, source_target_pairs={{1,2},{2,1},{3,4},{4,3},{5,6},{6,5},{7,8},{8,7},{9,10},{10,9},{11,... | collective-permute-start | bytes 589832 | tf_op jit(solution)/shard_map/ppermute | solution.py:533
  29.2 16.6 %collective-permute-start.7 = (f32[6,2,4,8,128]{4,3,2,1,0:T(8,128)S(1)}, f32[6,2,4,8,128]{4,3,2,1,0:T(8,128)S(1)}, u32[]{:S(2)}, u32[]{:S(2)}) collective-permute-start(f32[6,2,4,8,128]{4,3,2,1,0:T(8,128)S(1)} %get-tuple-element.43), channel_id=1, source_target_pairs={{0,32},{32,0},{64,96},{96,64},{1,33},{33,1},{65,97},{97,65},{2,34}... | collective-permute-start | bytes 589832 | tf_op jit(solution)/shard_map/ppermute | solution.py:533
  29.6 16.3 %collective-permute-start.8 = (f32[6,2,4,8,128]{4,3,2,1,0:T(8,128)S(1)}, f32[6,2,4,8,128]{4,3,2,1,0:T(8,128)S(1)}, u32[]{:S(2)}, u32[]{:S(2)}) collective-permute-start(f32[6,2,4,8,128]{4,3,2,1,0:T(8,128)S(1)} %get-tuple-element.44), channel_id=1, source_target_pairs={{32,64},{64,32},{33,65},{65,33},{34,66},{66,34},{35,67},{67,35},{3... | collective-permute-start | bytes 589832 | tf_op jit(solution)/shard_map/ppermute | solution.py:533
  33.3 12.6 %collective-permute-start.9 = (f32[6,2,32,128]{3,2,1,0:T(8,128)S(1)}, f32[6,2,32,128]{3,2,1,0:T(8,128)S(1)}, u32[]{:S(2)}, u32[]{:S(2)}) collective-permute-start(f32[6,2,32,128]{3,2,1,0:T(8,128)S(1)} %get-tuple-element.45), channel_id=1, source_target_pairs={{0,1},{1,0},{2,3},{3,2},{4,5},{5,4},{6,7},{7,6},{8,9},{9,8},{10,11... | collective-permute-start | bytes 589832 | tf_op jit(solution)/shard_map/ppermute | solution.py:533

commit v10 on v9

--- a/solution.py
+++ b/solution.py
@@ -541,7 +541,7 @@
     far_high = exchange(far_high, AXES, 1, wrap=True)
     nears = [exchange(near, AXES, 0) for near in nears]
     q_low = turn_low(old_owner, hold_low, *nears[:2], far_low)
-    out, token, *low_ends = step(0, LOW, 8, diffusivity, q_low)
+    out, token, *low_ends = step(0, LOW, 4, diffusivity, q_low)
     q_high, z_own, y_own, z_pair, z_cross, y_near, y_far = turn_high(
         old_owner, token, hold_high, *nears[2:], far_high, q_low
     )
@@ -549,7 +549,7 @@
     y_far = exchange(y_far, "gy", 1)
     z_pair = exchange(z_pair, "gx", 0)
     z_cross = exchange(z_cross, "gx", 1)
-    out, _, *high_ends = step(LOW, B - LOW, 8, diffusivity, q_high, out)
+    out, _, *high_ends = step(LOW, B - LOW, 4, diffusivity, q_high, out)
     out = ends(
         diffusivity, z_own, y_own, y_far, z_pair, z_cross, y_near, *low_ends, *high_ends, out
     )

time: 50 us -> 49.9 us (level)
  no operation moved by 1% of the time
where the time goes in v10:
time: 49.9 us; the launch traced here: 49.7 us
  Pallas kernels  27.7 us (56%)
  starting transfers between devices  19.1 us (38%)
  waiting for transfers between devices  2.1 us (4%)
  local copies, waits for them, and re-layouts  0.69 us (1%)
    ppermute x10, starting transfers between devices, exchange(): return lax.ppermute(block, axes, pairs)  19.1 us
    pallas_call x2, Pallas kernels, step(): pl.pallas_call(functools.partial(step_body, first, count, chunk), name='s...  14.6 us
    pallas_call x2, Pallas kernels, from_slots(): pl.pallas_call(body, name=name, out_shape=shapes, in_specs=[HBM] * len(ar...  6.22 us
    pallas_call x1, Pallas kernels, ends(): pl.pallas_call(ends_body, name='ends', out_shape=jax.ShapeDtypeStruct((F,...  3.91 us
    pallas_call x2, Pallas kernels, turn(): pl.pallas_call(body, name=name, out_shape=tuple((jax.ShapeDtypeStruct(sha...  2.99 us
    ppermute x10, waiting for transfers between devices, exchange(): return lax.ppermute(block, axes, pairs)  2.1 us
  transfers between devices with their start and end apart: 10, of which 2 were waited for; matrix products, arithmetic and copies ran while one was open for 0% of the time, Pallas kernels for 40%

profile of v10, /device:TPU:27, one launch (start us, length us, event | category | flops | bytes accessed | tf_op | source)
XLA Modules:
  0.0 49.7 jit_solution(10148117323855943835)
XLA Ops:
  0.0 2.2 %far.1 = (f32[2,6,18,8,128]{4,3,2,1,0:T(8,128)}, f32[8,128]{1,0:T(8,128)}) custom-call(f32[6,32,8,8,1,128]{5,4,3,2,1,0:T(1,128)} %bitcast.10), custom_call_target="tpu_custom_call" | custom-call | bytes 1000 | tf_op jit(solution)/shard_map/far/pallas_call | solution.py:66
  2.2 2.3 %collective-permute-start.5 = (f32[2,6,18,8,128]{4,3,2,1,0:T(8,128)}, f32[2,6,18,8,128]{4,3,2,1,0:T(8,128)S(1)}, u32[]{:S(2)}, u32[]{:S(2)}) collective-permute-start(f32[2,6,18,8,128]{4,3,2,1,0:T(8,128)} %get-tuple-element.38), channel_id=1, source_target_pairs={{1,2},{2,1},{3,4},{4,3},{5,6},{6,5},{7,8},{8,7},{9,10},{10,9},{11,... | collective-permute-start | bytes 2654216 | tf_op jit(solution)/shard_map/ppermute | solution.py:533
  4.5 0.7 %copy-done.3 = f32[8,128]{1,0:T(8,128)S(1)} copy-done((f32[8,128]{1,0:T(8,128)S(1)}, f32[8,128]{1,0:T(8,128)}, u32[]{:S(2)}) %copy-start.3) | copy-done | bytes 4120
  5.2 4.0 %near.1 = (f32[2,6,14,8,128]{4,3,2,1,0:T(8,128)S(1)}, f32[2,6,9,8,128]{4,3,2,1,0:T(8,128)S(1)}, f32[2,6,9,8,128]{4,3,2,1,0:T(8,128)S(1)}, f32[2,6,7,8,128]{4,3,2...) custom-call(f32[6,32,8,8,1,128]{5,4,3,2,1,0:T(1,128)S(1)} %bitcast.1, ...), custom_call_target="tpu_custom_call" | custom-call | bytes 1000 | tf_op jit(solution)/shard_map/near/pallas_call | solution.py:66
  9.2 0.0 copy-start.2
  9.2 2.2 %collective-permute-start.3 = (f32[2,6,9,8,128]{4,3,2,1,0:T(8,128)S(1)}, f32[2,6,9,8,128]{4,3,2,1,0:T(8,128)S(1)}, u32[]{:S(2)}, u32[]{:S(2)}) collective-permute-start(f32[2,6,9,8,128]{4,3,2,1,0:T(8,128)S(1)} %get-tuple-element.36), channel_id=1, source_target_pairs={{0,1},{1,0},{2,3},{3,2},{4,5},{5,4},{6,7},{7,6},{8,9},{9,8},{10,11... | collective-permute-start | bytes 1327112 | tf_op jit(solution)/shard_map/ppermute | solution.py:533
  11.4 0.0 collective-permute-start.2
  11.4 1.7 %collective-permute-start.4 = (f32[2,6,9,8,128]{4,3,2,1,0:T(8,128)S(1)}, f32[2,6,9,8,128]{4,3,2,1,0:T(8,128)S(1)}, u32[]{:S(2)}, u32[]{:S(2)}) collective-permute-start(f32[2,6,9,8,128]{4,3,2,1,0:T(8,128)S(1)} %get-tuple-element.37), channel_id=1, source_target_pairs={{0,1},{1,0},{2,3},{3,2},{4,5},{5,4},{6,7},{7,6},{8,9},{9,8},{10,11... | collective-permute-start | bytes 1327112 | tf_op jit(solution)/shard_map/ppermute | solution.py:533
  13.2 0.0 collective-permute-start
  13.2 0.0 collective-permute-done.3.near_0
  13.2 0.5 %collective-permute-start.1 = (f32[2,6,7,8,128]{4,3,2,1,0:T(8,128)S(1)}, f32[2,6,7,8,128]{4,3,2,1,0:T(8,128)S(1)}, u32[]{:S(2)}, u32[]{:S(2)}) collective-permute-start(f32[2,6,7,8,128]{4,3,2,1,0:T(8,128)S(1)} %get-tuple-element.33), channel_id=1, source_target_pairs={{0,1},{1,0},{2,3},{3,2},{4,5},{5,4},{6,7},{7,6},{8,9},{9,8},{10,11... | collective-permute-start | bytes 1032200 | tf_op jit(solution)/shard_map/ppermute | solution.py:533
  13.7 0.9 %collective-permute-done.4.near_1 = f32[2,6,9,8,128]{4,3,2,1,0:T(8,128)S(1)} collective-permute-done((f32[2,6,9,8,128]{4,3,2,1,0:T(8,128)S(1)}, f32[2,6,9,8,128]{4,3,2,1,0:T(8,128)S(1)}, u32[]{:S(2)}, u32[]{:S(2)}) %collective-permute-start.4) | collective-permute-done | bytes 442400 | tf_op jit(solution)/shard_map/ppermute | solution.py:533
  14.6 1.2 %collective-permute-done.5.far = f32[2,6,18,8,128]{4,3,2,1,0:T(8,128)S(1)} collective-permute-done((f32[2,6,18,8,128]{4,3,2,1,0:T(8,128)}, f32[2,6,18,8,128]{4,3,2,1,0:T(8,128)S(1)}, u32[]{:S(2)}, u32[]{:S(2)}) %collective-permute-start.5) | collective-permute-done | bytes 884768 | tf_op jit(solution)/shard_map/ppermute | solution.py:533
  15.8 1.4 %turn_low.1.q.q_low = f32[6,26,4,8,128]{4,3,2,1,0:T(8,128)S(1)} custom-call(s32[512]{0:T(512)S(1)} %copy-done.1, f32[4,6,18,8,128]{4,3,2,1,0:T(8,128)S(1)} %get-tuple-element.35.hold, f32[2,6,9,8,128]{4,3,2,1,0:T(8,128)S(1)} %collective-permute-done.3.near_0, f32[2,6,9,8,128]{4,3,2,1,0:T(8,128)S(1)} %collective-permute-done.4.near_1, ...), custom_call_target="tpu_custom_call" | custom-call | bytes 6000000 | tf_op jit(solution)/shard_map/turn_low/pallas_call | solution.py:185
  17.1 7.0 %step.2 = (f32[6,32,8,4,1,128]{5,4,3,2,1,0:T(1,128)}, f32[8,128]{1,0:T(8,128)S(1)}, f32[4,6,16,128]{3,2,1,0:T(8,128)S(1)}, f32[4,6,16,128]{3,2,1,0:T(8,128)S(1)}, f32[4,6,2,8,128]{4,3,2,1,0:T(8,128)S(1)}) custom-call(f32[6]{0:T(128)S(1)} %copy-done.2, f32[6,26,4,8,128]{4,3,2,1,0:T(8,128)S(1)} %turn_low.1.q.q_low), custom_call_target="tpu_custom_call" | custom-call | bytes 20000000 | tf_op jit(solution)/shard_map/step/pallas_call | solution.py:374
  24.1 0.0 collective-permute-done.near_0
  24.2 0.0 collective-permute-done.2.far
  24.2 1.6 %turn_high.1 = (f32[6,26,4,8,128]{4,3,2,1,0:T(8,128)S(1)}, f32[6,4,4,8,128]{4,3,2,1,0:T(8,128)S(1)}, f32[6,4,32,128]{3,2,1,0:T(8,128)S(1)}, f32[6,2,4,8,128]{4,3...) custom-call(s32[512]{0:T(512)S(1)} %copy-done.1, ...), custom_call_target="tpu_custom_call" | custom-call | bytes 6000000 | tf_op jit(solution)/shard_map/turn_high/pallas_call | solution.py:185
  25.8 3.4 %collective-permute-start.6 = (f32[6,2,32,128]{3,2,1,0:T(8,128)S(1)}, f32[6,2,32,128]{3,2,1,0:T(8,128)S(1)}, u32[]{:S(2)}, u32[]{:S(2)}) collective-permute-start(f32[6,2,32,128]{3,2,1,0:T(8,128)S(1)} %get-tuple-element.42), channel_id=1, source_target_pairs={{1,2},{2,1},{3,4},{4,3},{5,6},{6,5},{7,8},{8,7},{9,10},{10,9},{11,... | collective-permute-start | bytes 589832 | tf_op jit(solution)/shard_map/ppermute | solution.py:533
  29.2 0.3 collective-permute-start.7
  29.5 3.8 %collective-permute-start.8 = (f32[6,2,4,8,128]{4,3,2,1,0:T(8,128)S(1)}, f32[6,2,4,8,128]{4,3,2,1,0:T(8,128)S(1)}, u32[]{:S(2)}, u32[]{:S(2)}) collective-permute-start(f32[6,2,4,8,128]{4,3,2,1,0:T(8,128)S(1)} %get-tuple-element.44), channel_id=1, source_target_pairs={{32,64},{64,32},{33,65},{65,33},{34,66},{66,34},{35,67},{67,35},{3... | collective-permute-start | bytes 589832 | tf_op jit(solution)/shard_map/ppermute | solution.py:533
  33.3 4.9 %collective-permute-start.9 = (f32[6,2,32,128]{3,2,1,0:T(8,128)S(1)}, f32[6,2,32,128]{3,2,1,0:T(8,128)S(1)}, u32[]{:S(2)}, u32[]{:S(2)}) collective-permute-start(f32[6,2,32,128]{3,2,1,0:T(8,128)S(1)} %get-tuple-element.45), channel_id=1, source_target_pairs={{0,1},{1,0},{2,3},{3,2},{4,5},{5,4},{6,7},{7,6},{8,9},{9,8},{10,11... | collective-permute-start | bytes 589832 | tf_op jit(solution)/shard_map/ppermute | solution.py:533
  38.2 7.6 %step.3 = (f32[6,32,8,4,1,128]{5,4,3,2,1,0:T(1,128)}, f32[8,128]{1,0:T(8,128)}, f32[4,6,16,128]{3,2,1,0:T(8,128)S(1)}, f32[4,6,16,128]{3,2,1,0:T(8,128)S(1)}, f32[4,6,2,8,128]{4,3,2,1,0:T(8,128)S(1)}) custom-call(f32[6]{0:T(128)S(1)} %copy-done.2, f32[6,26,4,8,128]{4,3,2,1,0:T(8,128)S(1)} %get-tuple-element.49.q, ...), custom_call_target="tpu_custom_call", output_to_operand_aliasing={{0}: (2, {})} | custom-call | bytes 20000000 | tf_op jit(solution)/shard_map/step/pallas_call | solution.py:374
  45.8 3.9 %ends.1 = f32[6,32,8,4,1,128]{5,4,3,2,1,0:T(1,128)} custom-call(f32[6]{0:T(128)S(1)} %copy-done.2, f32[6,4,4,8,128]{4,3,2,1,0:T(8,128)S(1)} %get-tuple-element.40.z_own, f32[6,4,32,128]{3,2,1,0:T(8,128)S(1)} %get-tuple-element.41.y_own, f32[6,2,32,128]{3,2,1,0:T(8,128)S(1)} %collective-permute-done.6.y_far, ...), custom_call_target="tpu_custom_call", output_to_operand_aliasing={{}: (13, {})} | custom-call | bytes 6000000 | tf_op jit(solution)/shard_map/ends/pallas_call | solution.py:506
  (11 shorter events, 0.0 us)
Async XLA Ops:
  0.0 4.5 %copy-start = (f32[8,6,32768]{2,0,1:T(8,128)S(1)}, f32[8,6,32768]{2,0,1:T(8,128)}, u32[]{:S(2)}) copy-start(f32[8,6,32768]{2,0,1:T(8,128)} %param.4) | copy-start | bytes 18874372
  2.2 13.5 %collective-permute-start.5 = (f32[2,6,18,8,128]{4,3,2,1,0:T(8,128)}, f32[2,6,18,8,128]{4,3,2,1,0:T(8,128)S(1)}, u32[]{:S(2)}, u32[]{:S(2)}) collective-permute-start(f32[2,6,18,8,128]{4,3,2,1,0:T(8,128)} %get-tuple-element.38), channel_id=1, source_target_pairs={{1,2},{2,1},{3,4},{4,3},{5,6},{6,5},{7,8},{8,7},{9,10},{10,9},{11,... | collective-permute-start | bytes 2654216 | tf_op jit(solution)/shard_map/ppermute | solution.py:533
  4.5 0.7 %copy-start.3 = (f32[8,128]{1,0:T(8,128)S(1)}, f32[8,128]{1,0:T(8,128)}, u32[]{:S(2)}) copy-start(f32[8,128]{1,0:T(8,128)} %get-tuple-element.30.after) | copy-start | bytes 12292
  5.2 10.6 %copy-start.1 = (s32[512]{0:T(512)S(1)}, s32[512]{0:T(512)}, u32[]{:S(2)}) copy-start(s32[512]{0:T(512)} %owner.3) | copy-start | bytes 6148
  9.2 7.9 %copy-start.2 = (f32[6]{0:T(128)S(1)}, f32[6]{0:T(128)}, u32[]{:S(2)}) copy-start(f32[6]{0:T(128)} %spread.5) | copy-start | bytes 76
  9.2 3.9 %collective-permute-start.3 = (f32[2,6,9,8,128]{4,3,2,1,0:T(8,128)S(1)}, f32[2,6,9,8,128]{4,3,2,1,0:T(8,128)S(1)}, u32[]{:S(2)}, u32[]{:S(2)}) collective-permute-start(f32[2,6,9,8,128]{4,3,2,1,0:T(8,128)S(1)} %get-tuple-element.36), channel_id=1, source_target_pairs={{0,1},{1,0},{2,3},{3,2},{4,5},{5,4},{6,7},{7,6},{8,9},{9,8},{10,11... | collective-permute-start | bytes 1327112 | tf_op jit(solution)/shard_map/ppermute | solution.py:533
  11.4 12.7 %collective-permute-start.2 = (f32[2,6,14,8,128]{4,3,2,1,0:T(8,128)S(1)}, f32[2,6,14,8,128]{4,3,2,1,0:T(8,128)S(1)}, u32[]{:S(2)}, u32[]{:S(2)}) collective-permute-start(f32[2,6,14,8,128]{4,3,2,1,0:T(8,128)S(1)} %get-tuple-element.34), channel_id=1, source_target_pairs={{1,2},{2,1},{3,4},{4,3},{5,6},{6,5},{7,8},{8,7},{9,10},{10,9},{11,... | collective-permute-start | bytes 2064392 | tf_op jit(solution)/shard_map/ppermute | solution.py:533
  11.4 3.1 %collective-permute-start.4 = (f32[2,6,9,8,128]{4,3,2,1,0:T(8,128)S(1)}, f32[2,6,9,8,128]{4,3,2,1,0:T(8,128)S(1)}, u32[]{:S(2)}, u32[]{:S(2)}) collective-permute-start(f32[2,6,9,8,128]{4,3,2,1,0:T(8,128)S(1)} %get-tuple-element.37), channel_id=1, source_target_pairs={{0,1},{1,0},{2,3},{3,2},{4,5},{5,4},{6,7},{7,6},{8,9},{9,8},{10,11... | collective-permute-start | bytes 1327112 | tf_op jit(solution)/shard_map/ppermute | solution.py:533
  13.2 11.0 %collective-permute-start = (f32[2,6,7,8,128]{4,3,2,1,0:T(8,128)S(1)}, f32[2,6,7,8,128]{4,3,2,1,0:T(8,128)S(1)}, u32[]{:S(2)}, u32[]{:S(2)}) collective-permute-start(f32[2,6,7,8,128]{4,3,2,1,0:T(8,128)S(1)} %get-tuple-element.32), channel_id=1, source_target_pairs={{0,1},{1,0},{2,3},{3,2},{4,5},{5,4},{6,7},{7,6},{8,9},{9,8},{10,11... | collective-permute-start | bytes 1032200 | tf_op jit(solution)/shard_map/ppermute | solution.py:533
  13.2 11.0 %collective-permute-start.1 = (f32[2,6,7,8,128]{4,3,2,1,0:T(8,128)S(1)}, f32[2,6,7,8,128]{4,3,2,1,0:T(8,128)S(1)}, u32[]{:S(2)}, u32[]{:S(2)}) collective-permute-start(f32[2,6,7,8,128]{4,3,2,1,0:T(8,128)S(1)} %get-tuple-element.33), channel_id=1, source_target_pairs={{0,1},{1,0},{2,3},{3,2},{4,5},{5,4},{6,7},{7,6},{8,9},{9,8},{10,11... | collective-permute-start | bytes 1032200 | tf_op jit(solution)/shard_map/ppermute | solution.py:533
  25.8 19.9 %collective-permute-start.6 = (f32[6,2,32,128]{3,2,1,0:T(8,128)S(1)}, f32[6,2,32,128]{3,2,1,0:T(8,128)S(1)}, u32[]{:S(2)}, u32[]{:S(2)}) collective-permute-start(f32[6,2,32,128]{3,2,1,0:T(8,128)S(1)} %get-tuple-element.42), channel_id=1, source_target_pairs={{1,2},{2,1},{3,4},{4,3},{5,6},{6,5},{7,8},{8,7},{9,10},{10,9},{11,... | collective-permute-start | bytes 589832 | tf_op jit(solution)/shard_map/ppermute | solution.py:533
  29.2 16.6 %collective-permute-start.7 = (f32[6,2,4,8,128]{4,3,2,1,0:T(8,128)S(1)}, f32[6,2,4,8,128]{4,3,2,1,0:T(8,128)S(1)}, u32[]{:S(2)}, u32[]{:S(2)}) collective-permute-start(f32[6,2,4,8,128]{4,3,2,1,0:T(8,128)S(1)} %get-tuple-element.43), channel_id=1, source_target_pairs={{0,32},{32,0},{64,96},{96,64},{1,33},{33,1},{65,97},{97,65},{2,34}... | collective-permute-start | bytes 589832 | tf_op jit(solution)/shard_map/ppermute | solution.py:533
  29.5 16.3 %collective-permute-start.8 = (f32[6,2,4,8,128]{4,3,2,1,0:T(8,128)S(1)}, f32[6,2,4,8,128]{4,3,2,1,0:T(8,128)S(1)}, u32[]{:S(2)}, u32[]{:S(2)}) collective-permute-start(f32[6,2,4,8,128]{4,3,2,1,0:T(8,128)S(1)} %get-tuple-element.44), channel_id=1, source_target_pairs={{32,64},{64,32},{33,65},{65,33},{34,66},{66,34},{35,67},{67,35},{3... | collective-permute-start | bytes 589832 | tf_op jit(solution)/shard_map/ppermute | solution.py:533
  33.3 12.5 %collective-permute-start.9 = (f32[6,2,32,128]{3,2,1,0:T(8,128)S(1)}, f32[6,2,32,128]{3,2,1,0:T(8,128)S(1)}, u32[]{:S(2)}, u32[]{:S(2)}) collective-permute-start(f32[6,2,32,128]{3,2,1,0:T(8,128)S(1)} %get-tuple-element.45), channel_id=1, source_target_pairs={{0,1},{1,0},{2,3},{3,2},{4,5},{5,4},{6,7},{7,6},{8,9},{9,8},{10,11... | collective-permute-start | bytes 589832 | tf_op jit(solution)/shard_map/ppermute | solution.py:533

commit v11 on v9

--- a/solution.py
+++ b/solution.py
@@ -42,14 +42,17 @@
     ]
 
 
-def far_body(x, low, token, sem):
+def far_body(x, low, high, token, sem):
     token[...] = jnp.zeros_like(token)
-    run_all(leaving_copies(x, False, low, slice(0, HALF), sem))
-
-
-def near_body(x, after, high, *rest):
+    run_all(
+        leaving_copies(x, False, low, slice(0, HALF), sem.at[0])
+        + leaving_copies(x, False, high, slice(HALF, B), sem.at[1])
+    )
+
+
+def near_body(x, after, *rest):
     nears, (hold_low, hold_high, sem) = rest[: len(PARTS)], rest[len(PARTS) :]
-    copies = leaving_copies(x, False, high, slice(HALF, B), sem.at[2 + len(PARTS)])
+    copies = []
     for k, near in enumerate(nears):
         copies += leaving_copies(x, True, near, slice(*PARTS[k]), sem.at[2 + k])
     for k, hold in enumerate((hold_low, hold_high)):
@@ -76,14 +79,16 @@
 
 
 def far_boxes(x):
-    return from_slots(far_body, "far", [x], [(2, F, HALF, ROWS, LANES), (ROWS, LANES)], (2,), WIDE)
+    boxes = lambda planes: (2, F, planes, ROWS, LANES)
+    shapes = [boxes(HALF), boxes(B - HALF), (ROWS, LANES)]
+    return from_slots(far_body, "far", [x], shapes, (2, 2), WIDE)
 
 
 def near_boxes(x, after):
     boxes = lambda count, planes: (count, F, planes, ROWS, LANES)
-    shapes = [boxes(2, B - HALF)] + [boxes(2, end - start) for start, end in PARTS]
+    shapes = [boxes(2, end - start) for start, end in PARTS]
     shapes += [boxes(CAP, HALF), boxes(CAP, B - HALF)]
-    return from_slots(near_body, "near", [x, after], shapes, (3 + len(PARTS), CAP), 24 << 20)
+    return from_slots(near_body, "near", [x, after], shapes, (2 + len(PARTS), CAP), 24 << 20)
 
 
 def device_number():
@@ -535,8 +540,8 @@
 
 def local(old_state, old_owner, old_slot, diffusivity):
     x = old_state.reshape(8, F, B, ROWS, LANES).transpose(1, 2, 3, 0, 4)[..., None, :]
-    far_low, token = far_boxes(x)
-    far_high, *nears, hold_low, hold_high = near_boxes(x, token)
+    far_low, far_high, token = far_boxes(x)
+    *nears, hold_low, hold_high = near_boxes(x, token)
     far_low = exchange(far_low, AXES, 1, wrap=True)
     far_high = exchange(far_high, AXES, 1, wrap=True)
     nears = [exchange(near, AXES, 0) for near in nears]

time: 50 us -> 50.4 us (level)
  transfers between devices with their start and end apart: 10 -> 10, of which waited for: 2 -> 2; matrix products, arithmetic and copies ran while one was open for 0% -> 0% of each run, Pallas kernels for 40% -> 39%
where the time goes in v11:
time: 50.4 us; the launch traced here: 50.3 us
  Pallas kernels  27.7 us (55%)
  starting transfers between devices  19.1 us (38%)
  waiting for transfers between devices  2.59 us (5%)
  local copies, waits for them, and re-layouts  0.7 us (1%)
    ppermute x10, starting transfers between devices, exchange(): return lax.ppermute(block, axes, pairs)  19.1 us
    pallas_call x2, Pallas kernels, step(): pl.pallas_call(functools.partial(step_body, first, count, chunk), name='s...  14.7 us
    pallas_call x2, Pallas kernels, from_slots(): pl.pallas_call(body, name=name, out_shape=shapes, in_specs=[HBM] * len(ar...  6.16 us
    pallas_call x1, Pallas kernels, ends(): pl.pallas_call(ends_body, name='ends', out_shape=jax.ShapeDtypeStruct((F,...  3.91 us
    pallas_call x2, Pallas kernels, turn(): pl.pallas_call(body, name=name, out_shape=tuple((jax.ShapeDtypeStruct(sha...  2.99 us
    ppermute x10, waiting for transfers between devices, exchange(): return lax.ppermute(block, axes, pairs)  2.59 us
  transfers between devices with their start and end apart: 10, of which 2 were waited for; matrix products, arithmetic and copies ran while one was open for 0% of the time, Pallas kernels for 39%

profile of v11, /device:TPU:27, one launch (start us, length us, event | category | flops | bytes accessed | tf_op | source)
XLA Modules:
  0.0 50.3 jit_solution(6607366352925084949)
XLA Ops:
  0.0 2.7 %far.1 = (f32[2,6,18,8,128]{4,3,2,1,0:T(8,128)}, f32[2,6,14,8,128]{4,3,2,1,0:T(8,128)}, f32[8,128]{1,0:T(8,128)}) custom-call(f32[6,32,8,8,1,128]{5,4,3,2,1,0:T(1,128)} %bitcast.10), custom_call_target="tpu_custom_call" | custom-call | bytes 1000 | tf_op jit(solution)/shard_map/far/pallas_call | solution.py:69
  2.7 2.3 %collective-permute-start.5 = (f32[2,6,18,8,128]{4,3,2,1,0:T(8,128)}, f32[2,6,18,8,128]{4,3,2,1,0:T(8,128)S(1)}, u32[]{:S(2)}, u32[]{:S(2)}) collective-permute-start(f32[2,6,18,8,128]{4,3,2,1,0:T(8,128)} %get-tuple-element.38), channel_id=1, source_target_pairs={{1,2},{2,1},{3,4},{4,3},{5,6},{6,5},{7,8},{8,7},{9,10},{10,9},{11,... | collective-permute-start | bytes 2654216 | tf_op jit(solution)/shard_map/ppermute | solution.py:538
  5.0 0.7 %copy-done.3 = f32[8,128]{1,0:T(8,128)S(1)} copy-done((f32[8,128]{1,0:T(8,128)S(1)}, f32[8,128]{1,0:T(8,128)}, u32[]{:S(2)}) %copy-start.3) | copy-done | bytes 4120
  5.7 3.5 %near.1 = (f32[2,6,9,8,128]{4,3,2,1,0:T(8,128)S(1)}, f32[2,6,9,8,128]{4,3,2,1,0:T(8,128)S(1)}, f32[2,6,7,8,128]{4,3,2,1,0:T(8,128)S(1)}, f32[2,6,7,8,128]{4,3,2,...) custom-call(f32[6,32,8,8,1,128]{5,4,3,2,1,0:T(1,128)S(1)} %bitcast.11, ...), custom_call_target="tpu_custom_call" | custom-call | bytes 1000 | tf_op jit(solution)/shard_map/near/pallas_call | solution.py:69
  9.1 0.0 copy-start.2
  9.2 2.2 %collective-permute-start.3 = (f32[2,6,9,8,128]{4,3,2,1,0:T(8,128)S(1)}, f32[2,6,9,8,128]{4,3,2,1,0:T(8,128)S(1)}, u32[]{:S(2)}, u32[]{:S(2)}) collective-permute-start(f32[2,6,9,8,128]{4,3,2,1,0:T(8,128)S(1)} %get-tuple-element.36), channel_id=1, source_target_pairs={{0,1},{1,0},{2,3},{3,2},{4,5},{5,4},{6,7},{7,6},{8,9},{9,8},{10,11... | collective-permute-start | bytes 1327112 | tf_op jit(solution)/shard_map/ppermute | solution.py:538
  11.4 0.0 collective-permute-start.2
  11.4 1.7 %collective-permute-start.4 = (f32[2,6,9,8,128]{4,3,2,1,0:T(8,128)S(1)}, f32[2,6,9,8,128]{4,3,2,1,0:T(8,128)S(1)}, u32[]{:S(2)}, u32[]{:S(2)}) collective-permute-start(f32[2,6,9,8,128]{4,3,2,1,0:T(8,128)S(1)} %get-tuple-element.37), channel_id=1, source_target_pairs={{0,1},{1,0},{2,3},{3,2},{4,5},{5,4},{6,7},{7,6},{8,9},{9,8},{10,11... | collective-permute-start | bytes 1327112 | tf_op jit(solution)/shard_map/ppermute | solution.py:538
  13.1 0.5 %collective-permute-start.1 = (f32[2,6,7,8,128]{4,3,2,1,0:T(8,128)S(1)}, f32[2,6,7,8,128]{4,3,2,1,0:T(8,128)S(1)}, u32[]{:S(2)}, u32[]{:S(2)}) collective-permute-start(f32[2,6,7,8,128]{4,3,2,1,0:T(8,128)S(1)} %get-tuple-element.33), channel_id=1, source_target_pairs={{0,1},{1,0},{2,3},{3,2},{4,5},{5,4},{6,7},{7,6},{8,9},{9,8},{10,11... | collective-permute-start | bytes 1032200 | tf_op jit(solution)/shard_map/ppermute | solution.py:538
  13.6 0.9 %collective-permute-done.4.near_1 = f32[2,6,9,8,128]{4,3,2,1,0:T(8,128)S(1)} collective-permute-done((f32[2,6,9,8,128]{4,3,2,1,0:T(8,128)S(1)}, f32[2,6,9,8,128]{4,3,2,1,0:T(8,128)S(1)}, u32[]{:S(2)}, u32[]{:S(2)}) %collective-permute-start.4) | collective-permute-done | bytes 442400 | tf_op jit(solution)/shard_map/ppermute | solution.py:538
  14.5 1.7 %collective-permute-done.5.far = f32[2,6,18,8,128]{4,3,2,1,0:T(8,128)S(1)} collective-permute-done((f32[2,6,18,8,128]{4,3,2,1,0:T(8,128)}, f32[2,6,18,8,128]{4,3,2,1,0:T(8,128)S(1)}, u32[]{:S(2)}, u32[]{:S(2)}) %collective-permute-start.5) | collective-permute-done | bytes 884768 | tf_op jit(solution)/shard_map/ppermute | solution.py:538
  16.2 1.4 %turn_low.1.q.q_low = f32[6,26,4,8,128]{4,3,2,1,0:T(8,128)S(1)} custom-call(s32[512]{0:T(512)S(1)} %copy-done.1, f32[4,6,18,8,128]{4,3,2,1,0:T(8,128)S(1)} %get-tuple-element.35.hold, f32[2,6,9,8,128]{4,3,2,1,0:T(8,128)S(1)} %collective-permute-done.3.near_0, f32[2,6,9,8,128]{4,3,2,1,0:T(8,128)S(1)} %collective-permute-done.4.near_1, ...), custom_call_target="tpu_custom_call" | custom-call | bytes 6000000 | tf_op jit(solution)/shard_map/turn_low/pallas_call | solution.py:190
  17.6 7.0 %step.2 = (f32[6,32,8,4,1,128]{5,4,3,2,1,0:T(1,128)}, f32[8,128]{1,0:T(8,128)S(1)}, f32[4,6,16,128]{3,2,1,0:T(8,128)S(1)}, f32[4,6,16,128]{3,2,1,0:T(8,128)S(1)}, f32[4,6,2,8,128]{4,3,2,1,0:T(8,128)S(1)}) custom-call(f32[6]{0:T(128)S(1)} %copy-done.2, f32[6,26,4,8,128]{4,3,2,1,0:T(8,128)S(1)} %turn_low.1.q.q_low), custom_call_target="tpu_custom_call" | custom-call | bytes 20000000 | tf_op jit(solution)/shard_map/step/pallas_call | solution.py:379
  24.7 0.0 collective-permute-done.2.far
  24.7 1.6 %turn_high.1 = (f32[6,26,4,8,128]{4,3,2,1,0:T(8,128)S(1)}, f32[6,4,4,8,128]{4,3,2,1,0:T(8,128)S(1)}, f32[6,4,32,128]{3,2,1,0:T(8,128)S(1)}, f32[6,2,4,8,128]{4,3...) custom-call(s32[512]{0:T(512)S(1)} %copy-done.1, ...), custom_call_target="tpu_custom_call" | custom-call | bytes 6000000 | tf_op jit(solution)/shard_map/turn_high/pallas_call | solution.py:190
  26.3 3.4 %collective-permute-start.6 = (f32[6,2,32,128]{3,2,1,0:T(8,128)S(1)}, f32[6,2,32,128]{3,2,1,0:T(8,128)S(1)}, u32[]{:S(2)}, u32[]{:S(2)}) collective-permute-start(f32[6,2,32,128]{3,2,1,0:T(8,128)S(1)} %get-tuple-element.42), channel_id=1, source_target_pairs={{1,2},{2,1},{3,4},{4,3},{5,6},{6,5},{7,8},{8,7},{9,10},{10,9},{11,... | collective-permute-start | bytes 589832 | tf_op jit(solution)/shard_map/ppermute | solution.py:538
  29.7 0.3 collective-permute-start.7
  30.0 3.8 %collective-permute-start.8 = (f32[6,2,4,8,128]{4,3,2,1,0:T(8,128)S(1)}, f32[6,2,4,8,128]{4,3,2,1,0:T(8,128)S(1)}, u32[]{:S(2)}, u32[]{:S(2)}) collective-permute-start(f32[6,2,4,8,128]{4,3,2,1,0:T(8,128)S(1)} %get-tuple-element.44), channel_id=1, source_target_pairs={{32,64},{64,32},{33,65},{65,33},{34,66},{66,34},{35,67},{67,35},{3... | collective-permute-start | bytes 589832 | tf_op jit(solution)/shard_map/ppermute | solution.py:538
  33.8 4.9 %collective-permute-start.9 = (f32[6,2,32,128]{3,2,1,0:T(8,128)S(1)}, f32[6,2,32,128]{3,2,1,0:T(8,128)S(1)}, u32[]{:S(2)}, u32[]{:S(2)}) collective-permute-start(f32[6,2,32,128]{3,2,1,0:T(8,128)S(1)} %get-tuple-element.45), channel_id=1, source_target_pairs={{0,1},{1,0},{2,3},{3,2},{4,5},{5,4},{6,7},{7,6},{8,9},{9,8},{10,11... | collective-permute-start | bytes 589832 | tf_op jit(solution)/shard_map/ppermute | solution.py:538
  38.7 7.6 %step.3 = (f32[6,32,8,4,1,128]{5,4,3,2,1,0:T(1,128)}, f32[8,128]{1,0:T(8,128)}, f32[4,6,16,128]{3,2,1,0:T(8,128)S(1)}, f32[4,6,16,128]{3,2,1,0:T(8,128)S(1)}, f32[4,6,2,8,128]{4,3,2,1,0:T(8,128)S(1)}) custom-call(f32[6]{0:T(128)S(1)} %copy-done.2, f32[6,26,4,8,128]{4,3,2,1,0:T(8,128)S(1)} %get-tuple-element.49.q, ...), custom_call_target="tpu_custom_call", output_to_operand_aliasing={{0}: (2, {})} | custom-call | bytes 20000000 | tf_op jit(solution)/shard_map/step/pallas_call | solution.py:379
  46.3 0.0 collective-permute-done.6.y_far
  46.3 0.0 collective-permute-done.8.z_cross
  46.3 0.0 collective-permute-done.9.y_near
  46.3 3.9 %ends.1 = f32[6,32,8,4,1,128]{5,4,3,2,1,0:T(1,128)} custom-call(f32[6]{0:T(128)S(1)} %copy-done.2, f32[6,4,4,8,128]{4,3,2,1,0:T(8,128)S(1)} %get-tuple-element.40.z_own, f32[6,4,32,128]{3,2,1,0:T(8,128)S(1)} %get-tuple-element.41.y_own, f32[6,2,32,128]{3,2,1,0:T(8,128)S(1)} %collective-permute-done.6.y_far, ...), custom_call_target="tpu_custom_call", output_to_operand_aliasing={{}: (13, {})} | custom-call | bytes 6000000 | tf_op jit(solution)/shard_map/ends/pallas_call | solution.py:511
  (13 shorter events, 0.0 us)
Async XLA Ops:
  0.0 5.0 %copy-start = (f32[8,6,32768]{2,0,1:T(8,128)S(1)}, f32[8,6,32768]{2,0,1:T(8,128)}, u32[]{:S(2)}) copy-start(f32[8,6,32768]{2,0,1:T(8,128)} %param.4) | copy-start | bytes 18874372
  2.7 13.5 %collective-permute-start.5 = (f32[2,6,18,8,128]{4,3,2,1,0:T(8,128)}, f32[2,6,18,8,128]{4,3,2,1,0:T(8,128)S(1)}, u32[]{:S(2)}, u32[]{:S(2)}) collective-permute-start(f32[2,6,18,8,128]{4,3,2,1,0:T(8,128)} %get-tuple-element.38), channel_id=1, source_target_pairs={{1,2},{2,1},{3,4},{4,3},{5,6},{6,5},{7,8},{8,7},{9,10},{10,9},{11,... | collective-permute-start | bytes 2654216 | tf_op jit(solution)/shard_map/ppermute | solution.py:538
  5.0 0.7 %copy-start.3 = (f32[8,128]{1,0:T(8,128)S(1)}, f32[8,128]{1,0:T(8,128)}, u32[]{:S(2)}) copy-start(f32[8,128]{1,0:T(8,128)} %get-tuple-element.30.after) | copy-start | bytes 12292
  5.7 5.7 %copy-start.4 = (f32[2,6,14,8,128]{4,3,2,1,0:T(8,128)S(1)}, f32[2,6,14,8,128]{4,3,2,1,0:T(8,128)}, u32[]{:S(2)}) copy-start(f32[2,6,14,8,128]{4,3,2,1,0:T(8,128)} %get-tuple-element.34) | copy-start | bytes 2064388
  5.7 10.5 %copy-start.1 = (s32[512]{0:T(512)S(1)}, s32[512]{0:T(512)}, u32[]{:S(2)}) copy-start(s32[512]{0:T(512)} %owner.3) | copy-start | bytes 6148
  9.1 8.4 %copy-start.2 = (f32[6]{0:T(128)S(1)}, f32[6]{0:T(128)}, u32[]{:S(2)}) copy-start(f32[6]{0:T(128)} %spread.5) | copy-start | bytes 76
  9.2 4.0 %collective-permute-start.3 = (f32[2,6,9,8,128]{4,3,2,1,0:T(8,128)S(1)}, f32[2,6,9,8,128]{4,3,2,1,0:T(8,128)S(1)}, u32[]{:S(2)}, u32[]{:S(2)}) collective-permute-start(f32[2,6,9,8,128]{4,3,2,1,0:T(8,128)S(1)} %get-tuple-element.36), channel_id=1, source_target_pairs={{0,1},{1,0},{2,3},{3,2},{4,5},{5,4},{6,7},{7,6},{8,9},{9,8},{10,11... | collective-permute-start | bytes 1327112 | tf_op jit(solution)/shard_map/ppermute | solution.py:538
  11.4 13.3 %collective-permute-start.2 = (f32[2,6,14,8,128]{4,3,2,1,0:T(8,128)S(1)}, f32[2,6,14,8,128]{4,3,2,1,0:T(8,128)S(1)}, u32[]{:S(2)}, u32[]{:S(2)}) collective-permute-start(f32[2,6,14,8,128]{4,3,2,1,0:T(8,128)S(1)} %copy-done.4), channel_id=1, source_target_pairs={{1,2},{2,1},{3,4},{4,3},{5,6},{6,5},{7,8},{8,7},{9,10},{10,9},{11,... | collective-permute-start | bytes 2064392 | tf_op jit(solution)/shard_map/ppermute | solution.py:538
  11.4 3.2 %collective-permute-start.4 = (f32[2,6,9,8,128]{4,3,2,1,0:T(8,128)S(1)}, f32[2,6,9,8,128]{4,3,2,1,0:T(8,128)S(1)}, u32[]{:S(2)}, u32[]{:S(2)}) collective-permute-start(f32[2,6,9,8,128]{4,3,2,1,0:T(8,128)S(1)} %get-tuple-element.37), channel_id=1, source_target_pairs={{0,1},{1,0},{2,3},{3,2},{4,5},{5,4},{6,7},{7,6},{8,9},{9,8},{10,11... | collective-permute-start | bytes 1327112 | tf_op jit(solution)/shard_map/ppermute | solution.py:538
  13.1 11.5 %collective-permute-start = (f32[2,6,7,8,128]{4,3,2,1,0:T(8,128)S(1)}, f32[2,6,7,8,128]{4,3,2,1,0:T(8,128)S(1)}, u32[]{:S(2)}, u32[]{:S(2)}) collective-permute-start(f32[2,6,7,8,128]{4,3,2,1,0:T(8,128)S(1)} %get-tuple-element.32), channel_id=1, source_target_pairs={{0,1},{1,0},{2,3},{3,2},{4,5},{5,4},{6,7},{7,6},{8,9},{9,8},{10,11... | collective-permute-start | bytes 1032200 | tf_op jit(solution)/shard_map/ppermute | solution.py:538
  13.1 11.5 %collective-permute-start.1 = (f32[2,6,7,8,128]{4,3,2,1,0:T(8,128)S(1)}, f32[2,6,7,8,128]{4,3,2,1,0:T(8,128)S(1)}, u32[]{:S(2)}, u32[]{:S(2)}) collective-permute-start(f32[2,6,7,8,128]{4,3,2,1,0:T(8,128)S(1)} %get-tuple-element.33), channel_id=1, source_target_pairs={{0,1},{1,0},{2,3},{3,2},{4,5},{5,4},{6,7},{7,6},{8,9},{9,8},{10,11... | collective-permute-start | bytes 1032200 | tf_op jit(solution)/shard_map/ppermute | solution.py:538
  26.3 20.0 %collective-permute-start.6 = (f32[6,2,32,128]{3,2,1,0:T(8,128)S(1)}, f32[6,2,32,128]{3,2,1,0:T(8,128)S(1)}, u32[]{:S(2)}, u32[]{:S(2)}) collective-permute-start(f32[6,2,32,128]{3,2,1,0:T(8,128)S(1)} %get-tuple-element.42), channel_id=1, source_target_pairs={{1,2},{2,1},{3,4},{4,3},{5,6},{6,5},{7,8},{8,7},{9,10},{10,9},{11,... | collective-permute-start | bytes 589832 | tf_op jit(solution)/shard_map/ppermute | solution.py:538
  29.7 16.6 %collective-permute-start.7 = (f32[6,2,4,8,128]{4,3,2,1,0:T(8,128)S(1)}, f32[6,2,4,8,128]{4,3,2,1,0:T(8,128)S(1)}, u32[]{:S(2)}, u32[]{:S(2)}) collective-permute-start(f32[6,2,4,8,128]{4,3,2,1,0:T(8,128)S(1)} %get-tuple-element.43), channel_id=1, source_target_pairs={{0,32},{32,0},{64,96},{96,64},{1,33},{33,1},{65,97},{97,65},{2,34}... | collective-permute-start | bytes 589832 | tf_op jit(solution)/shard_map/ppermute | solution.py:538
  30.0 16.3 %collective-permute-start.8 = (f32[6,2,4,8,128]{4,3,2,1,0:T(8,128)S(1)}, f32[6,2,4,8,128]{4,3,2,1,0:T(8,128)S(1)}, u32[]{:S(2)}, u32[]{:S(2)}) collective-permute-start(f32[6,2,4,8,128]{4,3,2,1,0:T(8,128)S(1)} %get-tuple-element.44), channel_id=1, source_target_pairs={{32,64},{64,32},{33,65},{65,33},{34,66},{66,34},{35,67},{67,35},{3... | collective-permute-start | bytes 589832 | tf_op jit(solution)/shard_map/ppermute | solution.py:538
  33.8 12.6 %collective-permute-start.9 = (f32[6,2,32,128]{3,2,1,0:T(8,128)S(1)}, f32[6,2,32,128]{3,2,1,0:T(8,128)S(1)}, u32[]{:S(2)}, u32[]{:S(2)}) collective-permute-start(f32[6,2,32,128]{3,2,1,0:T(8,128)S(1)} %get-tuple-element.45), channel_id=1, source_target_pairs={{0,1},{1,0},{2,3},{3,2},{4,5},{5,4},{6,7},{7,6},{8,9},{9,8},{10,11... | collective-permute-start | bytes 589832 | tf_op jit(solution)/shard_map/ppermute | solution.py:538

commit v12 on v9

--- a/solution.py
+++ b/solution.py
@@ -434,7 +434,7 @@
 
 
 def ends_body(
-    spread, z_own, y_own, y_far, z_pair, z_cross, y_near,
+    spread, z_own, y_own, z_pair, z_cross, y_far, y_near,
     first_low, last_low, ends_low, first_high, last_high, ends_high, before, out,
     z_add, y_add, planes, first, last, sem_out,
 ):
@@ -551,7 +551,7 @@
     z_cross = exchange(z_cross, "gx", 1)
     out, _, *high_ends = step(LOW, B - LOW, 8, diffusivity, q_high, out)
     out = ends(
-        diffusivity, z_own, y_own, y_far, z_pair, z_cross, y_near, *low_ends, *high_ends, out
+        diffusivity, z_own, y_own, z_pair, z_cross, y_far, y_near, *low_ends, *high_ends, out
     )
     return out[..., 0, :].transpose(3, 0, 1, 2, 4).reshape(CAP, F, B * B * B)
 

time: 50 us -> 49.4 us (0.988)
  starting transfers between devices: 19.1 us -> 18.5 us
    ppermute x10, starting transfers between devices: 19.1 us -> 18.5 us  [exchange(): return lax.ppermute(block, axes, pairs)]
  transfers between devices with their start and end apart: 10 -> 10, of which waited for: 2 -> 2; matrix products, arithmetic and copies ran while one was open for 0% -> 0% of each run, Pallas kernels for 40% -> 41%
where the time goes in v12:
time: 49.4 us; the launch traced here: 49.3 us
  Pallas kernels  27.8 us (56%)
  starting transfers between devices  18.5 us (37%)
  waiting for transfers between devices  2.1 us (4%)
  local copies, waits for them, and re-layouts  0.69 us (1%)
    ppermute x10, starting transfers between devices, exchange(): return lax.ppermute(block, axes, pairs)  18.5 us
    pallas_call x2, Pallas kernels, step(): pl.pallas_call(functools.partial(step_body, first, count, chunk), name='s...  14.7 us
    pallas_call x2, Pallas kernels, from_slots(): pl.pallas_call(body, name=name, out_shape=shapes, in_specs=[HBM] * len(ar...  6.22 us
    pallas_call x1, Pallas kernels, ends(): pl.pallas_call(ends_body, name='ends', out_shape=jax.ShapeDtypeStruct((F,...  3.92 us
    pallas_call x2, Pallas kernels, turn(): pl.pallas_call(body, name=name, out_shape=tuple((jax.ShapeDtypeStruct(sha...  3 us
    ppermute x10, waiting for transfers between devices, exchange(): return lax.ppermute(block, axes, pairs)  2.1 us
  transfers between devices with their start and end apart: 10, of which 2 were waited for; matrix products, arithmetic and copies ran while one was open for 0% of the time, Pallas kernels for 41%

profile of v12, /device:TPU:27, one launch (start us, length us, event | category | flops | bytes accessed | tf_op | source)
XLA Modules:
  0.0 49.3 jit_solution(3392345794068693304)
XLA Ops:
  0.0 2.2 %far.1 = (f32[2,6,18,8,128]{4,3,2,1,0:T(8,128)}, f32[8,128]{1,0:T(8,128)}) custom-call(f32[6,32,8,8,1,128]{5,4,3,2,1,0:T(1,128)} %bitcast.10), custom_call_target="tpu_custom_call" | custom-call | bytes 1000 | tf_op jit(solution)/shard_map/far/pallas_call | solution.py:66
  2.2 2.3 %collective-permute-start.5 = (f32[2,6,18,8,128]{4,3,2,1,0:T(8,128)}, f32[2,6,18,8,128]{4,3,2,1,0:T(8,128)S(1)}, u32[]{:S(2)}, u32[]{:S(2)}) collective-permute-start(f32[2,6,18,8,128]{4,3,2,1,0:T(8,128)} %get-tuple-element.38), channel_id=1, source_target_pairs={{1,2},{2,1},{3,4},{4,3},{5,6},{6,5},{7,8},{8,7},{9,10},{10,9},{11,... | collective-permute-start | bytes 2654216 | tf_op jit(solution)/shard_map/ppermute | solution.py:533
  4.5 0.7 %copy-done.3 = f32[8,128]{1,0:T(8,128)S(1)} copy-done((f32[8,128]{1,0:T(8,128)S(1)}, f32[8,128]{1,0:T(8,128)}, u32[]{:S(2)}) %copy-start.3) | copy-done | bytes 4120
  5.2 4.0 %near.1 = (f32[2,6,14,8,128]{4,3,2,1,0:T(8,128)S(1)}, f32[2,6,9,8,128]{4,3,2,1,0:T(8,128)S(1)}, f32[2,6,9,8,128]{4,3,2,1,0:T(8,128)S(1)}, f32[2,6,7,8,128]{4,3,2...) custom-call(f32[6,32,8,8,1,128]{5,4,3,2,1,0:T(1,128)S(1)} %bitcast.1, ...), custom_call_target="tpu_custom_call" | custom-call | bytes 1000 | tf_op jit(solution)/shard_map/near/pallas_call | solution.py:66
  9.2 0.0 copy-start.2
  9.2 2.2 %collective-permute-start.3 = (f32[2,6,9,8,128]{4,3,2,1,0:T(8,128)S(1)}, f32[2,6,9,8,128]{4,3,2,1,0:T(8,128)S(1)}, u32[]{:S(2)}, u32[]{:S(2)}) collective-permute-start(f32[2,6,9,8,128]{4,3,2,1,0:T(8,128)S(1)} %get-tuple-element.36), channel_id=1, source_target_pairs={{0,1},{1,0},{2,3},{3,2},{4,5},{5,4},{6,7},{7,6},{8,9},{9,8},{10,11... | collective-permute-start | bytes 1327112 | tf_op jit(solution)/shard_map/ppermute | solution.py:533
  11.4 0.0 collective-permute-start.2
  11.4 1.7 %collective-permute-start.4 = (f32[2,6,9,8,128]{4,3,2,1,0:T(8,128)S(1)}, f32[2,6,9,8,128]{4,3,2,1,0:T(8,128)S(1)}, u32[]{:S(2)}, u32[]{:S(2)}) collective-permute-start(f32[2,6,9,8,128]{4,3,2,1,0:T(8,128)S(1)} %get-tuple-element.37), channel_id=1, source_target_pairs={{0,1},{1,0},{2,3},{3,2},{4,5},{5,4},{6,7},{7,6},{8,9},{9,8},{10,11... | collective-permute-start | bytes 1327112 | tf_op jit(solution)/shard_map/ppermute | solution.py:533
  13.2 0.0 collective-permute-start
  13.2 0.0 collective-permute-done.3.near_0
  13.2 0.5 %collective-permute-start.1 = (f32[2,6,7,8,128]{4,3,2,1,0:T(8,128)S(1)}, f32[2,6,7,8,128]{4,3,2,1,0:T(8,128)S(1)}, u32[]{:S(2)}, u32[]{:S(2)}) collective-permute-start(f32[2,6,7,8,128]{4,3,2,1,0:T(8,128)S(1)} %get-tuple-element.33), channel_id=1, source_target_pairs={{0,1},{1,0},{2,3},{3,2},{4,5},{5,4},{6,7},{7,6},{8,9},{9,8},{10,11... | collective-permute-start | bytes 1032200 | tf_op jit(solution)/shard_map/ppermute | solution.py:533
  13.7 0.9 %collective-permute-done.4.near_1 = f32[2,6,9,8,128]{4,3,2,1,0:T(8,128)S(1)} collective-permute-done((f32[2,6,9,8,128]{4,3,2,1,0:T(8,128)S(1)}, f32[2,6,9,8,128]{4,3,2,1,0:T(8,128)S(1)}, u32[]{:S(2)}, u32[]{:S(2)}) %collective-permute-start.4) | collective-permute-done | bytes 442400 | tf_op jit(solution)/shard_map/ppermute | solution.py:533
  14.6 1.2 %collective-permute-done.5.far = f32[2,6,18,8,128]{4,3,2,1,0:T(8,128)S(1)} collective-permute-done((f32[2,6,18,8,128]{4,3,2,1,0:T(8,128)}, f32[2,6,18,8,128]{4,3,2,1,0:T(8,128)S(1)}, u32[]{:S(2)}, u32[]{:S(2)}) %collective-permute-start.5) | collective-permute-done | bytes 884768 | tf_op jit(solution)/shard_map/ppermute | solution.py:533
  15.8 1.4 %turn_low.1.q.q_low = f32[6,26,4,8,128]{4,3,2,1,0:T(8,128)S(1)} custom-call(s32[512]{0:T(512)S(1)} %copy-done.1, f32[4,6,18,8,128]{4,3,2,1,0:T(8,128)S(1)} %get-tuple-element.35.hold, f32[2,6,9,8,128]{4,3,2,1,0:T(8,128)S(1)} %collective-permute-done.3.near_0, f32[2,6,9,8,128]{4,3,2,1,0:T(8,128)S(1)} %collective-permute-done.4.near_1, ...), custom_call_target="tpu_custom_call" | custom-call | bytes 6000000 | tf_op jit(solution)/shard_map/turn_low/pallas_call | solution.py:185
  17.1 7.0 %step.2 = (f32[6,32,8,4,1,128]{5,4,3,2,1,0:T(1,128)}, f32[8,128]{1,0:T(8,128)S(1)}, f32[4,6,16,128]{3,2,1,0:T(8,128)S(1)}, f32[4,6,16,128]{3,2,1,0:T(8,128)S(1)}, f32[4,6,2,8,128]{4,3,2,1,0:T(8,128)S(1)}) custom-call(f32[6]{0:T(128)S(1)} %copy-done.2, f32[6,26,4,8,128]{4,3,2,1,0:T(8,128)S(1)} %turn_low.1.q.q_low), custom_call_target="tpu_custom_call" | custom-call | bytes 20000000 | tf_op jit(solution)/shard_map/step/pallas_call | solution.py:374
  24.2 0.0 collective-permute-done.1.near_1
  24.2 1.6 %turn_high.1 = (f32[6,26,4,8,128]{4,3,2,1,0:T(8,128)S(1)}, f32[6,4,4,8,128]{4,3,2,1,0:T(8,128)S(1)}, f32[6,4,32,128]{3,2,1,0:T(8,128)S(1)}, f32[6,2,4,8,128]{4,3...) custom-call(s32[512]{0:T(512)S(1)} %copy-done.1, ...), custom_call_target="tpu_custom_call" | custom-call | bytes 6000000 | tf_op jit(solution)/shard_map/turn_high/pallas_call | solution.py:185
  25.9 0.3 collective-permute-start.6
  26.2 3.8 %collective-permute-start.7 = (f32[6,2,4,8,128]{4,3,2,1,0:T(8,128)S(1)}, f32[6,2,4,8,128]{4,3,2,1,0:T(8,128)S(1)}, u32[]{:S(2)}, u32[]{:S(2)}) collective-permute-start(f32[6,2,4,8,128]{4,3,2,1,0:T(8,128)S(1)} %get-tuple-element.43), channel_id=1, source_target_pairs={{32,64},{64,32},{33,65},{65,33},{34,66},{66,34},{35,67},{67,35},{3... | collective-permute-start | bytes 589832 | tf_op jit(solution)/shard_map/ppermute | solution.py:533
  30.0 3.9 %collective-permute-start.8 = (f32[6,2,32,128]{3,2,1,0:T(8,128)S(1)}, f32[6,2,32,128]{3,2,1,0:T(8,128)S(1)}, u32[]{:S(2)}, u32[]{:S(2)}) collective-permute-start(f32[6,2,32,128]{3,2,1,0:T(8,128)S(1)} %get-tuple-element.44), channel_id=1, source_target_pairs={{1,2},{2,1},{3,4},{4,3},{5,6},{6,5},{7,8},{8,7},{9,10},{10,9},{11,... | collective-permute-start | bytes 589832 | tf_op jit(solution)/shard_map/ppermute | solution.py:533
  33.9 3.8 %collective-permute-start.9 = (f32[6,2,32,128]{3,2,1,0:T(8,128)S(1)}, f32[6,2,32,128]{3,2,1,0:T(8,128)S(1)}, u32[]{:S(2)}, u32[]{:S(2)}) collective-permute-start(f32[6,2,32,128]{3,2,1,0:T(8,128)S(1)} %get-tuple-element.45), channel_id=1, source_target_pairs={{0,1},{1,0},{2,3},{3,2},{4,5},{5,4},{6,7},{7,6},{8,9},{9,8},{10,11... | collective-permute-start | bytes 589832 | tf_op jit(solution)/shard_map/ppermute | solution.py:533
  37.7 7.6 %step.3 = (f32[6,32,8,4,1,128]{5,4,3,2,1,0:T(1,128)}, f32[8,128]{1,0:T(8,128)}, f32[4,6,16,128]{3,2,1,0:T(8,128)S(1)}, f32[4,6,16,128]{3,2,1,0:T(8,128)S(1)}, f32[4,6,2,8,128]{4,3,2,1,0:T(8,128)S(1)}) custom-call(f32[6]{0:T(128)S(1)} %copy-done.2, f32[6,26,4,8,128]{4,3,2,1,0:T(8,128)S(1)} %get-tuple-element.49.q, ...), custom_call_target="tpu_custom_call", output_to_operand_aliasing={{0}: (2, {})} | custom-call | bytes 20000000 | tf_op jit(solution)/shard_map/step/pallas_call | solution.py:374
  45.3 0.0 collective-permute-done.6.z_pair
  45.3 3.9 %ends.1 = f32[6,32,8,4,1,128]{5,4,3,2,1,0:T(1,128)} custom-call(f32[6]{0:T(128)S(1)} %copy-done.2, f32[6,4,4,8,128]{4,3,2,1,0:T(8,128)S(1)} %get-tuple-element.40.z_own, f32[6,4,32,128]{3,2,1,0:T(8,128)S(1)} %get-tuple-element.41.y_own, f32[6,2,4,8,128]{4,3,2,1,0:T(8,128)S(1)} %collective-permute-done.6.z_pair, ...), custom_call_target="tpu_custom_call", output_to_operand_aliasing={{}: (13, {})} | custom-call | bytes 6000000 | tf_op jit(solution)/shard_map/ends/pallas_call | solution.py:506
  (11 shorter events, 0.0 us)
Async XLA Ops:
  0.0 4.5 %copy-start = (f32[8,6,32768]{2,0,1:T(8,128)S(1)}, f32[8,6,32768]{2,0,1:T(8,128)}, u32[]{:S(2)}) copy-start(f32[8,6,32768]{2,0,1:T(8,128)} %param.4) | copy-start | bytes 18874372
  2.2 13.5 %collective-permute-start.5 = (f32[2,6,18,8,128]{4,3,2,1,0:T(8,128)}, f32[2,6,18,8,128]{4,3,2,1,0:T(8,128)S(1)}, u32[]{:S(2)}, u32[]{:S(2)}) collective-permute-start(f32[2,6,18,8,128]{4,3,2,1,0:T(8,128)} %get-tuple-element.38), channel_id=1, source_target_pairs={{1,2},{2,1},{3,4},{4,3},{5,6},{6,5},{7,8},{8,7},{9,10},{10,9},{11,... | collective-permute-start | bytes 2654216 | tf_op jit(solution)/shard_map/ppermute | solution.py:533
  4.5 0.7 %copy-start.3 = (f32[8,128]{1,0:T(8,128)S(1)}, f32[8,128]{1,0:T(8,128)}, u32[]{:S(2)}) copy-start(f32[8,128]{1,0:T(8,128)} %get-tuple-element.30.after) | copy-start | bytes 12292
  5.2 10.6 %copy-start.1 = (s32[512]{0:T(512)S(1)}, s32[512]{0:T(512)}, u32[]{:S(2)}) copy-start(s32[512]{0:T(512)} %owner.3) | copy-start | bytes 6148
  9.2 7.9 %copy-start.2 = (f32[6]{0:T(128)S(1)}, f32[6]{0:T(128)}, u32[]{:S(2)}) copy-start(f32[6]{0:T(128)} %spread.5) | copy-start | bytes 76
  9.2 3.9 %collective-permute-start.3 = (f32[2,6,9,8,128]{4,3,2,1,0:T(8,128)S(1)}, f32[2,6,9,8,128]{4,3,2,1,0:T(8,128)S(1)}, u32[]{:S(2)}, u32[]{:S(2)}) collective-permute-start(f32[2,6,9,8,128]{4,3,2,1,0:T(8,128)S(1)} %get-tuple-element.36), channel_id=1, source_target_pairs={{0,1},{1,0},{2,3},{3,2},{4,5},{5,4},{6,7},{7,6},{8,9},{9,8},{10,11... | collective-permute-start | bytes 1327112 | tf_op jit(solution)/shard_map/ppermute | solution.py:533
  11.4 12.8 %collective-permute-start.2 = (f32[2,6,14,8,128]{4,3,2,1,0:T(8,128)S(1)}, f32[2,6,14,8,128]{4,3,2,1,0:T(8,128)S(1)}, u32[]{:S(2)}, u32[]{:S(2)}) collective-permute-start(f32[2,6,14,8,128]{4,3,2,1,0:T(8,128)S(1)} %get-tuple-element.34), channel_id=1, source_target_pairs={{1,2},{2,1},{3,4},{4,3},{5,6},{6,5},{7,8},{8,7},{9,10},{10,9},{11,... | collective-permute-start | bytes 2064392 | tf_op jit(solution)/shard_map/ppermute | solution.py:533
  11.4 3.1 %collective-permute-start.4 = (f32[2,6,9,8,128]{4,3,2,1,0:T(8,128)S(1)}, f32[2,6,9,8,128]{4,3,2,1,0:T(8,128)S(1)}, u32[]{:S(2)}, u32[]{:S(2)}) collective-permute-start(f32[2,6,9,8,128]{4,3,2,1,0:T(8,128)S(1)} %get-tuple-element.37), channel_id=1, source_target_pairs={{0,1},{1,0},{2,3},{3,2},{4,5},{5,4},{6,7},{7,6},{8,9},{9,8},{10,11... | collective-permute-start | bytes 1327112 | tf_op jit(solution)/shard_map/ppermute | solution.py:533
  13.2 11.0 %collective-permute-start = (f32[2,6,7,8,128]{4,3,2,1,0:T(8,128)S(1)}, f32[2,6,7,8,128]{4,3,2,1,0:T(8,128)S(1)}, u32[]{:S(2)}, u32[]{:S(2)}) collective-permute-start(f32[2,6,7,8,128]{4,3,2,1,0:T(8,128)S(1)} %get-tuple-element.32), channel_id=1, source_target_pairs={{0,1},{1,0},{2,3},{3,2},{4,5},{5,4},{6,7},{7,6},{8,9},{9,8},{10,11... | collective-permute-start | bytes 1032200 | tf_op jit(solution)/shard_map/ppermute | solution.py:533
  13.2 11.0 %collective-permute-start.1 = (f32[2,6,7,8,128]{4,3,2,1,0:T(8,128)S(1)}, f32[2,6,7,8,128]{4,3,2,1,0:T(8,128)S(1)}, u32[]{:S(2)}, u32[]{:S(2)}) collective-permute-start(f32[2,6,7,8,128]{4,3,2,1,0:T(8,128)S(1)} %get-tuple-element.33), channel_id=1, source_target_pairs={{0,1},{1,0},{2,3},{3,2},{4,5},{5,4},{6,7},{7,6},{8,9},{9,8},{10,11... | collective-permute-start | bytes 1032200 | tf_op jit(solution)/shard_map/ppermute | solution.py:533
  25.9 19.4 %collective-permute-start.6 = (f32[6,2,4,8,128]{4,3,2,1,0:T(8,128)S(1)}, f32[6,2,4,8,128]{4,3,2,1,0:T(8,128)S(1)}, u32[]{:S(2)}, u32[]{:S(2)}) collective-permute-start(f32[6,2,4,8,128]{4,3,2,1,0:T(8,128)S(1)} %get-tuple-element.42), channel_id=1, source_target_pairs={{0,32},{32,0},{64,96},{96,64},{1,33},{33,1},{65,97},{97,65},{2,34}... | collective-permute-start | bytes 589832 | tf_op jit(solution)/shard_map/ppermute | solution.py:533
  26.2 19.1 %collective-permute-start.7 = (f32[6,2,4,8,128]{4,3,2,1,0:T(8,128)S(1)}, f32[6,2,4,8,128]{4,3,2,1,0:T(8,128)S(1)}, u32[]{:S(2)}, u32[]{:S(2)}) collective-permute-start(f32[6,2,4,8,128]{4,3,2,1,0:T(8,128)S(1)} %get-tuple-element.43), channel_id=1, source_target_pairs={{32,64},{64,32},{33,65},{65,33},{34,66},{66,34},{35,67},{67,35},{3... | collective-permute-start | bytes 589832 | tf_op jit(solution)/shard_map/ppermute | solution.py:533
  30.0 15.3 %collective-permute-start.8 = (f32[6,2,32,128]{3,2,1,0:T(8,128)S(1)}, f32[6,2,32,128]{3,2,1,0:T(8,128)S(1)}, u32[]{:S(2)}, u32[]{:S(2)}) collective-permute-start(f32[6,2,32,128]{3,2,1,0:T(8,128)S(1)} %get-tuple-element.44), channel_id=1, source_target_pairs={{1,2},{2,1},{3,4},{4,3},{5,6},{6,5},{7,8},{8,7},{9,10},{10,9},{11,... | collective-permute-start | bytes 589832 | tf_op jit(solution)/shard_map/ppermute | solution.py:533
  33.9 11.4 %collective-permute-start.9 = (f32[6,2,32,128]{3,2,1,0:T(8,128)S(1)}, f32[6,2,32,128]{3,2,1,0:T(8,128)S(1)}, u32[]{:S(2)}, u32[]{:S(2)}) collective-permute-start(f32[6,2,32,128]{3,2,1,0:T(8,128)S(1)} %get-tuple-element.45), channel_id=1, source_target_pairs={{0,1},{1,0},{2,3},{3,2},{4,5},{5,4},{6,7},{7,6},{8,9},{9,8},{10,11... | collective-permute-start | bytes 589832 | tf_op jit(solution)/shard_map/ppermute | solution.py:533
